TPU v7x, 32 devices: a whole 2x2x4 slice. The times are simulated.
32 devices in a mesh: seq: 4 (over z), fsdp: 8 (over y, x, core).
Axes of the slice: x: 2, y: 2, z: 4, core: 2. Of those that a mesh axis runs over, the one named last changes fastest.
Arguments:
- tokens: bfloat16 [2, 8, 256, 2048], P(None, 'fsdp', 'seq'), may hold values from -6 to 6
- lengths: int32 [2, 8, 4], P(None, 'fsdp'), may hold values from 1 to 128, 256 in all within a row
- in_weight: bfloat16 [2048, 12288], P(('seq', 'fsdp')), may hold values from -0.125 to 0.125
- decay_weight: bfloat16 [2048, 32], P(('seq', 'fsdp')), may hold values from -0.125 to 0.125
- conv_weight: bfloat16 [8192, 4], P(('seq', 'fsdp')), may hold values from -3 to 3
- a_log: float32 [16], replicated, may hold values from -4 to 0.5
- dt_bias: float32 [16], replicated, may hold values from -1.5 to 1
- norm_gains: bfloat16 [2, 2048], P(None, ('seq', 'fsdp')), may hold values from 0.5 to 1.5
- out_gain: float32 [256], replicated, may hold values from 0.5 to 1.5
- out_weight: bfloat16 [4096, 2048], P(('seq', 'fsdp')), may hold values from -0.1875 to 0.1875
- up_weight: bfloat16 [2048, 11008], P(('seq', 'fsdp')), may hold values from -0.125 to 0.125
- down_weight: bfloat16 [5504, 2048], P(('seq', 'fsdp')), may hold values from -0.15625 to 0.15625
- cotangent: bfloat16 [2, 8, 256, 2048], P(None, 'fsdp', 'seq'), may hold values from -6 to 6
Outputs:
- block_out: bfloat16 [2, 8, 256, 2048], P(None, 'fsdp', 'seq')
- grad_tokens: float32 [2, 8, 256, 2048], P(None, 'fsdp', 'seq')
- grad_in: float32 [2048, 12288], P(('seq', 'fsdp'))
- grad_decay: float32 [2048, 32], P(('seq', 'fsdp'))
- grad_conv: float32 [8192, 4], P(('seq', 'fsdp'))
- grad_a_log: float32 [16], replicated
- grad_dt_bias: float32 [16], replicated
- grad_norm_gains: float32 [2, 2048], P(None, ('seq', 'fsdp'))
- grad_out_gain: float32 [256], replicated
- grad_out: float32 [4096, 2048], P(('seq', 'fsdp'))
- grad_up: float32 [2048, 11008], P(('seq', 'fsdp'))
- grad_down: float32 [5504, 2048], P(('seq', 'fsdp'))
Inputs may be any that keep to these rules, and one draw needn't show every extreme that they name: Each pack's 4 lengths sum to 256; in each pack the longest document has exactly 128 tokens.
All inputs are finite; a program needn't handle non-finite values.
Results may differ from a plain program's by a relative error of at most 0.017.
Values may be sent and summed in bfloat16 or wider, within the bound.
No kernel may reach another device: no remote copies, remote signals or barrier semaphores. Data moves between devices by JAX's collectives and lax.ppermute only.
A program may use at most 512 MiB of HBM per device.

v0:
```python
from functools import partial

import jax
import jax.numpy as jnp
from jax import lax
from jax.sharding import PartitionSpec as P

D = 2048
H = 16
DK = 128
DV = 256
FF = 5504
CONV = 4
GROUP = 64
MICRO = 2


epsilon = 1e-06


def precise_total(form, left, right):
    return jnp.einsum(
        form, left, right, precision=lax.Precision.HIGHEST, preferred_element_type=jnp.float32
    )


def rms_apply(values, gain):
    return values * lax.rsqrt(jnp.mean(values * values, axis=-1, keepdims=True) + epsilon) * gain


def unit_rows(values):
    return values * lax.rsqrt(jnp.sum(values * values, axis=-1, keepdims=True) + epsilon)


def segment_ids(lengths_row, count):
    ends = jnp.cumsum(lengths_row, dtype=jnp.int32)[:-1]
    places = jnp.arange(count, dtype=jnp.int32)
    return jnp.sum((places[:, None] >= ends[None, :]).astype(jnp.int32), axis=1, dtype=jnp.int32)


def short_conv(values, weight, segs):
    total = values * weight[:, CONV - 1]
    for lag in range(1, CONV):
        moved = jnp.concatenate(
            [jnp.zeros((lag, values.shape[1]), jnp.float32), values[:-lag]], axis=0
        )
        earlier = jnp.concatenate([jnp.full((lag,), -1, jnp.int32), segs[:-lag]], axis=0)
        same = jnp.where(earlier == segs, 1.0, 0.0).astype(jnp.float32)
        total = total + moved * same[:, None] * weight[:, CONV - 1 - lag]
    return total


def group_rule(query, keys, values, logdecay, beta, segs):
    count, heads = (query.shape[0], query.shape[1])
    blocks = count // GROUP

    def arrange(array):
        return jnp.swapaxes(array.reshape((blocks, GROUP) + array.shape[1:]), 1, 2)

    earlier = jnp.concatenate([jnp.full((1,), -1, jnp.int32), segs[:-1]], axis=0)
    lower = jnp.tril(jnp.ones((GROUP, GROUP), jnp.bool_))
    strict = jnp.tril(jnp.ones((GROUP, GROUP), jnp.float32), -1)
    identity = jnp.eye(GROUP, dtype=jnp.float32)

    def step(state_matrix, item):
        (
            query_block_rows,
            key_block_rows,
            value_block_rows,
            block_log,
            block_beta,
            block_seg,
            block_prev,
        ) = item
        cumul = jnp.cumsum(block_log, axis=1)
        same = (block_seg[:, None] == block_seg[None, :]) & lower
        spread = jnp.where(same, cumul[:, :, None] - cumul[:, None, :], 0.0)
        inner = jnp.where(same, jnp.exp(spread), 0.0)
        carried_state = jnp.where(block_seg == block_prev, 1.0, 0.0)[None, :] * jnp.exp(cumul)
        keys_keys = precise_total("htk,hsk->hts", key_block_rows, key_block_rows)
        system = identity + block_beta[:, :, None] * inner * keys_keys * strict
        target = block_beta[:, :, None] * (
            value_block_rows
            - carried_state[:, :, None]
            * precise_total("gjs,gse->gje", key_block_rows, state_matrix)
        )
        delta_update = lax.linalg.triangular_solve(
            system, target, left_side=True, lower=True, unit_diagonal=True
        )
        scores = precise_total("htk,hsk->hts", query_block_rows, key_block_rows) * inner
        output_rows = carried_state[:, :, None] * precise_total(
            "gjs,gse->gje", query_block_rows, state_matrix
        ) + precise_total("hts,hsv->htv", scores, delta_update)
        tail_rows = jnp.where(block_seg == block_seg[-1], 1.0, 0.0)[None, :] * jnp.exp(
            cumul[:, -1:] - cumul
        )
        kept = jnp.where(block_seg[-1] == block_prev, 1.0, 0.0) * jnp.exp(cumul[:, -1])
        state_matrix = kept[:, None, None] * state_matrix + precise_total(
            "amg,amr->agr", key_block_rows, tail_rows[:, :, None] * delta_update
        )
        return (state_matrix, output_rows)

    items = (
        arrange(query),
        arrange(keys),
        arrange(values),
        arrange(logdecay),
        arrange(beta),
        segs.reshape(blocks, GROUP),
        earlier.reshape(blocks, GROUP)[:, 0],
    )
    start = jnp.zeros((heads, DK, DV), jnp.float32)
    _, outputs = lax.scan(step, start, items)
    return jnp.swapaxes(outputs, 1, 2).reshape(count, heads, DV)


def head_mix(query_in, key_in, value_in, pairs_in, conv_local, a_local, dt_local, segs):
    count = query_in.shape[0]
    heads = a_local.shape[0]
    joined = jnp.concatenate([query_in, key_in, value_in], axis=1)
    conv = jax.nn.silu(short_conv(joined, conv_local, segs))
    width = heads * DK
    query = unit_rows(conv[:, :width].reshape(count, heads, DK)) * DK ** (-0.5)
    keys = unit_rows(conv[:, width : 2 * width].reshape(count, heads, DK))
    values = conv[:, 2 * width :].reshape(count, heads, DV)
    pair_view = pairs_in.reshape(count, heads, 2)
    logdecay = -jnp.exp(a_local) * jax.nn.softplus(pair_view[:, :, 0] + dt_local)
    beta = jax.nn.sigmoid(pair_view[:, :, 1])
    return group_rule(query, keys, values, logdecay, beta, segs).reshape(count, heads * DV)


def gated_norm(values, gate, gain):
    rows = values.shape[0]
    return rms_apply(values.reshape(rows, H, DV), gain).reshape(rows, H * DV) * jax.nn.silu(gate)


def swiglu(both):
    return jax.nn.silu(both[:, :FF]) * both[:, FF:]


def shards(
    tokens,
    lengths,
    in_weight,
    decay_weight,
    conv_weight,
    a_log,
    dt_bias,
    norm_gains,
    out_gain,
    out_weight,
    up_weight,
    down_weight,
    cotangent,
):
    seq_count = lax.axis_size("seq")
    heads_here = H // seq_count
    place = lax.axis_index("seq")
    head_start = place * heads_here
    a_local = lax.dynamic_slice_in_dim(a_log, head_start, heads_here)
    dt_local = lax.dynamic_slice_in_dim(dt_bias, head_start, heads_here)
    qk_width = H * DK
    split = 2 * qk_width + H * DV
    local_width = heads_here * DK

    def spread_heads(grad_local):
        return lax.dynamic_update_slice_in_dim(
            jnp.zeros((H,), jnp.float32), grad_local, head_start, 0
        )

    def outer(left, right):
        return jnp.dot(left.T, right, preferred_element_type=jnp.float32)

    shared = (
        lax.all_gather(in_weight, ("seq", "fsdp"), axis=0, tiled=True),
        lax.all_gather(decay_weight, ("seq", "fsdp"), axis=0, tiled=True),
        lax.all_gather(conv_weight, ("seq", "fsdp"), axis=0, tiled=True),
        lax.all_gather(norm_gains, ("seq", "fsdp"), axis=1, tiled=True),
        lax.all_gather(out_weight, ("seq", "fsdp"), axis=0, tiled=True),
        lax.all_gather(up_weight, ("seq", "fsdp"), axis=0, tiled=True),
        lax.all_gather(down_weight, ("seq", "fsdp"), axis=0, tiled=True),
    )
    finals = []
    grad_inputs = []
    total_mix = None
    total_mlp = None
    kept_rows = []
    grad_convsum = jnp.zeros((split, CONV), jnp.float32)
    grad_gainsum = jnp.zeros((2, D), jnp.float32)
    grad_alog = jnp.zeros((H,), jnp.float32)
    grad_dt = jnp.zeros((H,), jnp.float32)
    grad_outgain = jnp.zeros((DV,), jnp.float32)
    for micro in range(MICRO):
        w_in, w_decay, full_conv, gains, w_out, w_up, w_down = shared
        gains_f = gains.astype(jnp.float32)
        inputs = tokens[micro, 0].astype(jnp.float32)
        first_f, norm1_back = jax.vjp(rms_apply, inputs, gains_f[0])
        first = first_f.astype(jnp.bfloat16)
        proj = jnp.dot(first, w_in, preferred_element_type=jnp.float32)
        sent = proj[:, :split].astype(jnp.bfloat16)
        gate_out = proj[:, split:]
        pairs = jnp.dot(first, w_decay, preferred_element_type=jnp.float32).astype(jnp.bfloat16)
        query_h, key_h, value_h, pairs_h = (
            lax.all_to_all(sent[:, :qk_width], "seq", split_axis=1, concat_axis=0, tiled=True),
            lax.all_to_all(
                sent[:, qk_width : 2 * qk_width], "seq", split_axis=1, concat_axis=0, tiled=True
            ),
            lax.all_to_all(sent[:, 2 * qk_width :], "seq", split_axis=1, concat_axis=0, tiled=True),
            lax.all_to_all(pairs, "seq", split_axis=1, concat_axis=0, tiled=True),
        )
        segs = segment_ids(lengths[micro, 0], query_h.shape[0])
        mixer = partial(head_mix, segs=segs)
        pieces = [
            lax.dynamic_slice_in_dim(full_conv, head_start * DK, local_width),
            lax.dynamic_slice_in_dim(full_conv, qk_width + head_start * DK, local_width),
            lax.dynamic_slice_in_dim(full_conv, 2 * qk_width + head_start * DV, heads_here * DV),
        ]
        mixed_h, head_back = jax.vjp(
            mixer,
            query_h.astype(jnp.float32),
            key_h.astype(jnp.float32),
            value_h.astype(jnp.float32),
            pairs_h.astype(jnp.float32),
            jnp.concatenate(pieces, axis=0).astype(jnp.float32),
            a_local,
            dt_local,
        )
        mixed = lax.all_to_all(
            mixed_h.astype(jnp.bfloat16), "seq", split_axis=0, concat_axis=1, tiled=True
        )
        normed_f, gated_back = jax.vjp(gated_norm, mixed.astype(jnp.float32), gate_out, out_gain)
        normed = normed_f.astype(jnp.bfloat16)
        middle = inputs + jnp.dot(normed, w_out, preferred_element_type=jnp.float32)
        second_f, norm2_back = jax.vjp(rms_apply, middle, gains_f[1])
        second = second_f.astype(jnp.bfloat16)
        both = jnp.dot(second, w_up, preferred_element_type=jnp.float32)
        act_f, act_back = jax.vjp(swiglu, both)
        act = act_f.astype(jnp.bfloat16)
        finals.append(
            (middle + jnp.dot(act, w_down, preferred_element_type=jnp.float32)).astype(jnp.bfloat16)
        )
        grad_out_rows = cotangent[micro, 0]
        grad_act = jnp.dot(grad_out_rows, w_down.T, preferred_element_type=jnp.float32)
        (grad_both,) = act_back(grad_act)
        grad_both = grad_both.astype(jnp.bfloat16)
        grad_second = jnp.dot(grad_both, w_up.T, preferred_element_type=jnp.float32)
        grad_mid_norm, term_gain2 = norm2_back(grad_second)
        grad_middle = grad_out_rows.astype(jnp.float32) + grad_mid_norm
        grad_branch = grad_middle.astype(jnp.bfloat16)
        grad_normed = jnp.dot(grad_branch, w_out.T, preferred_element_type=jnp.float32)
        grad_mixed, grad_gate, term_outgain = gated_back(grad_normed)
        grad_mixed_h = lax.all_to_all(
            grad_mixed.astype(jnp.bfloat16), "seq", split_axis=1, concat_axis=0, tiled=True
        )
        grad_q, grad_k, grad_v, grad_p, grad_conv_local, grad_alog_local, grad_dt_local = head_back(
            grad_mixed_h.astype(jnp.float32)
        )
        back_q, back_k, back_v, back_p = (
            lax.all_to_all(
                grad_q.astype(jnp.bfloat16), "seq", split_axis=0, concat_axis=1, tiled=True
            ),
            lax.all_to_all(
                grad_k.astype(jnp.bfloat16), "seq", split_axis=0, concat_axis=1, tiled=True
            ),
            lax.all_to_all(
                grad_v.astype(jnp.bfloat16), "seq", split_axis=0, concat_axis=1, tiled=True
            ),
            lax.all_to_all(
                grad_p.astype(jnp.bfloat16), "seq", split_axis=0, concat_axis=1, tiled=True
            ),
        )
        grad_proj = jnp.concatenate(
            [back_q, back_k, back_v, grad_gate.astype(jnp.bfloat16)], axis=1
        )
        grad_first = jnp.dot(grad_proj, w_in.T, preferred_element_type=jnp.float32) + jnp.dot(
            back_p, w_decay.T, preferred_element_type=jnp.float32
        )
        grad_in_norm, term_gain1 = norm1_back(grad_first)
        grad_inputs.append(grad_middle + grad_in_norm)
        gain_terms = jnp.stack([term_gain1, term_gain2])
        kept_rows.append(
            (first, grad_proj, back_p, normed, grad_branch, second, grad_both, act, grad_out_rows)
        )
        full = jnp.zeros((split, CONV), jnp.float32)
        full = lax.dynamic_update_slice_in_dim(
            full, grad_conv_local[:local_width], head_start * DK, 0
        )
        full = lax.dynamic_update_slice_in_dim(
            full, grad_conv_local[local_width : 2 * local_width], qk_width + head_start * DK, 0
        )
        grad_convsum = grad_convsum + lax.dynamic_update_slice_in_dim(
            full, grad_conv_local[2 * local_width :], 2 * qk_width + head_start * DV, 0
        )
        grad_gainsum = grad_gainsum + gain_terms
        grad_alog = grad_alog + spread_heads(grad_alog_local)
        grad_dt = grad_dt + spread_heads(grad_dt_local)
        grad_outgain = grad_outgain + term_outgain
    joined = [jnp.concatenate([rows[index] for rows in kept_rows], axis=0) for index in range(9)]
    total_mlp = (
        lax.psum_scatter(
            outer(joined[5], joined[6]), ("seq", "fsdp"), scatter_dimension=0, tiled=True
        ),
        lax.psum_scatter(
            outer(joined[7], joined[8]), ("seq", "fsdp"), scatter_dimension=0, tiled=True
        ),
    )
    total_mix = (
        lax.psum_scatter(
            outer(joined[0], joined[1]), ("seq", "fsdp"), scatter_dimension=0, tiled=True
        ),
        lax.psum_scatter(
            outer(joined[0], joined[2]), ("seq", "fsdp"), scatter_dimension=0, tiled=True
        ),
        lax.psum_scatter(
            outer(joined[3], joined[4]), ("seq", "fsdp"), scatter_dimension=0, tiled=True
        ),
        lax.psum_scatter(grad_convsum, ("seq", "fsdp"), scatter_dimension=0, tiled=True),
        lax.psum_scatter(grad_gainsum, ("seq", "fsdp"), scatter_dimension=1, tiled=True),
    )
    small = lax.psum((grad_alog, grad_dt, grad_outgain), ("seq", "fsdp"))
    return (
        jnp.stack(finals)[:, None],
        jnp.stack(grad_inputs)[:, None],
        total_mix[0],
        total_mix[1],
        total_mix[3],
        small[0],
        small[1],
        total_mix[4],
        small[2],
        total_mix[2],
        total_mlp[0],
        total_mlp[1],
    )


def solution(mesh):
    placed = (
        P(None, "fsdp", "seq", None),
        P(None, "fsdp", None),
        P(("seq", "fsdp"), None),
        P(("seq", "fsdp"), None),
        P(("seq", "fsdp"), None),
        P(),
        P(),
        P(None, ("seq", "fsdp")),
        P(),
        P(("seq", "fsdp"), None),
        P(("seq", "fsdp"), None),
        P(("seq", "fsdp"), None),
        P(None, "fsdp", "seq", None),
    )
    return jax.shard_map(
        shards,
        mesh=mesh,
        in_specs=placed,
        out_specs=(
            P(None, "fsdp", "seq", None),
            P(None, "fsdp", "seq", None),
            P(("seq", "fsdp"), None),
            P(("seq", "fsdp"), None),
            P(("seq", "fsdp"), None),
            P(),
            P(),
            P(None, ("seq", "fsdp")),
            P(),
            P(("seq", "fsdp"), None),
            P(("seq", "fsdp"), None),
            P(("seq", "fsdp"), None),
        ),
        check_vma=False,
    )
```

profile of v0, /device:TPU:0, one launch (start us, length us, event | category | flops | bytes accessed | tf_op | source)
XLA Modules:
  0.0 4563.7 jit_solution(14151431083782459184)
XLA Ops:
  10.0 43.6 all-gather
  53.7 38.6 all-gather.1
  98.8 40.9 all_gather.24
  152.4 139.2 %all-gather.8.cloned.1.call-done = bf16[2048,12288]{1,0:T(8,128)(2,1)} async-done(((bf16[64,12288]{1,0:T(8,128)(2,1)}), bf16[2048,12288]{1,0:T(8,128)(2,1)}) %all-gather.8.cloned.1.call-update) | async-done | bytes 50331664 | tf_op jit(solution)/shard_map/all_gather | solution.py:175
  291.7 22.3 fusion.519
  318.7 22.3 fusion.520
  348.2 14.2 all-to-all-done.1
  378.6 25.4 all-to-all-done.3
  438.9 19.0 all-to-all-done.8
  492.7 182.5 %while.190 = (s32[]{:T(128)}, f32[4,128,256]{2,1,0:T(8,128)S(1)}, bf16[4,4,64,256]{3,2,1,0:T(8,128)(2,1)}, pred[4,4,64,64]{3,2,1,0:T(32,128)(4,1)}, f32[4,4,64,6...) while((s32[]{:T(128)}, f32[4,128,256]{2,1,0:T(8,128)S(1)}, ...), condition=%wide.region_7.10_spmd.clone, body=%wide.region_5.9_spmd.clone.sunk | while | flops 454830144 | bytes 14790742 | solution.py:113
  506.8 20.3 custom-call.26
  552.5 20.3 custom-call.26
  598.2 20.3 custom-call.26
  643.9 20.3 custom-call.26
  708.4 175.6 %while.191 = (s32[]{:T(128)}, f32[4,128,256]{2,1,0:T(8,128)S(1)}, bf16[4,4,64,256]{3,2,1,0:T(8,128)(2,1)}, pred[4,4,64,64]{3,2,1,0:T(32,128)(4,1)}, f32[4,4,64,6...) while((s32[]{:T(128)}, f32[4,128,256]{2,1,0:T(8,128)S(1)}, ...), condition=%wide.region_17.20_spmd.clone, body=%wide.region_15.19_spmd.clone.sunk | while | flops 454830144 | bytes 14658026 | solution.py:113
  721.6 20.3 custom-call.27
  765.5 20.3 custom-call.27
  809.5 20.3 custom-call.27
  853.3 20.3 custom-call.27
  893.1 22.1 reshape.1746
  951.4 19.6 fusion.525
  971.0 14.5 fusion.455
  987.5 20.3 multiply_reduce_fusion.17
  1007.8 19.7 fusion.526
  1027.5 14.9 fusion.456
  1044.3 20.3 multiply_reduce_fusion.16
  1082.6 14.4 multiply_reduce_fusion.10
  1130.8 232.2 %while.192 = (s32[]{:T(128)}, f32[4,128,256]{2,1,0:T(8,128)S(1)}, f32[4,4,64,128]{3,2,1,0:T(8,128)}, f32[4,4,64,128]{3,2,1,0:T(8,128)}, f32[4,4,64,256]{3,2,1,0:...) while((s32[]{:T(128)}, f32[4,128,256]{2,1,0:T(8,128)S(1)}, ...), condition=%wide.region_33.38_spmd.clone, body=%wide.region_22.37_spmd.clone.sunk | while | flops 921638976 | bytes 19205884 | solution.py:113
  1142.3 19.7 custom-call.28
  1200.3 19.7 custom-call.28
  1258.3 19.7 custom-call.28
  1316.2 19.7 custom-call.28
  1384.1 231.9 %while.193 = (s32[]{:T(128)}, f32[4,128,256]{2,1,0:T(8,128)S(1)}, f32[4,4,64,128]{3,2,1,0:T(8,128)}, f32[4,4,64,128]{3,2,1,0:T(8,128)}, f32[4,4,64,256]{3,2,1,0:...) while((s32[]{:T(128)}, f32[4,128,256]{2,1,0:T(8,128)S(1)}, ...), condition=%wide.region_50.55_spmd.clone, body=%wide.region_39.54_spmd.clone.sunk | while | flops 921638976 | bytes 19205884 | solution.py:113
  1395.5 19.7 custom-call.29
  1453.4 19.7 custom-call.29
  1511.4 19.7 custom-call.29
  1569.4 19.7 custom-call.29
  1747.7 22.4 fusion.377
  1770.2 22.2 fusion.385
  1813.0 46.6 %fusion.341 = f32[2048,12288]{1,0:T(8,128)} fusion(bf16[64,4096]{1,0:T(8,128)(2,1)S(1)} %copy-done.72, bf16[64,4096]{1,0:T(8,128)(2,1)S(1)} %bitcast.1439, bf16[64,2048]{1,0:T(8,128)(2,1)S(1)} %bitcast.1472, bf16[64,2048]{1,0:T(8,128)(2,1)} %bitcast.1474, bf16[64,4096]{1,0:T(8,128)(2,1)S(1)} %copy-done.71, bf16[64,4096]{1,0:T(8,128)(2,1)S(1)} %bitcast.1437, ...), kind=kOutput, calls=%fused_computation.508 | convolution fusion | flops 6468665344 | bytes 104333312 | tf_op jit(solution)/shard_map/dot_general | solution.py:172
  1861.5 31.4 fusion.357
  1894.4 17.5 fusion.397
  1911.9 688.3 %fusion.20 = f32[176,2048]{1,0:T(8,128)S(1)} fusion(f32[5504,2048]{1,0:T(8,128)} %fusion.397), kind=kCustom, calls=%all-reduce-scatter | all-reduce-scatter fusion | flops 11534337 | bytes 46530560
  2601.3 66.3 %collective-permute-start = (f32[124,2048]{1,0:T(8,128)}, f32[124,2048]{1,0:T(8,128)}, u32[]{:S(2)}, u32[]{:S(2)}) collective-permute-start(f32[124,2048]{1,0:T(8,128)} %slice.332), channel_id=1, source_target_pairs={{0,1},{1,2},{2,3},{3,4},{4,5},{5,6},{6,7},{7,8},{8,9},{9,10},{10,1... | collective-permute-start | bytes 3047432
  2694.4 50.9 %all-reduce.44 = (f32[16]{0:T(128)}, f32[16]{0:T(128)}, f32[256]{0:T(256)}) all-reduce(f32[16]{0:T(128)S(1)} %get-tuple-element.5206, f32[16]{0:T(128)S(1)} %get-tuple-element.5205, f32[256]{0:T(256)S(1)} %add.601), channel_id=1, replica_groups=mesh['seq'=4,'fsdp'=8] {'seq','fsdp'}, use_global_device_ids=true, to_apply=%region_67.72 | all-reduce | flops 288 | bytes 2304 | tf_op jit(solution)/shard_map/psum | solution.py:320
  2763.4 14.0 reduce-scatter.17.cloned.1.call-done
  2777.4 835.2 %reduce-scatter.15.cloned.1.call-done = f32[64,12288]{1,0:T(8,128)} async-done(((f32[2048,12288]{1,0:T(8,128)}), f32[64,12288]{1,0:T(8,128)}) %reduce-scatter.15.cloned.1.call-update) | async-done | bytes 3145744 | tf_op jit(solution)/shard_map/reduce_scatter | solution.py:308
  3612.6 944.0 %reduce-scatter.19.cloned.1.call-done = f32[64,11008]{1,0:T(8,128)} async-done(((f32[2048,11008]{1,0:T(8,128)}), f32[64,11008]{1,0:T(8,128)}) %reduce-scatter.19.cloned.1.call-update) | async-done | bytes 2818064 | tf_op jit(solution)/shard_map/reduce_scatter | solution.py:300
  (1688 shorter events, 963.8 us)
Async XLA Ops:
  7.2 284.5 %all-gather.8.cloned.1.call-start = ((), (), s32[]{:S(2)}) async-start(), calls=%async_computation.26 | async-start | bytes 51904512 | tf_op jit(solution)/shard_map/all_gather | solution.py:175
  7.9 84.8 %copy-start.38 = (bf16[2,1,64,2048]{3,2,1,0:T(8,128)(2,1)S(1)}, bf16[2,1,64,2048]{3,2,1,0:T(8,128)(2,1)}, u32[]{:S(2)}) copy-start(bf16[2,1,64,2048]{3,2,1,0:T(8,128)(2,1)} %param.28) | copy-start | bytes 1572868
  7.9 885.2 %all-gather.14.cloned.1.call-start = ((), (), s32[]{:S(2)}) async-start(), calls=%async_computation.32 | async-start | bytes 23789568 | tf_op jit(solution)/shard_map/all_gather | solution.py:181
  8.7 928.3 %all-gather.10.cloned.1.call-start = ((), (), s32[]{:S(2)}) async-start(), calls=%async_computation.27 | async-start | bytes 17301504 | tf_op jit(solution)/shard_map/all_gather | solution.py:179
  9.4 88.4 %copy-start.241 = (s32[2,1,4]{2,1,0:T(1,128)S(1)}, s32[2,1,4]{2,1,0:T(1,128)}, u32[]{:S(2)}) copy-start(s32[2,1,4]{2,1,0:T(1,128)} %param.29) | copy-start | bytes 100
  9.4 89.3 %copy-start.231 = (bf16[256,4]{0,1:T(4,128)(2,1)S(1)}, bf16[256,4]{0,1:T(4,128)(2,1)}, u32[]{:S(2)}) copy-start(bf16[256,4]{0,1:T(4,128)(2,1)} %param.32) | copy-start | bytes 6148
  9.4 941.9 %all-gather.12.cloned.1.call-start = ((), (), s32[]{:S(2)}) async-start(), calls=%async_computation.28 | async-start | bytes 46497792 | tf_op jit(solution)/shard_map/all_gather | solution.py:180
  10.0 131.8 %copy-start.210 = (f32[256]{0:T(256)S(1)}, f32[256]{0:T(256)}, u32[]{:S(2)}) copy-start(f32[256]{0:T(256)} %param.36) | copy-start | bytes 3076
  93.5 971.1 %copy-start.147 = (f32[1,2048]{1,0:T(1,128)}, f32[1,2048]{1,0:T(1,128)S(1)}, u32[]{:S(2)}) copy-start(f32[1,2048]{1,0:T(1,128)S(1)} %get-tuple-element.5159) | copy-start | bytes 24580
  93.7 220.3 %copy-start.61 = (bf16[64,2048]{1,0:T(8,128)(2,1)}, bf16[64,2048]{1,0:T(8,128)(2,1)S(1)}, u32[]{:S(2)}) copy-start(bf16[64,2048]{1,0:T(8,128)(2,1)S(1)} %get-tuple-element.5142) | copy-start | bytes 786436
  93.7 224.9 %copy-start.63 = (bf16[64,2048]{1,0:T(8,128)(2,1)}, bf16[64,2048]{1,0:T(8,128)(2,1)S(1)}, u32[]{:S(2)}) copy-start(bf16[64,2048]{1,0:T(8,128)(2,1)S(1)} %get-tuple-element.5143) | copy-start | bytes 786436
  94.6 54.4 %all-to-all-start.5 = ((bf16[4,2,256]{2,1,0:T(2,128)(2,1)}), bf16[4,2,256]{2,1,0:T(2,128)(2,1)S(1)}, u32[]{:S(2)}, u32[]{:S(2)}) async-start(bf16[4,2,256]{2,1,0:T(2,128)(2,1)} %reshape.1776), calls=%async_computation.5 | async-start | bytes 8192 | tf_op jit(solution)/shard_map/all_to_all | solution.py:209
  142.1 317.2 %copy-start.158 = (f32[2048,1]{0,1:T(1,128)}, f32[2048,1]{0,1:T(1,128)S(1)}, u32[]{:S(2)}) copy-start(f32[2048,1]{0,1:T(1,128)S(1)} %get-tuple-element.5152) | copy-start | bytes 24580
  142.1 317.2 %copy-start.160 = (f32[2048,1]{0,1:T(1,128)}, f32[2048,1]{0,1:T(1,128)S(1)}, u32[]{:S(2)}) copy-start(f32[2048,1]{0,1:T(1,128)S(1)} %get-tuple-element.5153) | copy-start | bytes 24580
  142.1 317.2 %copy-start.162 = (f32[2048,1]{0,1:T(1,128)}, f32[2048,1]{0,1:T(1,128)S(1)}, u32[]{:S(2)}) copy-start(f32[2048,1]{0,1:T(1,128)S(1)} %get-tuple-element.5154) | copy-start | bytes 24580
  142.1 317.2 %copy-start.164 = (f32[2048,1]{0,1:T(1,128)}, f32[2048,1]{0,1:T(1,128)S(1)}, u32[]{:S(2)}) copy-start(f32[2048,1]{0,1:T(1,128)S(1)} %get-tuple-element.5155) | copy-start | bytes 24580
  142.2 265.9 %copy-start.227 = (f32[4]{0:T(128)}, f32[4]{0:T(128)S(1)}, u32[]{:S(2)}) copy-start(f32[4]{0:T(128)S(1)} %fusion.495) | copy-start | bytes 52
  144.4 263.7 %copy-start.228 = (f32[4]{0:T(128)}, f32[4]{0:T(128)S(1)}, u32[]{:S(2)}) copy-start(f32[4]{0:T(128)S(1)} %dynamic_slice.760) | copy-start | bytes 52
  149.0 165.9 %all-to-all-start = ((bf16[4,2,256]{2,1,0:T(2,128)(2,1)}), bf16[4,2,256]{2,1,0:T(2,128)(2,1)S(1)}, u32[]{:S(2)}, u32[]{:S(2)}) async-start(bf16[4,2,256]{2,1,0:T(2,128)(2,1)} %reshape.1778), calls=%async_computation | async-start | bytes 8192 | tf_op jit(solution)/shard_map/all_to_all | solution.py:209
  315.2 26.4 all-to-all-start.2
  341.7 20.7 all-to-all-start.1
  362.4 10.5 all-to-all-start.7
  373.0 86.3 %copy-start.88 = (bf16[64,4,512]{2,0,1:T(8,128)(2,1)}, bf16[64,4,512]{2,0,1:T(8,128)(2,1)S(1)}, u32[]{:S(2)}) copy-start(bf16[64,4,512]{2,0,1:T(8,128)(2,1)S(1)} %all-to-all-done.7) | copy-start | bytes 786436
  373.0 31.1 all-to-all-start.3
  404.0 20.5 all-to-all-start.6
  424.5 33.4 all-to-all-start.8
  677.5 208.8 %all-to-all-start.4 = ((bf16[4,64,1024]{2,1,0:T(8,128)(2,1)}), bf16[4,64,1024]{2,1,0:T(8,128)(2,1)}, u32[]{:S(2)}, u32[]{:S(2)}) async-start(bf16[4,64,1024]{2,1,0:T(8,128)(2,1)} %bitcast.1490), calls=%async_computation.4 | async-start | bytes 1048576 | tf_op jit(solution)/shard_map/all_to_all | solution.py:228
  886.3 35.0 all-to-all-start.9
  946.2 118.4 %copy-start.17 = (f32[64,2048]{1,0:T(8,128)}, f32[64,2048]{1,0:T(8,128)S(1)}, u32[]{:S(2)}) copy-start(f32[64,2048]{1,0:T(8,128)S(1)} %get-tuple-element.5197) | copy-start | bytes 1572868
  946.2 118.4 %copy-start.213 = (f32[64]{0:T(128)}, f32[64]{0:T(128)S(1)}, u32[]{:S(2)}) copy-start(f32[64]{0:T(128)S(1)} %fusion.483) | copy-start | bytes 772
  951.2 113.5 %copy-start.15 = (f32[64,2048]{1,0:T(8,128)}, f32[64,2048]{1,0:T(8,128)S(1)}, u32[]{:S(2)}) copy-start(f32[64,2048]{1,0:T(8,128)S(1)} %get-tuple-element.5199) | copy-start | bytes 1572868
  951.2 113.5 %copy-start.215 = (f32[64]{0:T(128)}, f32[64]{0:T(128)S(1)}, u32[]{:S(2)}) copy-start(f32[64]{0:T(128)S(1)} %fusion.485) | copy-start | bytes 772
  1099.0 18.0 all-to-all-start.10
  1117.0 258.2 %all-to-all-start.15 = ((bf16[64,4,1024]{2,0,1:T(8,128)(2,1)}), bf16[64,4,1024]{2,0,1:T(8,128)(2,1)}, u32[]{:S(2)}, u32[]{:S(2)}) async-start(bf16[64,4,1024]{2,0,1:T(8,128)(2,1)} %bitcast.1049), calls=%async_computation.15 | async-start | bytes 1048576 | tf_op jit(solution)/shard_map/all_to_all | solution.py:252
  1621.3 34.9 all-to-all-start.14
  1656.2 10.7 all-to-all-start.19
  1677.1 14.5 all-to-all-start.11
  1704.7 13.3 all-to-all-start.16
  1718.7 15.2 all-to-all-start.13
  1733.9 13.7 all-to-all-start.18
  1737.4 1018.6 %reduce-scatter.23.cloned.1.call-start = ((), (), s32[]{:S(2)}) async-start(), calls=%async_computation.34 | async-start | bytes 4325376
  1740.3 1017.2 %reduce-scatter.21.cloned.1.call-start = ((), (), s32[]{:S(2)}) async-start(), calls=%async_computation.33 | async-start | bytes 1081344
  1742.7 1019.3 %reduce-scatter.25.cloned.1.call-start = ((), (), s32[]{:S(2)}) async-start(), calls=%async_computation.35 | async-start | bytes 1081344
  1798.4 979.0 %reduce-scatter.17.cloned.1.call-start = ((), (), s32[]{:S(2)}) async-start(), calls=%async_computation.30 | async-start | bytes 34603008 | tf_op jit(solution)/shard_map/reduce_scatter | solution.py:314
  1811.7 1800.9 %reduce-scatter.15.cloned.1.call-start = ((), (), s32[]{:S(2)}) async-start(), calls=%async_computation.29 | async-start | bytes 103809024 | tf_op jit(solution)/shard_map/reduce_scatter | solution.py:308
  1859.6 2697.0 %reduce-scatter.19.cloned.1.call-start = ((), (), s32[]{:S(2)}) async-start(), calls=%async_computation.31 | async-start | bytes 92995584 | tf_op jit(solution)/shard_map/reduce_scatter | solution.py:300
  2601.3 76.1 %copy-start.60 = (bf16[64,5504]{1,0:T(8,128)(2,1)S(1)}, bf16[64,5504]{1,0:T(8,128)(2,1)}, u32[]{:S(2)}) copy-start(bf16[64,5504]{1,0:T(8,128)(2,1)} %get-tuple-element.5117) | copy-start | bytes 2113540
  2601.3 144.0 %collective-permute-start = (f32[124,2048]{1,0:T(8,128)}, f32[124,2048]{1,0:T(8,128)}, u32[]{:S(2)}, u32[]{:S(2)}) collective-permute-start(f32[124,2048]{1,0:T(8,128)} %slice.332), channel_id=1, source_target_pairs={{0,1},{1,2},{2,3},{3,4},{4,5},{5,6},{6,7},{7,8},{8,9},{9,10},{10,1... | collective-permute-start | bytes 3047432
  (325 other events, 2812.2 us)
Sparse Core Ops, SparseCore 0:
  10.9 280.7 all-gather.7
  294.5 174.5 all-gather.13
  471.9 113.8 all-gather.9
  588.5 258.9 all-gather.11
  1740.4 144.1 reduce-scatter.22
  1887.3 167.7 reduce-scatter.20
  2057.4 136.1 reduce-scatter.24
  2196.5 580.8 reduce-scatter.16
  2784.4 828.1 reduce-scatter.14
  3615.4 941.2 reduce-scatter.18
where the time goes:
time: 4590 us; the launch traced here: 4560 us
  waiting for transfers between devices  2060 us (45%)
  blocking collectives  886 us (19%)
  matrix products  593 us (13%)
  other arithmetic  533 us (12%)
  local copies, waits for them, and re-layouts  321 us (7%)
  starting transfers between devices  145 us (3%)
    reduce_scatter x1, waiting for transfers between devices, shards(): lax.psum_scatter(outer(joined[5], joined[6]), ('seq', 'fsdp'), scatter_di...  944 us
    reduce_scatter x1, waiting for transfers between devices, shards(): lax.psum_scatter(outer(joined[0], joined[1]), ('seq', 'fsdp'), scatter_di...  835 us
    unnamed x1, blocking collectives  688 us
    another operation x80, other arithmetic, step(): lax.linalg.triangular_solve(system, target, left_side=True, lower=True, u...  330 us
    dot_general x144, matrix products, precise_total(): jnp.einsum(form, left, right, precision=lax.Precision.HIGHEST, preferred_...  181 us
    all_gather x1, waiting for transfers between devices, shards(): lax.all_gather(in_weight, ('seq', 'fsdp'), axis=0, tiled=True)  139 us
    dot_general x4, matrix products, outer(): return jnp.dot(left.T, right, preferred_element_type=jnp.float32)  109 us
  transfers between devices with their start and end apart: 29, of which 15 were waited for; matrix products, arithmetic and copies ran while one was open for 38% of the time, Pallas kernels for 0%

commit v1 on v0

v1 whole, which is shorter than its diff:
```python
from functools import partial

import jax
import jax.numpy as jnp
from jax import lax
from jax.experimental import pallas as pl
from jax.experimental.layout import Layout, with_layout_constraint
from jax.experimental.pallas import tpu as pltpu
from jax.sharding import PartitionSpec as P

D = 2048
H = 16
DK = 128
DV = 256
FF = 5504
CONV = 4
EPS = 1e-06
BLOCK = 128
LANES = 128
F32 = jnp.float32
BF16 = jnp.bfloat16


def round_up(value, step):
    return -(-value // step) * step


NN = (((1,), (0,)), ((), ()))
NT = (((1,), (1,)), ((), ()))
TN = (((0,), (0,)), ((), ()))


def dot1(left, right, form=NN):
    return lax.dot_general(
        left.astype(BF16), right.astype(BF16), form, preferred_element_type=F32
    )


def halves(value):
    high = value.astype(BF16)
    return high, (value - high.astype(F32)).astype(BF16)


def dot3(left, right, form=NN):
    left_high, left_low = halves(left)
    right_high, right_low = halves(right)
    dot = partial(lax.dot_general, dimension_numbers=form, preferred_element_type=F32)
    return dot(left_high, right_high) + (dot(left_high, right_low) + dot(left_low, right_high))


def sigmoid(value):
    return 1.0 / (1.0 + jnp.exp(-value))


def pack_masks(ends, count):
    place = lax.broadcasted_iota(jnp.int32, (count, 1), 0)
    start = jnp.zeros((count, 1), jnp.int32)
    for end in ends:
        start = jnp.where(place >= end, jnp.maximum(start, end), start)
    rows = lax.broadcasted_iota(jnp.int32, (count, count), 0)
    cols = lax.broadcasted_iota(jnp.int32, (count, count), 1)
    return place, start, rows, cols


def conv_silu(raw, taps, place, start):
    total = raw * taps[CONV - 1 : CONV]
    for lag in range(1, CONV):
        moved = pltpu.roll(raw, lag, 0)
        same = place - lag >= start
        total = total + jnp.where(same, moved, 0.0) * taps[CONV - 1 - lag : CONV - lag]
    gate = sigmoid(total)
    return total, gate, total * gate


def conv_silu_back(grad, total, gate, raw, taps, place, start):
    grad_total = grad * gate * (1.0 + total * (1.0 - gate))
    grad_raw = grad_total * taps[CONV - 1 : CONV]
    grad_taps = [None] * CONV
    grad_taps[CONV - 1] = jnp.sum(grad_total * raw, axis=0, keepdims=True)
    count = raw.shape[0]
    for lag in range(1, CONV):
        same = place - lag >= start
        kept = jnp.where(same, grad_total, 0.0)
        moved = pltpu.roll(raw, lag, 0)
        grad_taps[CONV - 1 - lag] = jnp.sum(kept * moved, axis=0, keepdims=True)
        grad_raw = grad_raw + pltpu.roll(kept, count - lag, 0) * taps[CONV - 1 - lag : CONV - lag]
    return grad_raw, grad_taps


def unit_rows(values):
    scale = lax.rsqrt(jnp.sum(values * values, axis=1, keepdims=True) + EPS)
    return values * scale, scale


def unit_rows_back(grad, values, scale):
    inner = jnp.sum(values * grad, axis=1, keepdims=True)
    return scale * grad - values * (scale * scale * scale * inner)


def column(values, lanes, index):
    return jnp.sum(jnp.where(lanes == index, values, 0.0), axis=1, keepdims=True)


def decay_grid(log_rate, start, rows, cols):
    count = log_rate.shape[0]
    lower = jnp.where(cols <= rows, 1.0, 0.0).astype(BF16)
    spread = jnp.where(cols < rows, jnp.broadcast_to(log_rate, (count, count)), 0.0)
    first = spread.astype(BF16)
    rest = spread - first.astype(F32)
    second = rest.astype(BF16)
    third = (rest - second.astype(F32)).astype(BF16)
    dot = partial(lax.dot_general, dimension_numbers=NN, preferred_element_type=F32)
    summed = dot(lower, first) + (dot(lower, second) + dot(lower, third))
    inside = (cols <= rows) & (cols >= start)
    return jnp.where(inside, jnp.exp(jnp.where(inside, summed, 0.0)), 0.0)


def unit_lower_inverse(strict):
    size = strict.shape[0]
    rows = lax.broadcasted_iota(jnp.int32, (size, size), 0)
    cols = lax.broadcasted_iota(jnp.int32, (size, size), 1)
    result = jnp.where(rows == cols, 1.0, 0.0).astype(F32)
    level = 0
    while (1 << level) < size:
        width = 1 << level
        joint = (
            ((rows >> (level + 1)) == (cols >> (level + 1)))
            & ((rows & width) != 0)
            & ((cols & width) == 0)
        )
        part = jnp.where(joint, strict, 0.0)
        if level == 0:
            result = result - part
        else:
            result = result - dot3(result, dot3(part, result))
        level += 1
    return result


def read_rows(ref, offset, width):
    shape = ref.shape
    return ref[:, 0, :, pl.ds(offset, width)].reshape(shape[0] * shape[2], width)


def write_rows(ref, offset, value):
    shape = ref.shape
    ref[:, 0, :, pl.ds(offset, value.shape[1])] = value.reshape(
        shape[0], shape[2], value.shape[1]
    ).astype(ref.dtype)


def pack_ends(lengths_ref, micro, docs):
    ends, total = [], 0
    for index in range(docs - 1):
        total = total + lengths_ref[micro, index]
        ends.append(total)
    return ends


def head_inputs(sent_ref, taps_ref, rate_ref, head, heads, place, start):
    qw = heads * DK
    out = {}
    for name, offset, width in (
        ("q", head * DK, DK),
        ("k", qw + head * DK, DK),
        ("v", 2 * qw + head * DV, DV),
    ):
        offset = pl.multiple_of(offset, LANES)
        raw = read_rows(sent_ref, offset, width).astype(F32)
        taps = taps_ref[:, pl.ds(offset, width)]
        out[name] = (offset, raw, taps) + conv_silu(raw, taps, place, start)
    offset = 2 * qw + heads * DV
    pairs = read_rows(sent_ref, offset, LANES).astype(F32)
    lanes = lax.broadcasted_iota(jnp.int32, pairs.shape, 1)
    decay_in = column(pairs, lanes, 2 * head) + rate_ref[1, head]
    soft = jnp.maximum(decay_in, 0.0) + jnp.log1p(jnp.exp(-jnp.abs(decay_in)))
    out["log"] = rate_ref[0, head] * soft
    out["decay_in"] = decay_in
    out["beta"] = sigmoid(column(pairs, lanes, 2 * head + 1))
    out["lanes"] = lanes
    return out


def mixer_forward_kernel(
    micro, per_step, heads, docs, lengths_ref, rate_ref, sent_ref, taps_ref,
    mixed_ref, update_ref, inverse_ref,
):
    count = sent_ref.shape[0] * sent_ref.shape[2]
    place, start, rows, cols = pack_masks(pack_ends(lengths_ref, micro, docs), count)
    blocks = count // BLOCK
    for local in range(per_step):
        head = pl.program_id(0) * per_step + local
        made = head_inputs(sent_ref, taps_ref, rate_ref, head, heads, place, start)
        query = unit_rows(made["q"][5])[0] * DK ** (-0.5)
        keys = unit_rows(made["k"][5])[0]
        values = made["v"][5]
        beta = made["beta"]
        decay = decay_grid(made["log"], start, rows, cols)
        system = jnp.where(cols < rows, decay, 0.0) * beta * dot3(keys, keys, NT)
        target = beta * values
        updates = []
        for block in range(blocks):
            at = slice(block * BLOCK, (block + 1) * BLOCK)
            inverse = unit_lower_inverse(system[at, at])
            inverse_ref[local, block] = inverse
            right = target[at]
            for earlier in range(block):
                right = right - dot3(
                    system[at, earlier * BLOCK : (earlier + 1) * BLOCK], updates[earlier]
                )
            updates.append(dot3(inverse, right))
        update = jnp.concatenate(updates, axis=0)
        update_ref[local] = update
        scores = decay * dot1(query, keys, NT)
        write_rows(mixed_ref, pl.multiple_of(head * DV, LANES), dot1(scores, update))


def mixer_backward_kernel(
    micro, per_step, heads, docs, lengths_ref, rate_ref, sent_ref, taps_ref,
    update_ref, inverse_ref, grad_ref,
    grad_sent_ref, grad_taps_ref, small_ref,
):
    count = sent_ref.shape[0] * sent_ref.shape[2]
    place, start, rows, cols = pack_masks(pack_ends(lengths_ref, micro, docs), count)
    blocks = count // BLOCK
    pair_offset = 2 * heads * DK + heads * DV

    @pl.when(pl.program_id(0) == 0)
    def _():
        small_ref[...] = jnp.zeros_like(small_ref)
        grad_taps_ref[...] = jnp.zeros_like(grad_taps_ref)
        write_rows(grad_sent_ref, pair_offset, jnp.zeros((count, LANES), BF16))

    grad_pairs = read_rows(grad_sent_ref, pair_offset, LANES).astype(F32)
    small_lanes = lax.broadcasted_iota(jnp.int32, (1, LANES), 1)
    for local in range(per_step):
        head = pl.program_id(0) * per_step + local
        made = head_inputs(sent_ref, taps_ref, rate_ref, head, heads, place, start)
        unit_q, scale_q = unit_rows(made["q"][5])
        query = unit_q * DK ** (-0.5)
        keys, scale_k = unit_rows(made["k"][5])
        values = made["v"][5]
        beta = made["beta"]
        grad_mixed = read_rows(grad_ref, pl.multiple_of(head * DV, LANES), DV)
        decay = decay_grid(made["log"], start, rows, cols)
        strict = jnp.where(cols < rows, decay, 0.0)
        keys_keys = dot3(keys, keys, NT)
        weighted = strict * beta
        system = weighted * keys_keys
        scores = decay * dot1(query, keys, NT)
        update = update_ref[local]
        grad_scores = dot1(grad_mixed, update, NT)
        grad_update = dot1(scores, grad_mixed, TN)
        grad_targets = [None] * blocks
        for block in reversed(range(blocks)):
            at = slice(block * BLOCK, (block + 1) * BLOCK)
            right = grad_update[at]
            for later in range(block + 1, blocks):
                right = right - dot3(
                    system[later * BLOCK : (later + 1) * BLOCK, at], grad_targets[later], TN
                )
            grad_targets[block] = dot3(inverse_ref[local, block], right, TN)
        grad_target = jnp.concatenate(grad_targets, axis=0)
        grad_system = -dot1(grad_target, update, NT)
        grad_values = beta * grad_target
        grad_beta = jnp.sum(grad_target * values, axis=1, keepdims=True) + jnp.sum(
            grad_system * strict * keys_keys, axis=1, keepdims=True
        )
        grad_kk = grad_system * weighted
        grad_qk = grad_scores * decay
        grad_query = dot1(grad_qk, keys) * DK ** (-0.5)
        grad_keys = dot1(grad_kk, keys) + dot1(grad_kk, keys, TN) + dot1(grad_qk, query, TN)
        grad_spread = grad_scores * scores + grad_system * system
        lower = jnp.where(cols <= rows, 1.0, 0.0).astype(BF16)
        high, low = halves(grad_spread)
        dot = partial(lax.dot_general, dimension_numbers=TN, preferred_element_type=F32)
        after = dot(lower, high) + dot(lower, low)
        grad_log = jnp.sum(jnp.where(cols < rows, after, 0.0), axis=1, keepdims=True)
        grad_decay = grad_log * rate_ref[0, head] * sigmoid(made["decay_in"])
        grad_beta_in = grad_beta * beta * (1.0 - beta)
        lanes = made["lanes"]
        grad_pairs = jnp.where(lanes == 2 * head, grad_decay, grad_pairs)
        grad_pairs = jnp.where(lanes == 2 * head + 1, grad_beta_in, grad_pairs)
        grad_alog = jnp.sum(grad_log * made["log"], axis=0, keepdims=True)
        grad_dt = jnp.sum(grad_decay, axis=0, keepdims=True)
        small_ref[0:1] += jnp.where(small_lanes == head, grad_alog, 0.0)
        small_ref[1:2] += jnp.where(small_lanes == head, grad_dt, 0.0)
        for name, grad in (
            ("q", unit_rows_back(grad_query, made["q"][5], scale_q)),
            ("k", unit_rows_back(grad_keys, made["k"][5], scale_k)),
            ("v", grad_values),
        ):
            where, raw, taps, total, opened, _ = made[name]
            grad_raw, grad_taps = conv_silu_back(grad, total, opened, raw, taps, place, start)
            write_rows(grad_sent_ref, where, grad_raw)
            for tap in range(CONV):
                grad_taps_ref[tap : tap + 1, pl.ds(where, raw.shape[1])] += grad_taps[tap]
    write_rows(grad_sent_ref, pair_offset, grad_pairs)


def gate_forward_kernel(heads, mixed_ref, gate_ref, gain_ref, normed_ref):
    for head in range(heads):
        offset = head * DV
        mixed = read_rows(mixed_ref, offset, DV).astype(F32)
        gate = read_rows(gate_ref, offset, DV)
        scale = lax.rsqrt(jnp.mean(mixed * mixed, axis=1, keepdims=True) + EPS)
        write_rows(normed_ref, offset, mixed * scale * gain_ref[...] * (gate * sigmoid(gate)))


def gate_backward_kernel(
    heads, mixed_ref, gate_ref, gain_ref, grad_ref, grad_mixed_ref, grad_gate_ref, grad_gain_ref
):
    @pl.when(pl.program_id(0) == 0)
    def _():
        grad_gain_ref[...] = jnp.zeros_like(grad_gain_ref)

    gain = gain_ref[...]
    for head in range(heads):
        offset = head * DV
        mixed = read_rows(mixed_ref, offset, DV).astype(F32)
        gate = read_rows(gate_ref, offset, DV)
        grad = read_rows(grad_ref, offset, DV)
        scale = lax.rsqrt(jnp.mean(mixed * mixed, axis=1, keepdims=True) + EPS)
        soft = sigmoid(gate)
        plain_rows = mixed * scale
        write_rows(
            grad_gate_ref, offset, grad * plain_rows * gain * soft * (1.0 + gate * (1.0 - soft))
        )
        grad = grad * (gate * soft)
        grad_gain_ref[...] += jnp.sum(grad * plain_rows, axis=0, keepdims=True)
        grad = grad * gain
        inner = jnp.mean(mixed * grad, axis=1, keepdims=True)
        write_rows(
            grad_mixed_ref, offset, scale * grad - mixed * (scale * scale * scale * inner)
        )


def row_spec(array, micro):
    spans, micros, length, width = array.shape
    pick = micro if micros > 1 else 0
    return pl.BlockSpec((spans, 1, length, width), lambda h: (0, pick, 0, 0))


def span_spec(array, micro):
    _, micros, length, width = array.shape
    pick = micro if micros > 1 else 0
    return pl.BlockSpec((1, 1, length, width), lambda s: (s, pick, 0, 0))


def whole_spec(*dims):
    return pl.BlockSpec(dims, lambda h: (0,) * len(dims))


def mixer_cost(sent, heads, passes):
    count = sent.shape[0] * sent.shape[2]
    return pl.CostEstimate(
        flops=passes * heads * 2 * count * count * DV,
        bytes_accessed=passes * heads * count * count * 4,
        transcendentals=heads * count * count,
    )


def mixer_forward(micro, lengths, rates, sent, taps, heads):
    spans, _, length, width = sent.shape
    count, per_step = spans * length, 2 if heads % 2 == 0 else 1
    blocks = count // BLOCK
    smem = pl.BlockSpec(memory_space=pltpu.SMEM)
    mixed = jax.ShapeDtypeStruct((spans, 1, length, heads * DV), BF16)
    return pl.pallas_call(
        partial(mixer_forward_kernel, micro, per_step, heads, lengths.shape[1]),
        grid=(heads // per_step,),
        in_specs=[smem, smem, row_spec(sent, micro), whole_spec(CONV, width)],
        out_specs=[
            row_spec(mixed, 0),
            pl.BlockSpec((per_step, count, DV), lambda h: (h, 0, 0)),
            pl.BlockSpec((per_step, blocks, BLOCK, BLOCK), lambda h: (h, 0, 0, 0)),
        ],
        out_shape=[
            mixed,
            jax.ShapeDtypeStruct((heads, count, DV), F32),
            jax.ShapeDtypeStruct((heads, blocks, BLOCK, BLOCK), F32),
        ],
        compiler_params=pltpu.CompilerParams(vmem_limit_bytes=40 * 1024 * 1024),
        cost_estimate=mixer_cost(sent, heads, 60),
        name="mixer_forward",
    )(lengths, rates, sent, taps)


def mixer_backward(micro, lengths, rates, sent, taps, update, inverse, grad, heads):
    spans, _, length, width = sent.shape
    count, per_step = spans * length, 2 if heads % 2 == 0 else 1
    blocks = count // BLOCK
    smem = pl.BlockSpec(memory_space=pltpu.SMEM)
    grad_sent = jax.ShapeDtypeStruct((spans, 1, length, width), BF16)
    return pl.pallas_call(
        partial(mixer_backward_kernel, micro, per_step, heads, lengths.shape[1]),
        grid=(heads // per_step,),
        in_specs=[
            smem, smem, row_spec(sent, micro), whole_spec(CONV, width),
            pl.BlockSpec((per_step, count, DV), lambda h: (h, 0, 0)),
            pl.BlockSpec((per_step, blocks, BLOCK, BLOCK), lambda h: (h, 0, 0, 0)),
            row_spec(grad, 0),
        ],
        out_specs=[row_spec(grad_sent, 0), whole_spec(CONV, width), whole_spec(8, LANES)],
        out_shape=[
            grad_sent,
            jax.ShapeDtypeStruct((CONV, width), F32),
            jax.ShapeDtypeStruct((8, LANES), F32),
        ],
        compiler_params=pltpu.CompilerParams(vmem_limit_bytes=40 * 1024 * 1024),
        cost_estimate=mixer_cost(sent, heads, 40),
        name="mixer_backward",
    )(lengths, rates, sent, taps, update, inverse, grad)


def gate_forward(micro, mixed, gate, gain, heads):
    return pl.pallas_call(
        partial(gate_forward_kernel, heads),
        grid=(mixed.shape[0],),
        in_specs=[span_spec(mixed, 0), span_spec(gate, micro), whole_spec(1, DV)],
        out_specs=span_spec(mixed, 0),
        out_shape=jax.ShapeDtypeStruct(mixed.shape, BF16),
        cost_estimate=pl.CostEstimate(
            flops=20 * mixed.size, bytes_accessed=8 * mixed.size, transcendentals=mixed.size
        ),
        name="gate_forward",
    )(mixed, gate, gain)


def gate_backward(micro, mixed, gate, gain, grad, heads):
    out = jax.ShapeDtypeStruct(mixed.shape, BF16)
    return pl.pallas_call(
        partial(gate_backward_kernel, heads),
        grid=(mixed.shape[0],),
        in_specs=[
            span_spec(mixed, 0), span_spec(gate, micro), whole_spec(1, DV), span_spec(grad, 0),
        ],
        out_specs=[span_spec(out, 0), span_spec(out, 0), whole_spec(1, DV)],
        out_shape=[out, out, jax.ShapeDtypeStruct((1, DV), F32)],
        cost_estimate=pl.CostEstimate(
            flops=40 * mixed.size, bytes_accessed=14 * mixed.size, transcendentals=mixed.size
        ),
        name="gate_backward",
    )(mixed, gate, gain, grad)


def dot(left, right):
    return jnp.dot(left, right, preferred_element_type=F32)


def outer(left, right):
    return lax.dot_general(left, right, TN, preferred_element_type=F32)


def dot_back(left, right):
    return lax.dot_general(left, right, NT, preferred_element_type=F32)


def after(value, *earlier):
    return lax.optimization_barrier((value,) + earlier)[0]


def plain(array):
    return with_layout_constraint(array, Layout(major_to_minor=tuple(range(array.ndim))))


def exchange(blocks):
    return lax.all_to_all(blocks, "seq", split_axis=0, concat_axis=0, tiled=True)


def gather_rows(rows):
    spans = lax.axis_size("seq")
    return exchange(jnp.broadcast_to(rows[None], (spans,) + rows.shape))


def scatter_rows(partial_rows, spans):
    return exchange(
        partial_rows.astype(BF16).reshape((spans, -1) + partial_rows.shape[1:])
    )


def norm_scale(values):
    return lax.rsqrt(jnp.mean(values * values, axis=-1, keepdims=True) + EPS)


def norm_back(values, gain, grad):
    scale = norm_scale(values)
    inner = gain * grad
    back = scale * inner - values * (
        scale * scale * scale * jnp.mean(values * inner, axis=-1, keepdims=True)
    )
    return back, jnp.sum(values * scale * grad, axis=0)


def shards(
    tokens, lengths, in_weight, decay_weight, conv_weight, a_log, dt_bias, norm_gains, out_gain,
    out_weight, up_weight, down_weight, cotangent,
):
    spans, packs = lax.axis_size("seq"), lax.axis_size("fsdp")
    place = lax.axis_index("seq")
    micros, _, length, _ = tokens.shape
    heads = H // spans
    qw, vw, fw = heads * DK, heads * DV, FF // spans
    fp = round_up(fw, LANES)
    share = in_weight.shape[0]
    local_rows = micros * length

    def columns(array, start, count):
        return array[:, start : start + count * spans].reshape(share, spans, count)

    def widen(array, count):
        return jnp.pad(array, ((0, 0), (0, 0), (0, count - array.shape[2])))

    def by_span(pieces):
        return jnp.concatenate(pieces, axis=2).swapaxes(0, 1)

    def gather_weight(blocks):
        full = plain(lax.all_gather(plain(blocks), "fsdp", axis=1, tiled=True))
        return full.reshape(D, blocks.shape[2])

    conv_share = conv_weight.shape[0]
    conv_cols = CONV * conv_share // share
    small = jnp.concatenate([conv_weight.reshape(share, conv_cols), norm_gains.T], axis=1)
    small = jnp.broadcast_to(small[:, None], (share, spans, conv_cols + 2))
    pairs = jnp.concatenate([decay_weight.reshape(share, spans, 2 * heads), small], axis=2)
    pair_at = 2 * qw + vw
    mix_width = pair_at + LANES
    mix_blocks = by_span([
        columns(in_weight, 0, qw),
        columns(in_weight, H * DK, qw),
        columns(in_weight, 2 * H * DK, vw),
        widen(pairs, LANES),
    ])
    gate_blocks = by_span([columns(in_weight, 2 * H * DK + H * DV, vw)])
    up_blocks = by_span([
        widen(columns(up_weight, 0, fw), fp),
        widen(columns(up_weight, FF, fw), fp),
    ])
    local_tokens = tokens.reshape(local_rows, D)
    local_cot = cotangent.reshape(local_rows, D)
    grouped = (spans, micros, length)
    all_rows = spans * local_rows

    mix_blocks, up_blocks = lax.optimization_barrier((exchange(mix_blocks), up_blocks))
    w_mix = gather_weight(mix_blocks)
    all_tokens = gather_rows(after(local_tokens, mix_blocks))
    gate_blocks = exchange(after(gate_blocks, all_tokens))
    w_gate = gather_weight(after(gate_blocks, w_mix))
    w_out = lax.all_gather(after(out_weight, w_mix), "fsdp", axis=0, tiled=True)

    small = w_mix[:, pair_at + 2 * heads : pair_at + 2 * heads + conv_cols + 2]
    gains = small[:, conv_cols:].T.astype(F32)

    def own(base, width):
        step = conv_share // share
        rows = lax.dynamic_slice_in_dim(
            small[:, :conv_cols], (base + place * width) // step, width // step, axis=0
        )
        return rows.reshape(width, CONV).T

    taps = jnp.concatenate(
        [own(0, qw), own(H * DK, qw), own(2 * H * DK, vw), jnp.zeros((CONV, LANES), BF16)],
        axis=1,
    ).astype(F32)
    rates = jnp.stack([
        -jnp.exp(lax.dynamic_slice_in_dim(a_log, place * heads, heads)),
        lax.dynamic_slice_in_dim(dt_bias, place * heads, heads),
    ])
    gain_row = out_gain.reshape(1, DV)
    pack_lengths = lengths[:, 0]

    inputs = all_tokens.reshape(all_rows, D).astype(F32)
    input_scale = norm_scale(inputs)
    first = (inputs * input_scale * gains[0]).astype(BF16)
    sent = dot(first, w_mix).astype(BF16).reshape(grouped + (mix_width,))
    w_down = lax.all_gather(after(down_weight, sent), "fsdp", axis=0)
    cot = gather_rows(after(local_cot, sent)).reshape(all_rows, D)
    mixers = []
    for micro in range(micros):
        mixers.append(
            mixer_forward(micro, pack_lengths, rates, sent, taps, heads)
        )
        if micro == 0:
            up_blocks = exchange(after(up_blocks, cot, mixers[0][0]))
        sent = after(sent, mixers[-1][0])
    w_down = lax.optimization_barrier(w_down.reshape(fw, D))
    w_up = gather_weight(after(up_blocks, mixers[-1][0]))
    gate = dot(first, w_gate).reshape(grouped + (vw,))
    grad_act = dot_back(cot, w_down).reshape(grouped + (fw,))

    def part(array, micro):
        return array.reshape((micros, length) + array.shape[1:])[micro]

    normeds, branches = [], []
    for micro in range(micros):
        normeds.append(gate_forward(micro, mixers[micro][0], gate, gain_row, heads))
        rows = dot(normeds[-1].reshape(-1, vw), w_out).astype(BF16)
        branches.append(scatter_rows(after(rows, up_blocks), spans))
    middles, seconds = [], []
    for micro in range(micros):
        middle = part(local_tokens, micro).astype(F32) + jnp.sum(
            branches[micro].astype(F32), axis=0
        )
        middles.append(middle)
        seconds.append(gather_rows((middle * norm_scale(middle) * gains[1]).astype(BF16)))

    acts, grad_boths, grad_seconds, sums = [], [], [], [None] * micros
    for micro in range(micros):
        both = dot(seconds[micro].reshape(-1, D), w_up)
        gated, upper = both[:, :fp], both[:, fp:]
        soft = jax.nn.sigmoid(gated)
        acts.append((gated * soft * upper).astype(BF16).reshape(spans, length, fp))
        grad = jnp.pad(grad_act[:, micro].reshape(-1, fw), ((0, 0), (0, fp - fw)))
        grad_both = jnp.concatenate(
            [
                (grad * upper * soft * (1.0 + gated * (1.0 - soft))).astype(BF16),
                (grad * gated * soft).astype(BF16),
            ],
            axis=1,
        )
        grad_boths.append(grad_both.reshape(spans, length, 2 * fp))
        rows = dot_back(grad_both, w_up).astype(BF16)
        grad_seconds.append(scatter_rows(rows, spans))
    act = jnp.stack(acts, axis=1).reshape(all_rows, fp)[:, :fw]
    final_rows = [dot(a.reshape(-1, fp)[:, :fw], w_down).astype(BF16) for a in acts]
    down_grads = outer(act, cot).astype(BF16).reshape(packs, -1, D)
    spare = [final_rows[:1], final_rows[1:] + [down_grads]]
    grad_middles, grad_branches, grad_gain2 = [], [], 0.0
    for micro in range(micros):
        grad_second = jnp.sum(
            after(grad_seconds[micro], *spare[min(micro, 1)]).astype(F32), axis=0
        )
        grad_norm, grad_gain = norm_back(middles[micro], gains[1], grad_second)
        grad_gain2 = grad_gain2 + grad_gain
        grad_middles.append(part(local_cot, micro).astype(F32) + grad_norm)
        grad_branches.append(gather_rows(grad_middles[-1].astype(BF16)))

    def reduce_rows(grad, blocks):
        blocks = plain(grad.astype(BF16).reshape(blocks, -1, grad.shape[1]))
        return plain(lax.psum_scatter(blocks, "fsdp", scatter_dimension=1, tiled=True))

    def joined(blocks, start, width):
        return blocks[:, :, start : start + width].swapaxes(0, 1).astype(F32).reshape(share, -1)

    def all_micros(parts):
        return jnp.stack(parts, axis=1).reshape(all_rows, parts[0].shape[-1])

    up_grads = reduce_rows(
        outer(after(all_micros(seconds), grad_seconds[0]), all_micros(grad_boths)), spans
    )
    finals, waits = [], grad_branches[-1]
    for micro in range(micros):
        waits = scatter_rows(after(final_rows[micro], waits), spans)
        finals.append(middles[micro] + jnp.sum(waits.astype(F32), axis=0))
        sums[micro] = waits
    block_out = jnp.stack(finals).reshape(local_rows, D)

    grad_mixeds, grad_gates, grad_gain = [], [], 0.0
    for micro in range(micros):
        grad = dot_back(grad_branches[micro].reshape(-1, D), w_out)
        grad_mixed, grad_gate, term = gate_backward(
            micro, mixers[micro][0], gate, gain_row,
            grad.reshape(spans, 1, length, vw), heads,
        )
        grad_mixeds.append(grad_mixed)
        grad_gates.append(grad_gate.reshape(spans, length, vw))
        grad_gain = grad_gain + term
    grad_mixeds[0] = after(grad_mixeds[0], up_grads)
    grad_sents, grad_taps, grad_small = [], 0.0, 0.0
    for micro in range(micros):
        _, update, inverse = mixers[micro]
        grad_sent, term_taps, term_small = mixer_backward(
            micro, pack_lengths, rates, sent, taps, update, inverse, grad_mixeds[micro], heads
        )
        if micro + 1 < micros:
            grad_mixeds[micro + 1] = after(grad_mixeds[micro + 1], grad_sent)
        grad_sents.append(grad_sent.reshape(spans, length, mix_width))
        grad_taps, grad_small = grad_taps + term_taps, grad_small + term_small
    grad_proj = all_micros([
        jnp.concatenate(pair, axis=-1) for pair in zip(grad_sents, grad_gates)
    ])
    in_product = outer(after(first, sums[-1]), grad_proj)
    in_grads = reduce_rows(in_product, spans)
    grad_first = dot_back(grad_proj[:, :mix_width], w_mix) + dot_back(
        grad_proj[:, mix_width:], w_gate
    )
    grad_gain1 = jnp.sum(inputs * input_scale * grad_first, axis=0)
    first_rows = grad_first.astype(BF16)
    grad_first = scatter_rows(first_rows, spans)
    out_grads = outer(
        after(all_micros([n[:, 0] for n in normeds]), first_rows), all_micros(grad_branches)
    )
    out_grads = out_grads.astype(BF16).reshape(packs, -1, D)
    down_rows = down_grads.shape[1]
    row_grads = lax.psum_scatter(
        after(jnp.concatenate([out_grads, down_grads], axis=1), in_product),
        "fsdp", scatter_dimension=0,
    ).astype(F32)
    grad_out, grad_down = row_grads[:-down_rows], row_grads[-down_rows:]
    grad_norm1, _ = norm_back(
        local_tokens.astype(F32), gains[0], jnp.sum(grad_first.astype(F32), axis=0)
    )
    grad_tokens = jnp.stack(grad_middles).reshape(local_rows, D) + grad_norm1
    up_grads = exchange(after(up_grads, grad_first))
    in_grads = exchange(after(in_grads, up_grads))
    grad_up = jnp.concatenate([joined(up_grads, 0, fw), joined(up_grads, fp, fw)], axis=1)
    grad_in = jnp.concatenate(
        [
            joined(in_grads, 0, qw),
            joined(in_grads, qw, qw),
            joined(in_grads, 2 * qw, vw),
            joined(in_grads, mix_width, vw),
        ],
        axis=1,
    )
    grad_decay = joined(in_grads, pair_at, 2 * heads)

    gain_rows = jnp.stack([grad_gain1, grad_gain2])
    flat = jnp.concatenate([
        grad_taps[:, :pair_at].reshape(-1), gain_rows.reshape(-1), grad_gain.reshape(-1),
        grad_small[:2].reshape(-1),
    ])
    flat = jnp.pad(flat, (0, round_up(flat.size, 8 * LANES) - flat.size)).reshape(-1, LANES)
    flat = lax.psum(flat, "fsdp")
    flat = lax.all_gather(flat, "seq", axis=0).reshape(spans, -1)
    taps_flat = flat[:, : CONV * pair_at].reshape(spans, CONV, pair_at)

    def all_taps(start, width):
        return taps_flat[:, :, start : start + width].swapaxes(0, 1).reshape(CONV, -1)

    grad_conv = jnp.concatenate(
        [all_taps(0, qw), all_taps(qw, qw), all_taps(2 * qw, vw)], axis=1
    )
    index = place * packs + lax.axis_index("fsdp")
    grad_conv = lax.dynamic_slice_in_dim(grad_conv, index * conv_share, conv_share, axis=1).T
    at = CONV * pair_at
    gains_flat = jnp.sum(flat[:, at : at + 2 * D], axis=0).reshape(2, D)
    gain_share = norm_gains.shape[1]
    grad_gains = lax.dynamic_slice_in_dim(gains_flat, index * gain_share, gain_share, axis=1)
    at = at + 2 * D
    grad_gain = jnp.sum(flat[:, at : at + DV], axis=0)
    at = at + DV
    return (
        block_out.astype(BF16).reshape(micros, 1, length, D),
        grad_tokens.reshape(micros, 1, length, D),
        grad_in,
        grad_decay,
        grad_conv,
        flat[:, at : at + heads].reshape(H),
        flat[:, at + LANES : at + LANES + heads].reshape(H),
        grad_gains,
        grad_gain,
        grad_out,
        grad_up,
        grad_down,
    )


def solution(mesh):
    rows = P(("seq", "fsdp"), None)
    packs = P(None, "fsdp", "seq", None)
    gains = P(None, ("seq", "fsdp"))
    return jax.shard_map(
        shards,
        mesh=mesh,
        in_specs=(
            packs, P(None, "fsdp", None), rows, rows, rows, P(), P(), gains, P(), rows, rows, rows,
            packs,
        ),
        out_specs=(packs, packs, rows, rows, rows, P(), P(), gains, P(), rows, rows, rows),
        check_vma=False,
    )
```

time: 4590 us -> 818 us (0.18)
  waiting for transfers between devices: 2060 us -> 308 us
  blocking collectives: 886 us -> 94.6 us
  other arithmetic: 533 us -> 54.1 us
  matrix products: 593 us -> 130 us
  local copies, waits for them, and re-layouts: 321 us -> 56.2 us
  Pallas kernels: 0 us -> 78.6 us
  starting transfers between devices: 145 us -> 72.5 us
    reduce_scatter x3, waiting for transfers between devices: 1790 us -> 60.1 us  [the longest x1 60.1 us: shards(): lax.psum_scatter(after(jnp.concatenate([out_grads, down_grads], axis=1),...]
    unnamed x1 -> x0, blocking collectives: 688 us -> none
    dot_general x176 -> x19, matrix products: 555 us -> 130 us  [the longest x8 50.7 us: dot(): return jnp.dot(left, right, preferred_element_type=F32)]
    another operation x109 -> x12, other arithmetic: 348 us -> 9.98 us  [the longest x7 7.01 us: all_micros(): return jnp.stack(parts, axis=1).reshape(all_rows, parts[0].shape[-1])]
    all_gather x4 -> x5, waiting for transfers between devices: 139 us -> 0.05 us  [the longest x3 0.02 us: gather_weight(): full = plain(lax.all_gather(plain(blocks), 'fsdp', axis=1, tiled=True))]
    all_to_all x18 -> x16, waiting for transfers between devices: 120 us -> 247 us  [exchange(): lax.all_to_all(blocks, 'seq', split_axis=0, concat_axis=0, tiled=True)]
    all_gather x3 -> x1, blocking collectives: 123 us -> 23.1 us  [shards(): flat = lax.all_gather(flat, 'seq', axis=0).reshape(spans, -1)]
    pallas_call x0 -> x8, Pallas kernels: none -> 78.6 us  [the longest x2 40.4 us: mixer_forward(): pl.pallas_call(partial(mixer_forward_kernel, micro, per_step, heads, leng...]
  transfers between devices with their start and end apart: 29 -> 24, of which waited for: 15 -> 13; matrix products, arithmetic and copies ran while one was open for 38% -> 22% of each run, Pallas kernels for 0% -> 10%
where the time goes in v1:
time: 818 us; the launch traced here: 810 us
  waiting for transfers between devices  308 us (38%)
  matrix products  130 us (16%)
  blocking collectives  94.6 us (12%)
  Pallas kernels  78.6 us (10%)
  starting transfers between devices  72.5 us (9%)
  local copies, waits for them, and re-layouts  56.2 us (7%)
  other arithmetic  54.1 us (7%)
  between operations  15.9 us (2%)
    all_to_all x16, waiting for transfers between devices, exchange(): lax.all_to_all(blocks, 'seq', split_axis=0, concat_axis=0, tiled=True)  247 us
    all_to_all x16, starting transfers between devices, exchange(): lax.all_to_all(blocks, 'seq', split_axis=0, concat_axis=0, tiled=True)  71.3 us
    reduce_scatter x1, waiting for transfers between devices, shards(): lax.psum_scatter(after(jnp.concatenate([out_grads, down_grads], axis=1),...  60.1 us
    dot_general x8, matrix products, dot(): return jnp.dot(left, right, preferred_element_type=F32)  50.7 us
    all_to_all x2, blocking collectives, exchange(): lax.all_to_all(blocks, 'seq', split_axis=0, concat_axis=0, tiled=True)  46.9 us
    dot_general x7, matrix products, dot_back(): return lax.dot_general(left, right, NT, preferred_element_type=F32)  46.2 us
    pallas_call x2, Pallas kernels, mixer_forward(): pl.pallas_call(partial(mixer_forward_kernel, micro, per_step, heads, leng...  40.4 us
    dot_general x4, matrix products, outer(): return lax.dot_general(left, right, TN, preferred_element_type=F32)  33.1 us
  transfers between devices with their start and end apart: 24, of which 13 were waited for; matrix products, arithmetic and copies ran while one was open for 22% of the time, Pallas kernels for 10%

profile of v1, /device:TPU:0, one launch (start us, length us, event | category | flops | bytes accessed | tf_op | source)
XLA Modules:
  0.0 809.6 jit_solution(1507461473701872065)
XLA Ops:
  12.3 6.3 all-to-all-start
  25.3 20.4 %all-to-all-done = bf16[4,64,2176]{2,1,0:T(8,128)(2,1)S(1)} async-done(((bf16[4,64,2176]{2,1,0:T(8,128)(2,1)}), bf16[4,64,2176]{2,1,0:T(8,128)(2,1)S(1)}, u32[]{:S(2)}, u32[]{:S(2)}) %all-to-all-start) | async-done | bytes 1114144 | tf_op jit(solution)/shard_map/all_to_all | solution.py:468
  52.2 47.6 %all-to-all-done.1 = bf16[4,128,2048]{2,1,0:T(8,128)(2,1)S(1)} async-done(((bf16[4,128,2048]{2,1,0:T(8,128)(2,1)}), bf16[4,128,2048]{2,1,0:T(8,128)(2,1)S(1)}, u32[]{:S(2)}, u32[]{:S(2)}) %all-to-all-start.1) | async-done | bytes 2097184 | tf_op jit(solution)/shard_map/all_to_all | solution.py:468
  99.8 17.1 %all_to_all.90 = bf16[4,64,1024]{2,1,0:T(8,128)(2,1)} all-to-all(bf16[4,64,1024]{2,1,0:T(8,128)(2,1)S(1)} %bitcast.344), channel_id=1, replica_groups=mesh['seq'=4,'fsdp'=8] {'seq'}, dimensions={0} | all-to-all | bytes 1048576 | tf_op jit(solution)/shard_map/all_to_all | solution.py:468
  120.9 10.0 %convolution_convert_fusion.2 = bf16[512,2176]{1,0:T(8,128)(2,1)S(1)} fusion(bf16[512,2048]{1,0:T(8,128)(2,1)S(1)} %bitcast.345, bf16[2048,2176]{1,0:T(8,128)(2,1)} %bitcast.386), kind=kOutput, calls=%fused_computation.5 | convolution fusion | flops 4564516864 | bytes 13238272 | tf_op jit(solution)/shard_map/dot_general | solution.py:448
  132.6 4.9 all-to-all-start.3
  139.9 20.2 %mixer_forward.2 = (bf16[4,1,64,1024]{3,2,1,0:T(8,128)(2,1)S(1)}, f32[4,256,256]{2,1,0:T(8,128)S(1)}, f32[4,2,128,128]{3,2,1,0:T(8,128)S(1)}) custom-call(s32[2,4]{1,0:T(2,128)S(1)} %bitcast.311, f32[2,4]{1,0:T(2,128)S(1)} %pad_maximum_fusion.11.rate_ref, bf16[4,2,64,2176]{3,2,1,0:T(8,128)(2,1)S(1)} %bitcast.315, f32[4,2176]{1,0:T(4,128)S(1)} %maximum_convert_fusion.2.taps_ref), custom_call_target="tpu_custom_call" | custom-call | flops 8053063680 | bytes 62914560 | tf_op jit(solution)/shard_map/mixer_forward/pallas_call | solution.py:369
  161.9 22.7 %all-to-all-done.3 = bf16[4,128,2048]{2,1,0:T(8,128)(2,1)} async-done(((bf16[4,128,2048]{2,1,0:T(8,128)(2,1)}), bf16[4,128,2048]{2,1,0:T(8,128)(2,1)}, u32[]{:S(2)}, u32[]{:S(2)}) %all-to-all-start.3) | async-done | bytes 2097184 | tf_op jit(solution)/shard_map/all_to_all | solution.py:468
  184.6 4.3 all-to-all-start.4
  189.5 20.2 %mixer_forward.3 = (bf16[4,1,64,1024]{3,2,1,0:T(8,128)(2,1)S(1)}, f32[4,256,256]{2,1,0:T(8,128)S(1)}, f32[4,2,128,128]{3,2,1,0:T(8,128)S(1)}) custom-call(s32[2,4]{1,0:T(2,128)S(1)} %bitcast.312, f32[2,4]{1,0:T(2,128)S(1)} %pad_maximum_fusion.11.rate_ref, bf16[4,2,64,2176]{3,2,1,0:T(8,128)(2,1)S(1)} %bitcast.316, f32[4,2176]{1,0:T(4,128)S(1)} %maximum_convert_fusion.2.taps_ref), custom_call_target="tpu_custom_call" | custom-call | flops 8053063680 | bytes 62914560 | tf_op jit(solution)/shard_map/mixer_forward/pallas_call | solution.py:369
  211.6 11.1 %all-to-all-done.4 = bf16[4,64,2816]{2,1,0:T(8,128)(2,1)} async-done(((bf16[4,64,2816]{2,1,0:T(8,128)(2,1)}), bf16[4,64,2816]{2,1,0:T(8,128)(2,1)}, u32[]{:S(2)}, u32[]{:S(2)}) %all-to-all-start.4) | async-done | bytes 1441824 | tf_op jit(solution)/shard_map/all_to_all | solution.py:468
  222.7 6.6 fusion.64.gate_ref
  233.0 4.6 convolution_convert_fusion.7
  245.6 5.1 convolution_convert_fusion.6
  250.7 16.4 %all-to-all-done.5 = bf16[4,64,2048]{2,1,0:T(8,128)(2,1)} async-done(((bf16[4,64,2048]{2,1,0:T(8,128)(2,1)}), bf16[4,64,2048]{2,1,0:T(8,128)(2,1)}, u32[]{:S(2)}, u32[]{:S(2)}) %all-to-all-start.5) | async-done | bytes 1048608 | tf_op jit(solution)/shard_map/all_to_all | solution.py:468
  274.0 22.7 %all-to-all-done.7 = bf16[4,64,2048]{2,1,0:T(8,128)(2,1)} async-done(((bf16[4,64,2048]{2,1,0:T(8,128)(2,1)}), bf16[4,64,2048]{2,1,0:T(8,128)(2,1)}, u32[]{:S(2)}, u32[]{:S(2)}) %all-to-all-start.7) | async-done | bytes 1048608 | tf_op jit(solution)/shard_map/all_to_all | solution.py:468
  306.0 5.9 reshape.980
  311.9 19.3 %all-to-all-done.6 = bf16[4,64,2048]{2,1,0:T(8,128)(2,1)} async-done(((bf16[4,64,2048]{2,1,0:T(8,128)(2,1)}), bf16[4,64,2048]{2,1,0:T(8,128)(2,1)}, u32[]{:S(2)}, u32[]{:S(2)}) %all-to-all-start.6) | async-done | bytes 1048608 | tf_op jit(solution)/shard_map/all_to_all | solution.py:468
  333.2 4.4 all-to-all-start.8
  337.6 6.5 fusion
  345.9 17.0 %all-to-all-done.8 = bf16[4,64,2048]{2,1,0:T(8,128)(2,1)} async-done(((bf16[4,64,2048]{2,1,0:T(8,128)(2,1)}), bf16[4,64,2048]{2,1,0:T(8,128)(2,1)}, u32[]{:S(2)}, u32[]{:S(2)}) %all-to-all-start.8) | async-done | bytes 1048608 | tf_op jit(solution)/shard_map/all_to_all | solution.py:468
  366.0 6.6 fusion.65
  374.3 8.9 %convolution_convert_fusion.4 = bf16[256,2048]{1,0:T(8,128)(2,1)} fusion(bf16[2048,2816]{1,0:T(8,128)(2,1)} %bitcast.407, bf16[256,1408]{1,0:T(8,128)(2,1)S(1)} %get-tuple-element.111, bf16[256,1408]{1,0:T(8,128)(2,1)S(1)} %get-tuple-element.110), kind=kOutput, calls=%fused_computation.24 | convolution fusion | flops 2956197888 | bytes 14024704 | tf_op jit(solution)/shard_map/dot_general | solution.py:456
  387.8 6.7 fusion.66
  400.5 12.3 %all-to-all-done.13 = bf16[4,64,2048]{2,1,0:T(8,128)(2,1)} async-done(((bf16[4,64,2048]{2,1,0:T(8,128)(2,1)}), bf16[4,64,2048]{2,1,0:T(8,128)(2,1)}, u32[]{:S(2)}, u32[]{:S(2)}) %all-to-all-start.13) | async-done | bytes 1048608 | tf_op jit(solution)/shard_map/all_to_all | solution.py:468
  412.8 11.1 %convolution_convert_fusion = bf16[2048,2816]{1,0:T(8,128)(2,1)} fusion(bf16[512,2048]{1,0:T(8,128)(2,1)} %bitcast.342, bf16[512,2816]{1,0:T(8,128)(2,1)} %bitcast.337), kind=kOutput, calls=%fused_computation | convolution fusion | flops 5911347200 | bytes 16515072 | tf_op jit(solution)/shard_map/dot_general | solution.py:452
  423.9 8.9 %convolution_convert_fusion.5 = bf16[256,2048]{1,0:T(8,128)(2,1)} fusion(bf16[2048,2816]{1,0:T(8,128)(2,1)} %bitcast.409, bf16[256,1408]{1,0:T(8,128)(2,1)} %copy-done.35, bf16[256,1408]{1,0:T(8,128)(2,1)} %copy-done.34), kind=kOutput, calls=%fused_computation.25 | convolution fusion | flops 2956197888 | bytes 14024704 | tf_op jit(solution)/shard_map/dot_general | solution.py:456
  432.8 4.8 all-to-all-start.9
  439.4 7.5 convolution_convert_fusion.1
  446.9 6.3 reshape.925
  453.2 5.7 convolution_convert_fusion.9
  458.8 5.4 convolution_convert_fusion.8
  468.7 29.8 %all_to_all.91 = bf16[4,64,2048]{2,1,0:T(8,128)(2,1)} all-to-all(bf16[4,64,2048]{2,1,0:T(8,128)(2,1)S(1)} %broadcast_in_dim.22), channel_id=1, replica_groups=mesh['seq'=4,'fsdp'=8] {'seq'}, dimensions={0} | all-to-all | bytes 2097152 | tf_op jit(solution)/shard_map/all_to_all | solution.py:468
  503.8 24.8 %all-to-all-done.14 = bf16[4,64,2048]{2,1,0:T(8,128)(2,1)} async-done(((bf16[4,64,2048]{2,1,0:T(8,128)(2,1)}), bf16[4,64,2048]{2,1,0:T(8,128)(2,1)}, u32[]{:S(2)}, u32[]{:S(2)}) %all-to-all-start.14) | async-done | bytes 1048608 | tf_op jit(solution)/shard_map/all_to_all | solution.py:468
  532.9 4.8 fusion.15.grad_ref
  541.8 4.8 fusion.12.grad_ref
  550.6 7.6 all-to-all-done.11
  564.0 11.2 %mixer_backward.2 = (bf16[4,1,64,2176]{3,2,1,0:T(8,128)(2,1)S(1)}, f32[4,2176]{1,0:T(4,128)S(1)}, f32[8,128]{1,0:T(8,128)S(1)}) custom-call(s32[2,4]{1,0:T(2,128)S(1)} %bitcast.313, f32[2,4]{1,0:T(2,128)S(1)} %pad_maximum_fusion.11.rate_ref, bf16[4,2,64,2176]{3,2,1,0:T(8,128)(2,1)S(1)} %bitcast.317, f32[4,2176]{1,0:T(4,128)S(1)} %maximum_convert_fusion.2.taps_ref, ...), custom_call_target="tpu_custom_call" | custom-call | flops 5368709120 | bytes 41943040 | tf_op jit(solution)/shard_map/mixer_backward/pallas_call | solution.py:395
  575.2 11.5 %mixer_backward.3 = (bf16[4,1,64,2176]{3,2,1,0:T(8,128)(2,1)S(1)}, f32[4,2176]{1,0:T(4,128)S(1)}, f32[8,128]{1,0:T(8,128)S(1)}) custom-call(s32[2,4]{1,0:T(2,128)S(1)} %bitcast.314, f32[2,4]{1,0:T(2,128)S(1)} %pad_maximum_fusion.11.rate_ref, bf16[4,2,64,2176]{3,2,1,0:T(8,128)(2,1)S(1)} %bitcast.318, f32[4,2176]{1,0:T(4,128)S(1)} %maximum_convert_fusion.2.taps_ref, ...), custom_call_target="tpu_custom_call" | custom-call | flops 5368709120 | bytes 41943040 | tf_op jit(solution)/shard_map/mixer_backward/pallas_call | solution.py:395
  591.3 4.3 fusion.22
  595.7 8.1 multiply_reduce_fusion
  603.7 12.2 %fusion.67 = bf16[2048,3200]{1,0:T(8,128)(2,1)} fusion(bf16[512,2048]{1,0:T(8,128)(2,1)S(1)} %get-tuple-element.89, bf16[512,3200]{1,0:T(8,128)(2,1)} %bitcast.334), kind=kOutput, calls=%fused_computation.182 | convolution fusion | flops 6710886400 | bytes 18481152 | tf_op jit(solution)/shard_map/dot_general | solution.py:452
  621.6 7.6 pad_maximum_fusion
  629.3 5.3 all-to-all-start.15
  641.2 24.7 %psum.7 = f32[1,104,128]{2,1,0:T(8,128)S(1)} all-reduce(f32[1,104,128]{2,1,0:T(8,128)S(1)} %fusion.49), channel_id=1, replica_groups=mesh['seq'=4,'fsdp'=8] {'fsdp'}, use_global_device_ids=true, to_apply=%region_19.20 | all-reduce | flops 13312 | bytes 106496 | tf_op jit(solution)/shard_map/psum | solution.py:724
  665.9 23.1 %all_gather.31 = f32[4,104,128]{2,1,0:T(8,128)S(1)} all-gather(f32[1,104,128]{2,1,0:T(8,128)S(1)} %psum.7), channel_id=1, replica_groups=mesh['seq'=4,'fsdp'=8] {'seq'}, dimensions={0}, use_global_device_ids=true | all-gather | bytes 266240 | tf_op jit(solution)/shard_map/all_gather | solution.py:725
  700.1 24.7 %all-to-all-done.16 = bf16[4,64,2816]{2,1,0:T(8,128)(2,1)S(1)} async-done(((bf16[4,64,2816]{2,1,0:T(8,128)(2,1)}), bf16[4,64,2816]{2,1,0:T(8,128)(2,1)S(1)}, u32[]{:S(2)}, u32[]{:S(2)}) %all-to-all-start.16) | async-done | bytes 1441824 | tf_op jit(solution)/shard_map/all_to_all | solution.py:468
  735.4 60.1 %reduce-scatter.8.cloned.1.call-done = bf16[1,300,2048]{2,1,0:T(8,128)(2,1)} async-done(((bf16[8,300,2048]{2,1,0:T(8,128)(2,1)}), bf16[1,300,2048]{2,1,0:T(8,128)(2,1)}) %reduce-scatter.8.cloned.1.call-update) | async-done | bytes 1228816 | tf_op jit(solution)/shard_map/reduce_scatter | solution.py:695
  (297 shorter events, 151.7 us)
Async XLA Ops:
  12.3 33.4 %all-to-all-start = ((bf16[4,64,2176]{2,1,0:T(8,128)(2,1)}), bf16[4,64,2176]{2,1,0:T(8,128)(2,1)S(1)}, u32[]{:S(2)}, u32[]{:S(2)}) async-start(bf16[4,64,2176]{2,1,0:T(8,128)(2,1)} %maximum_bitcast_fusion.2), calls=%async_computation | async-start | bytes 2228224 | tf_op jit(solution)/shard_map/all_to_all | solution.py:468
  18.6 98.2 %all-gather.8.cloned.1.call-start = ((), (), s32[]{:S(2)}) async-start(), calls=%async_computation.21 | async-start | bytes 10027008 | tf_op jit(solution)/shard_map/all_gather | solution.py:518
  24.1 22.7 %copy-start.11 = (bf16[2,1,64,2048]{3,2,1,0:T(8,128)(2,1)S(1)}, bf16[2,1,64,2048]{3,2,1,0:T(8,128)(2,1)}, u32[]{:S(2)}) copy-start(bf16[2,1,64,2048]{3,2,1,0:T(8,128)(2,1)} %param.13) | copy-start | bytes 1572868
  48.3 51.4 %all-to-all-start.1 = ((bf16[4,128,2048]{2,1,0:T(8,128)(2,1)}), bf16[4,128,2048]{2,1,0:T(8,128)(2,1)S(1)}, u32[]{:S(2)}, u32[]{:S(2)}) async-start(bf16[4,128,2048]{2,1,0:T(8,128)(2,1)} %broadcast_in_dim.17), calls=%async_computation.1 | async-start | bytes 4194304 | tf_op jit(solution)/shard_map/all_to_all | solution.py:468
  52.1 170.6 %all-gather.10.cloned.1.call-start = ((), (), s32[]{:S(2)}) async-start(), calls=%async_computation.22 | async-start | bytes 4718592 | tf_op jit(solution)/shard_map/all_gather | solution.py:518
  99.8 20.6 %copy-start.20 = (bf16[4,128,2048]{2,1,0:T(8,128)(2,1)}, bf16[4,128,2048]{2,1,0:T(8,128)(2,1)S(1)}, u32[]{:S(2)}) copy-start(bf16[4,128,2048]{2,1,0:T(8,128)(2,1)S(1)} %all-to-all-done.1) | copy-start | bytes 6291460
  116.9 116.1 %all-gather.12.cloned.1.call-start = ((), (), s32[]{:S(2)}) async-start(), calls=%async_computation.23 | async-start | bytes 4718592 | tf_op jit(solution)/shard_map/all_gather | solution.py:549
  117.6 188.4 %all-gather.16.cloned.1.call-start = ((), (), s32[]{:S(2)}) async-start(), calls=%async_computation.28 | async-start | bytes 6488064 | tf_op jit(solution)/shard_map/all_gather | solution.py:576
  120.9 10.0 %copy-start.41 = (bf16[4,128,2048]{2,1,0:T(8,128)(2,1)}, bf16[4,128,2048]{2,1,0:T(8,128)(2,1)S(1)}, u32[]{:S(2)}) copy-start(bf16[4,128,2048]{2,1,0:T(8,128)(2,1)S(1)} %multiply_convert_fusion.1) | copy-start | bytes 6291460
  120.9 10.1 %copy-start.28 = (bf16[2,1,64,2048]{3,2,1,0:T(8,128)(2,1)S(1)}, bf16[2,1,64,2048]{3,2,1,0:T(8,128)(2,1)}, u32[]{:S(2)}) copy-start(bf16[2,1,64,2048]{3,2,1,0:T(8,128)(2,1)} %param.25) | copy-start | bytes 1572868
  132.6 52.0 %all-to-all-start.3 = ((bf16[4,128,2048]{2,1,0:T(8,128)(2,1)}), bf16[4,128,2048]{2,1,0:T(8,128)(2,1)}, u32[]{:S(2)}, u32[]{:S(2)}) async-start(bf16[4,128,2048]{2,1,0:T(8,128)(2,1)} %broadcast_in_dim.19), calls=%async_computation.3 | async-start | bytes 4194304 | tf_op jit(solution)/shard_map/all_to_all | solution.py:468
  184.6 38.1 %all-to-all-start.4 = ((bf16[4,64,2816]{2,1,0:T(8,128)(2,1)}), bf16[4,64,2816]{2,1,0:T(8,128)(2,1)}, u32[]{:S(2)}, u32[]{:S(2)}) async-start(bf16[4,64,2816]{2,1,0:T(8,128)(2,1)} %fusion.10), calls=%async_computation.4 | async-start | bytes 2883584 | tf_op jit(solution)/shard_map/all_to_all | solution.py:468
  189.0 177.0 %all-gather.14.cloned.1.call-start = ((), (), s32[]{:S(2)}) async-start(), calls=%async_computation.24 | async-start | bytes 12976128 | tf_op jit(solution)/shard_map/all_gather | solution.py:518
  211.6 17.8 %copy-start.9 = (f32[4,2,128,128]{3,2,1,0:T(8,128)}, f32[4,2,128,128]{3,2,1,0:T(8,128)S(1)}, u32[]{:S(2)}) copy-start(f32[4,2,128,128]{3,2,1,0:T(8,128)S(1)} %get-tuple-element.84.inverse_ref) | copy-start | bytes 1572868
  237.6 29.5 %all-to-all-start.5 = ((bf16[4,64,2048]{2,1,0:T(8,128)(2,1)}), bf16[4,64,2048]{2,1,0:T(8,128)(2,1)}, u32[]{:S(2)}, u32[]{:S(2)}) async-start(bf16[4,64,2048]{2,1,0:T(8,128)(2,1)} %bitcast.360), calls=%async_computation.5 | async-start | bytes 2097152 | tf_op jit(solution)/shard_map/all_to_all | solution.py:468
  267.1 29.6 %all-to-all-start.7 = ((bf16[4,64,2048]{2,1,0:T(8,128)(2,1)}), bf16[4,64,2048]{2,1,0:T(8,128)(2,1)}, u32[]{:S(2)}, u32[]{:S(2)}) async-start(bf16[4,64,2048]{2,1,0:T(8,128)(2,1)} %bitcast.358), calls=%async_computation.7 | async-start | bytes 2097152 | tf_op jit(solution)/shard_map/all_to_all | solution.py:468
  271.4 26.9 %copy-start.12 = (bf16[2,1,64,2048]{3,2,1,0:T(8,128)(2,1)S(1)}, bf16[2,1,64,2048]{3,2,1,0:T(8,128)(2,1)}, u32[]{:S(2)}) copy-start(bf16[2,1,64,2048]{3,2,1,0:T(8,128)(2,1)} %param.13) | copy-start | bytes 1572868
  301.7 29.5 %all-to-all-start.6 = ((bf16[4,64,2048]{2,1,0:T(8,128)(2,1)}), bf16[4,64,2048]{2,1,0:T(8,128)(2,1)}, u32[]{:S(2)}, u32[]{:S(2)}) async-start(bf16[4,64,2048]{2,1,0:T(8,128)(2,1)} %broadcast_in_dim.20), calls=%async_computation.6 | async-start | bytes 2097152 | tf_op jit(solution)/shard_map/all_to_all | solution.py:468
  333.2 29.7 %all-to-all-start.8 = ((bf16[4,64,2048]{2,1,0:T(8,128)(2,1)}), bf16[4,64,2048]{2,1,0:T(8,128)(2,1)}, u32[]{:S(2)}, u32[]{:S(2)}) async-start(bf16[4,64,2048]{2,1,0:T(8,128)(2,1)} %broadcast_in_dim.21), calls=%async_computation.8 | async-start | bytes 2097152 | tf_op jit(solution)/shard_map/all_to_all | solution.py:468
  366.0 6.7 copy-start.27
  374.3 8.9 %copy-start.36 = (bf16[256,1408]{1,0:T(8,128)(2,1)}, bf16[256,1408]{1,0:T(8,128)(2,1)S(1)}, u32[]{:S(2)}) copy-start(bf16[256,1408]{1,0:T(8,128)(2,1)S(1)} %get-tuple-element.110) | copy-start | bytes 2162692
  374.3 8.9 %copy-start.38 = (bf16[256,1408]{1,0:T(8,128)(2,1)}, bf16[256,1408]{1,0:T(8,128)(2,1)S(1)}, u32[]{:S(2)}) copy-start(bf16[256,1408]{1,0:T(8,128)(2,1)S(1)} %get-tuple-element.111) | copy-start | bytes 2162692
  383.3 29.5 %all-to-all-start.13 = ((bf16[4,64,2048]{2,1,0:T(8,128)(2,1)}), bf16[4,64,2048]{2,1,0:T(8,128)(2,1)}, u32[]{:S(2)}, u32[]{:S(2)}) async-start(bf16[4,64,2048]{2,1,0:T(8,128)(2,1)} %bitcast.356), calls=%async_computation.13 | async-start | bytes 2097152 | tf_op jit(solution)/shard_map/all_to_all | solution.py:468
  387.5 175.2 %reduce-scatter.4.cloned.1.call-start = ((), (), s32[]{:S(2)}) async-start(), calls=%async_computation.25 | async-start | bytes 12976128 | tf_op jit(solution)/shard_map/reduce_scatter | solution.py:640
  387.8 6.7 copy-start.37
  387.8 6.7 copy-start.39
  432.8 31.4 %all-to-all-start.9 = ((bf16[4,64,2048]{2,1,0:T(8,128)(2,1)}), bf16[4,64,2048]{2,1,0:T(8,128)(2,1)}, u32[]{:S(2)}, u32[]{:S(2)}) async-start(bf16[4,64,2048]{2,1,0:T(8,128)(2,1)} %bitcast.357), calls=%async_computation.9 | async-start | bytes 2097152 | tf_op jit(solution)/shard_map/all_to_all | solution.py:468
  453.1 5.7 copy-start.33
  499.6 29.1 %all-to-all-start.14 = ((bf16[4,64,2048]{2,1,0:T(8,128)(2,1)}), bf16[4,64,2048]{2,1,0:T(8,128)(2,1)}, u32[]{:S(2)}, u32[]{:S(2)}) async-start(bf16[4,64,2048]{2,1,0:T(8,128)(2,1)} %broadcast_in_dim.23), calls=%async_computation.14 | async-start | bytes 2097152 | tf_op jit(solution)/shard_map/all_to_all | solution.py:468
  528.7 29.5 %all-to-all-start.11 = ((bf16[4,64,2048]{2,1,0:T(8,128)(2,1)}), bf16[4,64,2048]{2,1,0:T(8,128)(2,1)}, u32[]{:S(2)}, u32[]{:S(2)}) async-start(bf16[4,64,2048]{2,1,0:T(8,128)(2,1)} %bitcast.355), calls=%async_computation.11 | async-start | bytes 2097152 | tf_op jit(solution)/shard_map/all_to_all | solution.py:468
  550.6 12.1 %copy-start.3 = (bf16[4,1,64,1024]{3,2,1,0:T(8,128)(2,1)S(1)}, bf16[4,1,64,1024]{3,2,1,0:T(8,128)(2,1)}, u32[]{:S(2)}) copy-start(bf16[4,1,64,1024]{3,2,1,0:T(8,128)(2,1)} %get-tuple-element.80.grad_ref) | copy-start | bytes 1572868
  558.2 45.5 %all-to-all-start.12 = ((bf16[4,64,2048]{2,1,0:T(8,128)(2,1)}), bf16[4,64,2048]{2,1,0:T(8,128)(2,1)}, u32[]{:S(2)}, u32[]{:S(2)}) async-start(bf16[4,64,2048]{2,1,0:T(8,128)(2,1)} %bitcast.354), calls=%async_computation.12 | async-start | bytes 2097152 | tf_op jit(solution)/shard_map/all_to_all | solution.py:468
  562.5 162.3 %reduce-scatter.6.cloned.1.call-start = ((), (), s32[]{:S(2)}) async-start(), calls=%async_computation.26 | async-start | bytes 14745600 | tf_op jit(solution)/shard_map/reduce_scatter | solution.py:640
  564.0 11.3 %copy-start.2 = (bf16[4,1,64,1024]{3,2,1,0:T(8,128)(2,1)S(1)}, bf16[4,1,64,1024]{3,2,1,0:T(8,128)(2,1)}, u32[]{:S(2)}) copy-start(bf16[4,1,64,1024]{3,2,1,0:T(8,128)(2,1)} %get-tuple-element.86.grad_ref) | copy-start | bytes 1572868
  564.0 11.3 %copy-start.8 = (f32[4,256,256]{2,1,0:T(8,128)S(1)}, f32[4,256,256]{2,1,0:T(8,128)}, u32[]{:S(2)}) copy-start(f32[4,256,256]{2,1,0:T(8,128)} %copy-done.7) | copy-start | bytes 3145732
  564.0 11.3 %copy-start.10 = (f32[4,2,128,128]{3,2,1,0:T(8,128)S(1)}, f32[4,2,128,128]{3,2,1,0:T(8,128)}, u32[]{:S(2)}) copy-start(f32[4,2,128,128]{3,2,1,0:T(8,128)} %copy-done.9) | copy-start | bytes 1572868
  575.2 11.5 %copy-start.47 = (bf16[4,1,64,1024]{3,2,1,0:T(8,128)(2,1)S(1)}, bf16[4,1,64,1024]{3,2,1,0:T(8,128)(2,1)}, u32[]{:S(2)}) copy-start(bf16[4,1,64,1024]{3,2,1,0:T(8,128)(2,1)} %get-tuple-element.88) | copy-start | bytes 1572868
  587.9 7.7 slice-start.2
  588.3 7.3 slice-start.3
  588.6 7.1 copy-start.32
  616.0 179.5 %reduce-scatter.8.cloned.1.call-start = ((), (), s32[]{:S(2)}) async-start(), calls=%async_computation.27 | async-start | bytes 11206656 | tf_op jit(solution)/shard_map/reduce_scatter | solution.py:695
  629.3 5.3 copy-start.13
  629.3 5.3 copy-start.16
  629.3 5.3 copy-start.19
  629.3 5.3 copy-start.23
  629.3 59.8 %all-to-all-start.15 = ((bf16[4,128,2048]{2,1,0:T(8,128)(2,1)}), bf16[4,128,2048]{2,1,0:T(8,128)(2,1)}, u32[]{:S(2)}, u32[]{:S(2)}) async-start(bf16[4,128,2048]{2,1,0:T(8,128)(2,1)} %bitcast.341), calls=%async_computation.16 | async-start | bytes 4194304 | tf_op jit(solution)/shard_map/all_to_all | solution.py:468
  689.1 35.6 %all-to-all-start.16 = ((bf16[4,64,2816]{2,1,0:T(8,128)(2,1)}), bf16[4,64,2816]{2,1,0:T(8,128)(2,1)S(1)}, u32[]{:S(2)}, u32[]{:S(2)}) async-start(bf16[4,64,2816]{2,1,0:T(8,128)(2,1)} %reduce-scatter.4.cloned.1.call-done), calls=%async_computation.18 | async-start | bytes 2883584 | tf_op jit(solution)/shard_map/all_to_all | solution.py:468
  724.8 74.7 %all-to-all-start.17 = ((bf16[4,64,3200]{2,1,0:T(8,128)(2,1)}), bf16[4,64,3200]{2,1,0:T(8,128)(2,1)S(1)}, u32[]{:S(2)}, u32[]{:S(2)}) async-start(bf16[4,64,3200]{2,1,0:T(8,128)(2,1)} %reduce-scatter.6.cloned.1.call-done), calls=%async_computation.19 | async-start | bytes 3276800 | tf_op jit(solution)/shard_map/all_to_all | solution.py:468
  (41 other events, 101.7 us)
Sparse Core Ops, SparseCore 0:
  46.9 55.7 all-gather.7
  117.0 35.9 all-gather.9
  154.9 36.6 all-gather.11
  193.4 43.3 all-gather.15
  238.6 67.6 all-gather.13
  424.0 85.9 reduce-scatter.3
  616.1 96.9 reduce-scatter.5
  716.6 78.8 reduce-scatter.7

commit v2 on v1

--- a/solution.py
+++ b/solution.py
@@ -408,7 +408,7 @@
             jax.ShapeDtypeStruct((8, LANES), F32),
         ],
         compiler_params=pltpu.CompilerParams(vmem_limit_bytes=40 * 1024 * 1024),
-        cost_estimate=mixer_cost(sent, heads, 40),
+        cost_estimate=mixer_cost(sent, heads, 1),
         name="mixer_backward",
     )(lengths, rates, sent, taps, update, inverse, grad)
 
@@ -444,6 +444,64 @@
     )(mixed, gate, gain, grad)
 
 
+def norm_forward_kernel(base_ref, terms_ref, gain_ref, middle_ref, rows_ref):
+    middle = base_ref[...].astype(F32)
+    for span in range(terms_ref.shape[0]):
+        middle = middle + terms_ref[span].astype(F32)
+    scale = lax.rsqrt(jnp.mean(middle * middle, axis=1, keepdims=True) + EPS)
+    rows = (middle * scale * gain_ref[...]).astype(BF16)
+    middle_ref[...] = middle
+    for span in range(rows_ref.shape[0]):
+        rows_ref[span] = rows
+
+
+def norm_backward_kernel(
+    base_ref, middle_ref, terms_ref, gain_ref, grad_ref, rows_ref, grad_gain_ref
+):
+    middle = middle_ref[...]
+    grad = terms_ref[0].astype(F32)
+    for span in range(1, terms_ref.shape[0]):
+        grad = grad + terms_ref[span].astype(F32)
+    scale = lax.rsqrt(jnp.mean(middle * middle, axis=1, keepdims=True) + EPS)
+    grad_gain_ref[...] = jnp.sum(middle * scale * grad, axis=0, keepdims=True)
+    inner = grad * gain_ref[...]
+    weight = scale * scale * scale * jnp.mean(middle * inner, axis=1, keepdims=True)
+    total = base_ref[...].astype(F32) + scale * inner - middle * weight
+    grad_ref[...] = total
+    rows = total.astype(BF16)
+    for span in range(rows_ref.shape[0]):
+        rows_ref[span] = rows
+
+
+def norm_forward(base, terms, gain):
+    return pl.pallas_call(
+        norm_forward_kernel,
+        out_shape=[
+            jax.ShapeDtypeStruct(base.shape, F32),
+            jax.ShapeDtypeStruct(terms.shape, BF16),
+        ],
+        cost_estimate=pl.CostEstimate(
+            flops=20 * base.size, bytes_accessed=40 * base.size, transcendentals=0
+        ),
+        name="norm_forward",
+    )(base, terms, gain)
+
+
+def norm_backward(base, middle, terms, gain):
+    return pl.pallas_call(
+        norm_backward_kernel,
+        out_shape=[
+            jax.ShapeDtypeStruct(base.shape, F32),
+            jax.ShapeDtypeStruct(terms.shape, BF16),
+            jax.ShapeDtypeStruct(gain.shape, F32),
+        ],
+        cost_estimate=pl.CostEstimate(
+            flops=30 * base.size, bytes_accessed=40 * base.size, transcendentals=0
+        ),
+        name="norm_backward",
+    )(base, middle, terms, gain)
+
+
 def dot(left, right):
     return jnp.dot(left, right, preferred_element_type=F32)
 
@@ -477,6 +535,10 @@
     return exchange(
         partial_rows.astype(BF16).reshape((spans, -1) + partial_rows.shape[1:])
     )
+
+
+def cut(array, start, size, axis=0):
+    return lax.dynamic_slice_in_dim(array, start, size, axis, allow_negative_indices=False)
 
 
 def norm_scale(values):
@@ -525,13 +587,13 @@
     pairs = jnp.concatenate([decay_weight.reshape(share, spans, 2 * heads), small], axis=2)
     pair_at = 2 * qw + vw
     mix_width = pair_at + LANES
-    mix_blocks = by_span([
+    in_blocks = by_span([
         columns(in_weight, 0, qw),
         columns(in_weight, H * DK, qw),
         columns(in_weight, 2 * H * DK, vw),
         widen(pairs, LANES),
+        columns(in_weight, 2 * H * DK + H * DV, vw),
     ])
-    gate_blocks = by_span([columns(in_weight, 2 * H * DK + H * DV, vw)])
     up_blocks = by_span([
         widen(columns(up_weight, 0, fw), fp),
         widen(columns(up_weight, FF, fw), fp),
@@ -541,21 +603,18 @@
     grouped = (spans, micros, length)
     all_rows = spans * local_rows
 
-    mix_blocks, up_blocks = lax.optimization_barrier((exchange(mix_blocks), up_blocks))
-    w_mix = gather_weight(mix_blocks)
-    all_tokens = gather_rows(after(local_tokens, mix_blocks))
-    gate_blocks = exchange(after(gate_blocks, all_tokens))
-    w_gate = gather_weight(after(gate_blocks, w_mix))
-    w_out = lax.all_gather(after(out_weight, w_mix), "fsdp", axis=0, tiled=True)
-
-    small = w_mix[:, pair_at + 2 * heads : pair_at + 2 * heads + conv_cols + 2]
+    in_blocks, up_blocks = lax.optimization_barrier((exchange(in_blocks), up_blocks))
+    w_mix = gather_weight(in_blocks[:, :, :mix_width])
+    all_tokens = gather_rows(after(local_tokens, in_blocks))
+
+    cot = gather_rows(after(local_cot, all_tokens)).reshape(all_rows, D)
+    small_at = pair_at + 2 * heads
+    small = plain(w_mix[:, small_at : small_at + conv_cols + 2])
     gains = small[:, conv_cols:].T.astype(F32)
 
     def own(base, width):
         step = conv_share // share
-        rows = lax.dynamic_slice_in_dim(
-            small[:, :conv_cols], (base + place * width) // step, width // step, axis=0
-        )
+        rows = cut(small[:, :conv_cols], base // step + place * (width // step), width // step)
         return rows.reshape(width, CONV).T
 
     taps = jnp.concatenate(
@@ -563,8 +622,8 @@
         axis=1,
     ).astype(F32)
     rates = jnp.stack([
-        -jnp.exp(lax.dynamic_slice_in_dim(a_log, place * heads, heads)),
-        lax.dynamic_slice_in_dim(dt_bias, place * heads, heads),
+        -jnp.exp(cut(a_log, place * heads, heads)),
+        cut(dt_bias, place * heads, heads),
     ])
     gain_row = out_gain.reshape(1, DV)
     pack_lengths = lengths[:, 0]
@@ -572,40 +631,41 @@
     inputs = all_tokens.reshape(all_rows, D).astype(F32)
     input_scale = norm_scale(inputs)
     first = (inputs * input_scale * gains[0]).astype(BF16)
-    sent = dot(first, w_mix).astype(BF16).reshape(grouped + (mix_width,))
-    w_down = lax.all_gather(after(down_weight, sent), "fsdp", axis=0)
-    cot = gather_rows(after(local_cot, sent)).reshape(all_rows, D)
+    sent = dot(first, w_mix).astype(BF16)
+    w_gate = gather_weight(after(in_blocks, all_tokens)[:, :, mix_width:])
+    w_down = lax.all_gather(after(down_weight, w_mix), "fsdp", axis=0)
+    w_out = lax.all_gather(after(out_weight, w_mix), "fsdp", axis=0, tiled=True)
+    sent = sent.reshape(grouped + (mix_width,))
     mixers = []
     for micro in range(micros):
         mixers.append(
             mixer_forward(micro, pack_lengths, rates, sent, taps, heads)
         )
-        if micro == 0:
-            up_blocks = exchange(after(up_blocks, cot, mixers[0][0]))
         sent = after(sent, mixers[-1][0])
+    up_blocks = exchange(after(up_blocks, cot, mixers[0][0]))
     w_down = lax.optimization_barrier(w_down.reshape(fw, D))
-    w_up = gather_weight(after(up_blocks, mixers[-1][0]))
     gate = dot(first, w_gate).reshape(grouped + (vw,))
     grad_act = dot_back(cot, w_down).reshape(grouped + (fw,))
 
     def part(array, micro):
         return array.reshape((micros, length) + array.shape[1:])[micro]
 
-    normeds, branches = [], []
+    normeds, branches, branch_rows = [], [], []
     for micro in range(micros):
         normeds.append(gate_forward(micro, mixers[micro][0], gate, gain_row, heads))
         rows = dot(normeds[-1].reshape(-1, vw), w_out).astype(BF16)
         branches.append(scatter_rows(after(rows, up_blocks), spans))
+        branch_rows.append(rows)
+    w_up = gather_weight(after(up_blocks, branch_rows[0]))
     middles, seconds = [], []
     for micro in range(micros):
-        middle = part(local_tokens, micro).astype(F32) + jnp.sum(
-            branches[micro].astype(F32), axis=0
-        )
+        middle, rows = norm_forward(part(local_tokens, micro), branches[micro], gains[1:])
         middles.append(middle)
-        seconds.append(gather_rows((middle * norm_scale(middle) * gains[1]).astype(BF16)))
-
-    acts, grad_boths, grad_seconds, sums = [], [], [], [None] * micros
+        seconds.append(exchange(rows))
+
+    acts, grad_boths, grad_seconds, sums = [], [], [], []
     for micro in range(micros):
+        seconds[micro] = after(seconds[micro], *sums)
         both = dot(seconds[micro].reshape(-1, D), w_up)
         gated, upper = both[:, :fp], both[:, fp:]
         soft = jax.nn.sigmoid(gated)
@@ -621,19 +681,20 @@
         grad_boths.append(grad_both.reshape(spans, length, 2 * fp))
         rows = dot_back(grad_both, w_up).astype(BF16)
         grad_seconds.append(scatter_rows(rows, spans))
+        sums.append(rows)
     act = jnp.stack(acts, axis=1).reshape(all_rows, fp)[:, :fw]
     final_rows = [dot(a.reshape(-1, fp)[:, :fw], w_down).astype(BF16) for a in acts]
     down_grads = outer(act, cot).astype(BF16).reshape(packs, -1, D)
     spare = [final_rows[:1], final_rows[1:] + [down_grads]]
     grad_middles, grad_branches, grad_gain2 = [], [], 0.0
     for micro in range(micros):
-        grad_second = jnp.sum(
-            after(grad_seconds[micro], *spare[min(micro, 1)]).astype(F32), axis=0
+        terms = after(grad_seconds[micro], *spare[min(micro, 1)])
+        grad_middle, rows, grad_gain = norm_backward(
+            part(local_cot, micro), middles[micro], terms, gains[1:]
         )
-        grad_norm, grad_gain = norm_back(middles[micro], gains[1], grad_second)
         grad_gain2 = grad_gain2 + grad_gain
-        grad_middles.append(part(local_cot, micro).astype(F32) + grad_norm)
-        grad_branches.append(gather_rows(grad_middles[-1].astype(BF16)))
+        grad_middles.append(grad_middle)
+        grad_branches.append(exchange(rows))
 
     def reduce_rows(grad, blocks):
         blocks = plain(grad.astype(BF16).reshape(blocks, -1, grad.shape[1]))
@@ -645,58 +706,55 @@
     def all_micros(parts):
         return jnp.stack(parts, axis=1).reshape(all_rows, parts[0].shape[-1])
 
-    up_grads = reduce_rows(
-        outer(after(all_micros(seconds), grad_seconds[0]), all_micros(grad_boths)), spans
-    )
-    finals, waits = [], grad_branches[-1]
+    up_product = outer(
+        after(all_micros(seconds), grad_seconds[0], *sums), all_micros(grad_boths)
+    ).astype(BF16)
+    up_grads = reduce_rows(up_product, spans)
+    grad_gates, grad_sents, grad_gain, grad_taps, grad_small = [], [], 0.0, 0.0, 0.0
     for micro in range(micros):
-        waits = scatter_rows(after(final_rows[micro], waits), spans)
-        finals.append(middles[micro] + jnp.sum(waits.astype(F32), axis=0))
-        sums[micro] = waits
-    block_out = jnp.stack(finals).reshape(local_rows, D)
-
-    grad_mixeds, grad_gates, grad_gain = [], [], 0.0
+        mixed, update, inverse = mixers[micro]
+        grad = after(grad_branches[micro], *grad_sents)
+        grad = dot_back(grad.reshape(-1, D), w_out).reshape(spans, 1, length, vw)
+        grad_mixed, grad_gate, term = gate_backward(micro, mixed, gate, gain_row, grad, heads)
+        if micro + 1 == micros:
+            grad_mixed = after(grad_mixed, up_grads)
+        grad_sent, term_taps, term_small = mixer_backward(
+            micro, pack_lengths, rates, sent, taps, update, inverse, grad_mixed, heads
+        )
+        grad_gates.append(grad_gate.reshape(spans, length, vw))
+        grad_sents.append(grad_sent.reshape(spans, length, mix_width))
+        grad_gain, grad_taps = grad_gain + term, grad_taps + term_taps
+        grad_small = grad_small + term_small
+    finals, wait = [], grad_sents[0]
     for micro in range(micros):
-        grad = dot_back(grad_branches[micro].reshape(-1, D), w_out)
-        grad_mixed, grad_gate, term = gate_backward(
-            micro, mixers[micro][0], gate, gain_row,
-            grad.reshape(spans, 1, length, vw), heads,
-        )
-        grad_mixeds.append(grad_mixed)
-        grad_gates.append(grad_gate.reshape(spans, length, vw))
-        grad_gain = grad_gain + term
-    grad_mixeds[0] = after(grad_mixeds[0], up_grads)
-    grad_sents, grad_taps, grad_small = [], 0.0, 0.0
-    for micro in range(micros):
-        _, update, inverse = mixers[micro]
-        grad_sent, term_taps, term_small = mixer_backward(
-            micro, pack_lengths, rates, sent, taps, update, inverse, grad_mixeds[micro], heads
-        )
-        if micro + 1 < micros:
-            grad_mixeds[micro + 1] = after(grad_mixeds[micro + 1], grad_sent)
-        grad_sents.append(grad_sent.reshape(spans, length, mix_width))
-        grad_taps, grad_small = grad_taps + term_taps, grad_small + term_small
+        wait = scatter_rows(after(final_rows[micro], wait), spans)
+        finals.append(wait)
+    block_out = jnp.stack([
+        middle + jnp.sum(terms.astype(F32), axis=0) for middle, terms in zip(middles, finals)
+    ]).reshape(local_rows, D)
+
     grad_proj = all_micros([
         jnp.concatenate(pair, axis=-1) for pair in zip(grad_sents, grad_gates)
     ])
-    in_product = outer(after(first, sums[-1]), grad_proj)
+    grad_down = lax.psum_scatter(
+        after(down_grads, grad_middles[0]), "fsdp", scatter_dimension=0
+    )
+    in_product = outer(after(first, finals[0]), grad_proj)
     in_grads = reduce_rows(in_product, spans)
+    grad_proj = after(grad_proj, in_product, finals[-1])
     grad_first = dot_back(grad_proj[:, :mix_width], w_mix) + dot_back(
         grad_proj[:, mix_width:], w_gate
     )
     grad_gain1 = jnp.sum(inputs * input_scale * grad_first, axis=0)
     first_rows = grad_first.astype(BF16)
+    first_rows, grad_down, up_grads = lax.optimization_barrier((first_rows, grad_down, up_grads))
     grad_first = scatter_rows(first_rows, spans)
     out_grads = outer(
-        after(all_micros([n[:, 0] for n in normeds]), first_rows), all_micros(grad_branches)
-    )
-    out_grads = out_grads.astype(BF16).reshape(packs, -1, D)
-    down_rows = down_grads.shape[1]
-    row_grads = lax.psum_scatter(
-        after(jnp.concatenate([out_grads, down_grads], axis=1), in_product),
-        "fsdp", scatter_dimension=0,
+        all_micros([n[:, 0] for n in normeds]), after(all_micros(grad_branches), first_rows)
+    )
+    grad_out = lax.psum_scatter(
+        out_grads.astype(BF16), "fsdp", scatter_dimension=0, tiled=True
     ).astype(F32)
-    grad_out, grad_down = row_grads[:-down_rows], row_grads[-down_rows:]
     grad_norm1, _ = norm_back(
         local_tokens.astype(F32), gains[0], jnp.sum(grad_first.astype(F32), axis=0)
     )
@@ -715,7 +773,7 @@
     )
     grad_decay = joined(in_grads, pair_at, 2 * heads)
 
-    gain_rows = jnp.stack([grad_gain1, grad_gain2])
+    gain_rows = jnp.stack([grad_gain1, grad_gain2[0]])
     flat = jnp.concatenate([
         grad_taps[:, :pair_at].reshape(-1), gain_rows.reshape(-1), grad_gain.reshape(-1),
         grad_small[:2].reshape(-1),
@@ -732,11 +790,11 @@
         [all_taps(0, qw), all_taps(qw, qw), all_taps(2 * qw, vw)], axis=1
     )
     index = place * packs + lax.axis_index("fsdp")
-    grad_conv = lax.dynamic_slice_in_dim(grad_conv, index * conv_share, conv_share, axis=1).T
+    grad_conv = cut(grad_conv, index * conv_share, conv_share, 1).T
     at = CONV * pair_at
     gains_flat = jnp.sum(flat[:, at : at + 2 * D], axis=0).reshape(2, D)
     gain_share = norm_gains.shape[1]
-    grad_gains = lax.dynamic_slice_in_dim(gains_flat, index * gain_share, gain_share, axis=1)
+    grad_gains = cut(gains_flat, index * gain_share, gain_share, 1)
     at = at + 2 * D
     grad_gain = jnp.sum(flat[:, at : at + DV], axis=0)
     at = at + DV
@@ -752,7 +810,7 @@
         grad_gain,
         grad_out,
         grad_up,
-        grad_down,
+        grad_down.astype(F32),
     )
 
 

time: 818 us -> 735 us (0.90)
  waiting for transfers between devices: 308 us -> 195 us
  blocking collectives: 94.6 us -> 119 us
  Pallas kernels: 78.6 us -> 90.6 us
  other arithmetic: 54.1 us -> 43.1 us
  local copies, waits for them, and re-layouts: 56.2 us -> 66.7 us
    all_to_all x16 -> x15, waiting for transfers between devices: 247 us -> 184 us  [exchange(): lax.all_to_all(blocks, 'seq', split_axis=0, concat_axis=0, tiled=True)]
    reduce_scatter x1 -> x2, waiting for transfers between devices: 60.1 us -> 0.01 us  [the longest x1 0.01 us: shards(): lax.psum_scatter(after(down_grads, grad_middles[0]), 'fsdp', scatter_dime...]
    all_to_all x2, blocking collectives: 46.9 us -> 77.8 us  [exchange(): lax.all_to_all(blocks, 'seq', split_axis=0, concat_axis=0, tiled=True)]
    pallas_call x0 -> x4, Pallas kernels: none -> 12.2 us  [the longest x2 6.97 us: norm_backward(): pl.pallas_call(norm_backward_kernel, out_shape=[jax.ShapeDtypeStruct(base...]
    unnamed x144 -> x117, local copies, waits for them, and re-layouts: 20.2 us -> 31.4 us
    reduce_sum x7 -> x2, other arithmetic: 10.9 us -> 1.65 us  [shards(): jnp.sum(terms.astype(F32), axis=0)]
    all_to_all x16 -> x15, starting transfers between devices: 71.3 us -> 64.8 us  [exchange(): lax.all_to_all(blocks, 'seq', split_axis=0, concat_axis=0, tiled=True)]
  transfers between devices with their start and end apart: 24 -> 24, of which waited for: 13 -> 15; matrix products, arithmetic and copies ran while one was open for 22% -> 26% of each run, Pallas kernels for 10% -> 12%
where the time goes in v2:
time: 735 us; the launch traced here: 727 us
  waiting for transfers between devices  195 us (27%)
  matrix products  132 us (18%)
  blocking collectives  119 us (16%)
  Pallas kernels  90.6 us (12%)
  local copies, waits for them, and re-layouts  66.7 us (9%)
  starting transfers between devices  66 us (9%)
  other arithmetic  43.1 us (6%)
  between operations  15 us (2%)
    all_to_all x15, waiting for transfers between devices, exchange(): lax.all_to_all(blocks, 'seq', split_axis=0, concat_axis=0, tiled=True)  184 us
    all_to_all x2, blocking collectives, exchange(): lax.all_to_all(blocks, 'seq', split_axis=0, concat_axis=0, tiled=True)  77.8 us
    all_to_all x15, starting transfers between devices, exchange(): lax.all_to_all(blocks, 'seq', split_axis=0, concat_axis=0, tiled=True)  64.8 us
    dot_general x8, matrix products, dot(): return jnp.dot(left, right, preferred_element_type=F32)  48.9 us
    dot_general x7, matrix products, dot_back(): return lax.dot_general(left, right, NT, preferred_element_type=F32)  47.7 us
    pallas_call x2, Pallas kernels, mixer_forward(): pl.pallas_call(partial(mixer_forward_kernel, micro, per_step, heads, leng...  40.4 us
    dot_general x4, matrix products, outer(): return lax.dot_general(left, right, TN, preferred_element_type=F32)  35.1 us
    unnamed x117, local copies, waits for them, and re-layouts  31.4 us
  transfers between devices with their start and end apart: 24, of which 15 were waited for; matrix products, arithmetic and copies ran while one was open for 26% of the time, Pallas kernels for 12%

profile of v2, /device:TPU:0, one launch (start us, length us, event | category | flops | bytes accessed | tf_op | source)
XLA Modules:
  0.0 727.2 jit_solution(16331614415564364806)
XLA Ops:
  14.0 6.3 all-to-all-start
  27.0 31.7 %all-to-all-done = bf16[4,64,3200]{2,1,0:T(8,128)(2,1)S(1)} async-done(((bf16[4,64,3200]{2,1,0:T(8,128)(2,1)}), bf16[4,64,3200]{2,1,0:T(8,128)(2,1)S(1)}, u32[]{:S(2)}, u32[]{:S(2)}) %all-to-all-start) | async-done | bytes 1638432 | tf_op jit(solution)/shard_map/all_to_all | solution.py:526
  60.5 50.2 %all_to_all.85 = bf16[4,128,2048]{2,1,0:T(8,128)(2,1)S(1)} all-to-all(bf16[4,128,2048]{2,1,0:T(8,128)(2,1)S(1)} %broadcast_in_dim.9), channel_id=1, replica_groups=mesh['seq'=4,'fsdp'=8] {'seq'}, dimensions={0} | all-to-all | bytes 4194304 | tf_op jit(solution)/shard_map/all_to_all | solution.py:526
  118.1 4.8 all-to-all-start.2
  131.7 9.1 %convolution_convert_fusion.2 = bf16[512,2176]{1,0:T(8,128)(2,1)S(1)} fusion(bf16[512,2048]{1,0:T(8,128)(2,1)} %bitcast.259, bf16[2048,2176]{1,0:T(8,128)(2,1)} %bitcast.300), kind=kOutput, calls=%fused_computation.4 | convolution fusion | flops 4564516864 | bytes 13238272 | tf_op jit(solution)/shard_map/dot_general | solution.py:506
  140.9 20.2 %mixer_forward.2 = (bf16[4,1,64,1024]{3,2,1,0:T(8,128)(2,1)S(1)}, f32[4,256,256]{2,1,0:T(8,128)S(1)}, f32[4,2,128,128]{3,2,1,0:T(8,128)S(1)}) custom-call(s32[2,4]{1,0:T(2,128)S(1)} %bitcast.231, f32[2,4]{1,0:T(2,128)S(1)} %pad_maximum_fusion.10.rate_ref, bf16[4,2,64,2176]{3,2,1,0:T(8,128)(2,1)S(1)} %bitcast.225, f32[4,2176]{1,0:T(4,128)S(1)} %maximum_convert_fusion.2.taps_ref), custom_call_target="tpu_custom_call" | custom-call | flops 8053063680 | bytes 62914560 | tf_op jit(solution)/shard_map/mixer_forward/pallas_call | solution.py:369
  163.7 8.0 %all-to-all-done.2 = bf16[4,128,2048]{2,1,0:T(8,128)(2,1)} async-done(((bf16[4,128,2048]{2,1,0:T(8,128)(2,1)}), bf16[4,128,2048]{2,1,0:T(8,128)(2,1)}, u32[]{:S(2)}, u32[]{:S(2)}) %all-to-all-start.2) | async-done | bytes 2097184 | tf_op jit(solution)/shard_map/all_to_all | solution.py:526
  171.7 4.4 all-to-all-start.3
  176.1 6.5 fusion.46.gate_ref
  186.3 7.6 %all-gather.12.cloned.1.call-done = bf16[1024,2048]{1,0:T(8,128)(2,1)} async-done(((bf16[128,2048]{1,0:T(8,128)(2,1)}), bf16[1024,2048]{1,0:T(8,128)(2,1)}) %all-gather.12.cloned.1.call-update) | async-done | bytes 4194320 | tf_op jit(solution)/shard_map/all_gather | solution.py:637
  193.8 4.6 convolution_convert_fusion.7
  198.4 11.5 %all-to-all-done.3 = bf16[4,64,2816]{2,1,0:T(8,128)(2,1)} async-done(((bf16[4,64,2816]{2,1,0:T(8,128)(2,1)}), bf16[4,64,2816]{2,1,0:T(8,128)(2,1)}, u32[]{:S(2)}, u32[]{:S(2)}) %all-to-all-start.3) | async-done | bytes 1441824 | tf_op jit(solution)/shard_map/all_to_all | solution.py:526
  210.0 4.5 all-to-all-start.4
  214.5 20.2 %mixer_forward.3 = (bf16[4,1,64,1024]{3,2,1,0:T(8,128)(2,1)S(1)}, f32[4,256,256]{2,1,0:T(8,128)S(1)}, f32[4,2,128,128]{3,2,1,0:T(8,128)S(1)}) custom-call(s32[2,4]{1,0:T(2,128)S(1)} %bitcast.232, f32[2,4]{1,0:T(2,128)S(1)} %pad_maximum_fusion.10.rate_ref, bf16[4,2,64,2176]{3,2,1,0:T(8,128)(2,1)S(1)} %bitcast.226, f32[4,2176]{1,0:T(4,128)S(1)} %maximum_convert_fusion.2.taps_ref), custom_call_target="tpu_custom_call" | custom-call | flops 8053063680 | bytes 62914560 | tf_op jit(solution)/shard_map/mixer_forward/pallas_call | solution.py:369
  240.9 4.6 convolution_convert_fusion.6
  245.5 5.1 all-to-all-start.9
  254.0 21.3 %all-to-all-done.9.terms_ref = bf16[4,64,2048]{2,1,0:T(8,128)(2,1)} async-done(((bf16[4,64,2048]{2,1,0:T(8,128)(2,1)}), bf16[4,64,2048]{2,1,0:T(8,128)(2,1)}, u32[]{:S(2)}, u32[]{:S(2)}) %all-to-all-start.9) | async-done | bytes 1048608 | tf_op jit(solution)/shard_map/all_to_all | solution.py:526
  281.5 5.9 reshape.489
  287.4 6.5 fusion
  295.7 8.4 %all-to-all-done.5 = bf16[4,64,2048]{2,1,0:T(8,128)(2,1)S(1)} async-done(((bf16[4,64,2048]{2,1,0:T(8,128)(2,1)}), bf16[4,64,2048]{2,1,0:T(8,128)(2,1)S(1)}, u32[]{:S(2)}, u32[]{:S(2)}) %all-to-all-start.5) | async-done | bytes 1048608 | tf_op jit(solution)/shard_map/all_to_all | solution.py:526
  304.1 4.5 all-to-all-start.10
  308.6 6.4 fusion.47
  318.0 8.4 %convolution_convert_fusion.5 = bf16[256,2048]{1,0:T(8,128)(2,1)} fusion(bf16[2048,2816]{1,0:T(8,128)(2,1)} %bitcast.317, bf16[256,1408]{1,0:T(8,128)(2,1)S(1)} %get-tuple-element.193, bf16[256,1408]{1,0:T(8,128)(2,1)S(1)} %get-tuple-element.192), kind=kOutput, calls=%fused_computation.24 | convolution fusion | flops 2956197888 | bytes 14024704 | tf_op jit(solution)/shard_map/dot_general | solution.py:514
  326.4 7.5 %all-to-all-done.10 = bf16[4,64,2048]{2,1,0:T(8,128)(2,1)} async-done(((bf16[4,64,2048]{2,1,0:T(8,128)(2,1)}), bf16[4,64,2048]{2,1,0:T(8,128)(2,1)}, u32[]{:S(2)}, u32[]{:S(2)}) %all-to-all-start.10) | async-done | bytes 1048608 | tf_op jit(solution)/shard_map/all_to_all | solution.py:526
  333.9 9.3 %fusion.48 = f32[256,2816]{1,0:T(8,128)} fusion(bf16[256,2048]{1,0:T(8,128)(2,1)} %bitcast.43, bf16[2048,2816]{1,0:T(8,128)(2,1)} %bitcast.318), kind=kOutput, calls=%fused_computation.137 | convolution fusion | flops 2952790016 | bytes 15466496 | tf_op jit(solution)/shard_map/dot_general | solution.py:506
  356.2 8.4 %convolution_convert_fusion.4 = bf16[256,2048]{1,0:T(8,128)(2,1)} fusion(bf16[2048,2816]{1,0:T(8,128)(2,1)} %bitcast.319, bf16[256,1408]{1,0:T(8,128)(2,1)S(1)} %get-tuple-element.191, bf16[256,1408]{1,0:T(8,128)(2,1)S(1)} %get-tuple-element.190), kind=kOutput, calls=%fused_computation.23 | convolution fusion | flops 2956197888 | bytes 14024704 | tf_op jit(solution)/shard_map/dot_general | solution.py:514
  364.7 7.2 all-to-all-done.6.terms_ref
  371.9 11.4 %convolution_convert_fusion = bf16[2048,2816]{1,0:T(8,128)(2,1)} fusion(bf16[512,2048]{1,0:T(8,128)(2,1)} %bitcast.257, bf16[512,2816]{1,0:T(8,128)(2,1)} %bitcast.252), kind=kOutput, calls=%fused_computation | convolution fusion | flops 5911347200 | bytes 16515072 | tf_op jit(solution)/shard_map/dot_general | solution.py:510
  391.1 9.0 %convolution_convert_fusion.1 = bf16[1376,2048]{1,0:T(8,128)(2,1)} fusion(bf16[512,2048]{1,0:T(8,128)(2,1)} %bitcast.24, bf16[512,1408]{1,0:T(8,128)(2,1)S(1)} %bitcast.265), kind=kOutput, calls=%fused_computation.1 | convolution fusion | flops 2888499200 | bytes 9175040 | tf_op jit(solution)/shard_map/dot_general | solution.py:510
  402.8 5.9 reshape.447
  418.2 5.6 convolution_convert_fusion.8
  427.2 16.3 %all-to-all-done.7 = bf16[4,64,2048]{2,1,0:T(8,128)(2,1)} async-done(((bf16[4,64,2048]{2,1,0:T(8,128)(2,1)}), bf16[4,64,2048]{2,1,0:T(8,128)(2,1)}, u32[]{:S(2)}, u32[]{:S(2)}) %all-to-all-start.7) | async-done | bytes 1048608 | tf_op jit(solution)/shard_map/all_to_all | solution.py:526
  443.4 4.4 all-to-all-start.13
  447.9 5.7 fusion.12.grad_ref
  461.0 11.3 %mixer_backward.2 = (bf16[4,1,64,2176]{3,2,1,0:T(8,128)(2,1)S(1)}, f32[4,2176]{1,0:T(4,128)S(1)}, f32[8,128]{1,0:T(8,128)S(1)}) custom-call(s32[2,4]{1,0:T(2,128)S(1)} %bitcast.233, f32[2,4]{1,0:T(2,128)S(1)} %pad_maximum_fusion.10.rate_ref, bf16[4,2,64,2176]{3,2,1,0:T(8,128)(2,1)S(1)} %bitcast.227, f32[4,2176]{1,0:T(4,128)S(1)} %maximum_convert_fusion.2.taps_ref, ...), custom_call_target="tpu_custom_call" | custom-call | flops 134217728 | bytes 1048576 | tf_op jit(solution)/shard_map/mixer_backward/pallas_call | solution.py:395
  473.2 4.2 all-to-all-start.8
  491.6 11.1 %all-to-all-done.8 = bf16[4,64,2048]{2,1,0:T(8,128)(2,1)} async-done(((bf16[4,64,2048]{2,1,0:T(8,128)(2,1)}), bf16[4,64,2048]{2,1,0:T(8,128)(2,1)}, u32[]{:S(2)}, u32[]{:S(2)}) %all-to-all-start.8) | async-done | bytes 1048608 | tf_op jit(solution)/shard_map/all_to_all | solution.py:526
  506.1 11.2 %mixer_backward.3 = (bf16[4,1,64,2176]{3,2,1,0:T(8,128)(2,1)S(1)}, f32[4,2176]{1,0:T(4,128)S(1)}, f32[8,128]{1,0:T(8,128)S(1)}) custom-call(s32[2,4]{1,0:T(2,128)S(1)} %bitcast.234, f32[2,4]{1,0:T(2,128)S(1)} %pad_maximum_fusion.10.rate_ref, bf16[4,2,64,2176]{3,2,1,0:T(8,128)(2,1)S(1)} %bitcast.228, f32[4,2176]{1,0:T(4,128)S(1)} %maximum_convert_fusion.2.taps_ref, ...), custom_call_target="tpu_custom_call" | custom-call | flops 134217728 | bytes 1048576 | tf_op jit(solution)/shard_map/mixer_backward/pallas_call | solution.py:395
  522.0 10.4 %fusion.49 = bf16[2048,3200]{1,0:T(8,128)(2,1)} fusion(bf16[512,2048]{1,0:T(8,128)(2,1)S(1)} %copy-done.34, bf16[512,3200]{1,0:T(8,128)(2,1)S(1)} %bitcast.247), kind=kOutput, calls=%fused_computation.138 | convolution fusion | flops 6710886400 | bytes 18481152 | tf_op jit(solution)/shard_map/dot_general | solution.py:510
  533.6 27.6 %all_to_all.86 = bf16[4,64,2048]{2,1,0:T(8,128)(2,1)S(1)} all-to-all(bf16[4,64,2048]{2,1,0:T(8,128)(2,1)S(1)} %bitcast.268), channel_id=1, replica_groups=mesh['seq'=4,'fsdp'=8] {'seq'}, dimensions={0} | all-to-all | bytes 2097152 | tf_op jit(solution)/shard_map/all_to_all | solution.py:526
  561.2 5.0 fusion.23
  566.3 10.0 %multiply_reduce_fusion = (f32[2048]{0:T(1024)S(1)}, bf16[512,2048]{1,0:T(8,128)(2,1)}) fusion(bf16[4,128,2048]{2,1,0:T(8,128)(2,1)S(1)} %copy-done.14, f32[512]{0:T(512)S(1)} %get-tuple-element.224, f32[512,2048]{1,0:T(8,128)S(1)} %fusion.23, bf16[2048,2176]{1,0:T(8,128)(2,1)} %bitcast.301, bf16[512,3200]{1,0:T(8,128)(2,1)S(1)} %bitcast.249), kind=kOutput, calls=%fused_computation.10 | convolution fusion | flops 4569692160 | bytes 19539968 | tf_op jit(solution)/shard_map/dot_general | solution.py:514
  583.9 4.4 convolution_convert_fusion.3
  592.1 35.3 %all-to-all-done.14 = bf16[4,128,2048]{2,1,0:T(8,128)(2,1)S(1)} async-done(((bf16[4,128,2048]{2,1,0:T(8,128)(2,1)}), bf16[4,128,2048]{2,1,0:T(8,128)(2,1)S(1)}, u32[]{:S(2)}, u32[]{:S(2)}) %all-to-all-start.14) | async-done | bytes 2097184 | tf_op jit(solution)/shard_map/all_to_all | solution.py:526
  627.4 4.4 all-to-all-start.15
  631.8 24.0 %psum.7 = f32[1,104,128]{2,1,0:T(8,128)S(1)} all-reduce(f32[1,104,128]{2,1,0:T(8,128)S(1)} %fusion.33), channel_id=1, replica_groups=mesh['seq'=4,'fsdp'=8] {'fsdp'}, use_global_device_ids=true, to_apply=%region_10.11 | all-reduce | flops 13312 | bytes 106496 | tf_op jit(solution)/shard_map/psum | solution.py:782
  655.8 16.9 %all_gather.31 = f32[4,104,128]{2,1,0:T(8,128)S(1)} all-gather(f32[1,104,128]{2,1,0:T(8,128)S(1)} %psum.7), channel_id=1, replica_groups=mesh['seq'=4,'fsdp'=8] {'seq'}, dimensions={0}, use_global_device_ids=true | all-gather | bytes 266240 | tf_op jit(solution)/shard_map/all_gather | solution.py:783
  693.8 23.8 %all-to-all-done.16 = bf16[4,64,3200]{2,1,0:T(8,128)(2,1)S(1)} async-done(((bf16[4,64,3200]{2,1,0:T(8,128)(2,1)}), bf16[4,64,3200]{2,1,0:T(8,128)(2,1)S(1)}, u32[]{:S(2)}, u32[]{:S(2)}) %all-to-all-start.16) | async-done | bytes 1638432 | tf_op jit(solution)/shard_map/all_to_all | solution.py:526
  (259 shorter events, 161.2 us)
Async XLA Ops:
  7.2 3.1 copy-start.44
  7.2 3.2 copy-start.41
  7.2 3.5 copy-start.38
  14.0 44.7 %all-to-all-start = ((bf16[4,64,3200]{2,1,0:T(8,128)(2,1)}), bf16[4,64,3200]{2,1,0:T(8,128)(2,1)S(1)}, u32[]{:S(2)}, u32[]{:S(2)}) async-start(bf16[4,64,3200]{2,1,0:T(8,128)(2,1)} %bitcast.7), calls=%async_computation | async-start | bytes 3276800 | tf_op jit(solution)/shard_map/all_to_all | solution.py:526
  20.3 95.4 %all-gather.8.cloned.1.call-start = ((), (), s32[]{:S(2)}) async-start(), calls=%async_computation.21 | async-start | bytes 10027008 | tf_op jit(solution)/shard_map/all_gather | solution.py:580
  27.0 33.2 %copy-start.15 = (bf16[2,1,64,2048]{3,2,1,0:T(8,128)(2,1)S(1)}, bf16[2,1,64,2048]{3,2,1,0:T(8,128)(2,1)}, u32[]{:S(2)}) copy-start(bf16[2,1,64,2048]{3,2,1,0:T(8,128)(2,1)} %param.13) | copy-start | bytes 1572868
  59.9 116.2 %all-gather.10.cloned.1.call-start = ((), (), s32[]{:S(2)}) async-start(), calls=%async_computation.22 | async-start | bytes 4718592 | tf_op jit(solution)/shard_map/all_gather | solution.py:580
  110.7 18.4 %copy-start.13 = (bf16[4,128,2048]{2,1,0:T(8,128)(2,1)}, bf16[4,128,2048]{2,1,0:T(8,128)(2,1)S(1)}, u32[]{:S(2)}) copy-start(bf16[4,128,2048]{2,1,0:T(8,128)(2,1)S(1)} %all_to_all.85) | copy-start | bytes 6291460
  110.7 5.7 copy-start.45
  110.7 5.7 copy-start.46
  110.7 5.8 copy-start.31
  113.1 80.7 %all-gather.12.cloned.1.call-start = ((), (), s32[]{:S(2)}) async-start(), calls=%async_computation.23 | async-start | bytes 4718592 | tf_op jit(solution)/shard_map/all_gather | solution.py:637
  115.8 165.7 %all-gather.16.cloned.1.call-start = ((), (), s32[]{:S(2)}) async-start(), calls=%async_computation.29 | async-start | bytes 6488064 | tf_op jit(solution)/shard_map/all_gather | solution.py:636
  118.1 53.6 %all-to-all-start.2 = ((bf16[4,128,2048]{2,1,0:T(8,128)(2,1)}), bf16[4,128,2048]{2,1,0:T(8,128)(2,1)}, u32[]{:S(2)}, u32[]{:S(2)}) async-start(bf16[4,128,2048]{2,1,0:T(8,128)(2,1)} %broadcast_in_dim.11), calls=%async_computation.2 | async-start | bytes 4194304 | tf_op jit(solution)/shard_map/all_to_all | solution.py:526
  131.7 9.1 %copy-start.12 = (s32[2,1,4]{2,1,0:T(1,128)S(1)}, s32[2,1,4]{2,1,0:T(1,128)}, u32[]{:S(2)}) copy-start(s32[2,1,4]{2,1,0:T(1,128)} %param.14) | copy-start | bytes 100
  171.7 38.3 %all-to-all-start.3 = ((bf16[4,64,2816]{2,1,0:T(8,128)(2,1)}), bf16[4,64,2816]{2,1,0:T(8,128)(2,1)}, u32[]{:S(2)}, u32[]{:S(2)}) async-start(bf16[4,64,2816]{2,1,0:T(8,128)(2,1)} %fusion.10), calls=%async_computation.3 | async-start | bytes 2883584 | tf_op jit(solution)/shard_map/all_to_all | solution.py:526
  176.0 132.6 %all-gather.14.cloned.1.call-start = ((), (), s32[]{:S(2)}) async-start(), calls=%async_computation.24 | async-start | bytes 12976128 | tf_op jit(solution)/shard_map/all_gather | solution.py:580
  210.0 35.6 %all-to-all-start.4 = ((bf16[4,64,2048]{2,1,0:T(8,128)(2,1)}), bf16[4,64,2048]{2,1,0:T(8,128)(2,1)}, u32[]{:S(2)}, u32[]{:S(2)}) async-start(bf16[4,64,2048]{2,1,0:T(8,128)(2,1)} %bitcast.272), calls=%async_computation.4 | async-start | bytes 2097152 | tf_op jit(solution)/shard_map/all_to_all | solution.py:526
  245.5 29.8 %all-to-all-start.9 = ((bf16[4,64,2048]{2,1,0:T(8,128)(2,1)}), bf16[4,64,2048]{2,1,0:T(8,128)(2,1)}, u32[]{:S(2)}, u32[]{:S(2)}) async-start(bf16[4,64,2048]{2,1,0:T(8,128)(2,1)} %bitcast.273), calls=%async_computation.9 | async-start | bytes 2097152 | tf_op jit(solution)/shard_map/all_to_all | solution.py:526
  275.3 28.7 %all-to-all-start.5 = ((bf16[4,64,2048]{2,1,0:T(8,128)(2,1)}), bf16[4,64,2048]{2,1,0:T(8,128)(2,1)S(1)}, u32[]{:S(2)}, u32[]{:S(2)}) async-start(bf16[4,64,2048]{2,1,0:T(8,128)(2,1)} %get-tuple-element.80), calls=%async_computation.5 | async-start | bytes 2097152 | tf_op jit(solution)/shard_map/all_to_all | solution.py:526
  304.1 11.0 %copy-start.26 = (bf16[4,64,2048]{2,1,0:T(8,128)(2,1)}, bf16[4,64,2048]{2,1,0:T(8,128)(2,1)S(1)}, u32[]{:S(2)}) copy-start(bf16[4,64,2048]{2,1,0:T(8,128)(2,1)S(1)} %all-to-all-done.5) | copy-start | bytes 3145732
  304.1 29.8 %all-to-all-start.10 = ((bf16[4,64,2048]{2,1,0:T(8,128)(2,1)}), bf16[4,64,2048]{2,1,0:T(8,128)(2,1)}, u32[]{:S(2)}, u32[]{:S(2)}) async-start(bf16[4,64,2048]{2,1,0:T(8,128)(2,1)} %get-tuple-element.95), calls=%async_computation.10 | async-start | bytes 2097152 | tf_op jit(solution)/shard_map/all_to_all | solution.py:526
  308.6 6.5 copy-start.23
  343.2 28.7 %all-to-all-start.6 = ((bf16[4,64,2048]{2,1,0:T(8,128)(2,1)}), bf16[4,64,2048]{2,1,0:T(8,128)(2,1)S(1)}, u32[]{:S(2)}, u32[]{:S(2)}) async-start(bf16[4,64,2048]{2,1,0:T(8,128)(2,1)} %bitcast.271), calls=%async_computation.6 | async-start | bytes 2097152 | tf_op jit(solution)/shard_map/all_to_all | solution.py:526
  346.7 156.0 %reduce-scatter.5.cloned.1.call-start = ((), (), s32[]{:S(2)}) async-start(), calls=%async_computation.25 | async-start | bytes 12976128 | tf_op jit(solution)/shard_map/reduce_scatter | solution.py:701
  347.2 3.4 copy-start.30
  371.9 11.4 %copy-start.24 = (bf16[4,64,2048]{2,1,0:T(8,128)(2,1)}, bf16[4,64,2048]{2,1,0:T(8,128)(2,1)S(1)}, u32[]{:S(2)}) copy-start(bf16[4,64,2048]{2,1,0:T(8,128)(2,1)S(1)} %all-to-all-done.6.terms_ref) | copy-start | bytes 3145732
  385.2 28.7 %all-to-all-start.12 = ((bf16[4,64,2048]{2,1,0:T(8,128)(2,1)}), bf16[4,64,2048]{2,1,0:T(8,128)(2,1)S(1)}, u32[]{:S(2)}, u32[]{:S(2)}) async-start(bf16[4,64,2048]{2,1,0:T(8,128)(2,1)} %bitcast.270), calls=%async_computation.12 | async-start | bytes 2097152 | tf_op jit(solution)/shard_map/all_to_all | solution.py:526
  388.7 187.6 %reduce-scatter.7.cloned.1.call-start = ((), (), s32[]{:S(2)}) async-start(), calls=%async_computation.26 | async-start | bytes 6488064 | tf_op jit(solution)/shard_map/reduce_scatter | solution.py:739
  389.0 11.1 %slice-start = ((s8[5636096]{0:T(1024)(128)(4,1)}), s8[4194304]{0:T(1024)(128)(4,1)S(1)}, s32[]{:S(2)}) async-start(s8[5636096]{0:T(1024)(128)(4,1)} %bitcast.243), calls=%async_computation.30 | async-start | bytes 8388608
  391.0 9.0 %slice-start.1 = ((s8[5636096]{0:T(1024)(128)(4,1)}), s8[1441792]{0:T(1024)(128)(4,1)S(1)}, s32[]{:S(2)}) async-start(s8[5636096]{0:T(1024)(128)(4,1)} %bitcast.243), calls=%async_computation.31 | async-start | bytes 2883584
  391.0 9.0 %copy-start.29 = (bf16[256,1408]{1,0:T(8,128)(2,1)S(1)}, bf16[256,1408]{1,0:T(8,128)(2,1)}, u32[]{:S(2)}) copy-start(bf16[256,1408]{1,0:T(8,128)(2,1)} %get-tuple-element.199) | copy-start | bytes 2162692
  413.9 9.9 %copy-start.25 = (bf16[4,64,2048]{2,1,0:T(8,128)(2,1)}, bf16[4,64,2048]{2,1,0:T(8,128)(2,1)S(1)}, u32[]{:S(2)}) copy-start(bf16[4,64,2048]{2,1,0:T(8,128)(2,1)S(1)} %all-to-all-done.12.terms_ref) | copy-start | bytes 3145732
  413.9 29.5 %all-to-all-start.7 = ((bf16[4,64,2048]{2,1,0:T(8,128)(2,1)}), bf16[4,64,2048]{2,1,0:T(8,128)(2,1)}, u32[]{:S(2)}, u32[]{:S(2)}) async-start(bf16[4,64,2048]{2,1,0:T(8,128)(2,1)} %get-tuple-element.89), calls=%async_computation.7 | async-start | bytes 2097152 | tf_op jit(solution)/shard_map/all_to_all | solution.py:526
  443.4 29.7 %all-to-all-start.13 = ((bf16[4,64,2048]{2,1,0:T(8,128)(2,1)}), bf16[4,64,2048]{2,1,0:T(8,128)(2,1)}, u32[]{:S(2)}, u32[]{:S(2)}) async-start(bf16[4,64,2048]{2,1,0:T(8,128)(2,1)} %get-tuple-element.104), calls=%async_computation.13 | async-start | bytes 2097152 | tf_op jit(solution)/shard_map/all_to_all | solution.py:526
  473.2 29.5 %all-to-all-start.8 = ((bf16[4,64,2048]{2,1,0:T(8,128)(2,1)}), bf16[4,64,2048]{2,1,0:T(8,128)(2,1)}, u32[]{:S(2)}, u32[]{:S(2)}) async-start(bf16[4,64,2048]{2,1,0:T(8,128)(2,1)} %bitcast.269), calls=%async_computation.8 | async-start | bytes 2097152 | tf_op jit(solution)/shard_map/all_to_all | solution.py:526
  477.4 200.6 %reduce-scatter.9.cloned.1.call-start = ((), (), s32[]{:S(2)}) async-start(), calls=%async_computation.27 | async-start | bytes 14745600 | tf_op jit(solution)/shard_map/reduce_scatter | solution.py:701
  477.7 3.8 copy-start.47
  506.1 11.3 %copy-start.37 = (bf16[4,1,64,1024]{3,2,1,0:T(8,128)(2,1)S(1)}, bf16[4,1,64,1024]{3,2,1,0:T(8,128)(2,1)}, u32[]{:S(2)}) copy-start(bf16[4,1,64,1024]{3,2,1,0:T(8,128)(2,1)} %get-tuple-element.110) | copy-start | bytes 1572868
  519.4 13.0 %copy-start.27 = (bf16[4,2,64,3200]{3,2,1,0:T(8,128)(2,1)}, bf16[4,2,64,3200]{3,2,1,0:T(8,128)(2,1)S(1)}, u32[]{:S(2)}) copy-start(bf16[4,2,64,3200]{3,2,1,0:T(8,128)(2,1)S(1)} %copy.149) | copy-start | bytes 9830404
  561.2 5.0 copy-start.14
  561.2 5.1 copy-start.28
  576.3 51.0 %all-to-all-start.14 = ((bf16[4,128,2048]{2,1,0:T(8,128)(2,1)}), bf16[4,128,2048]{2,1,0:T(8,128)(2,1)S(1)}, u32[]{:S(2)}, u32[]{:S(2)}) async-start(bf16[4,128,2048]{2,1,0:T(8,128)(2,1)} %bitcast.256), calls=%async_computation.16 | async-start | bytes 4194304 | tf_op jit(solution)/shard_map/all_to_all | solution.py:526
  580.0 111.7 %reduce-scatter.11.cloned.1.call-start = ((), (), s32[]{:S(2)}) async-start(), calls=%async_computation.28 | async-start | bytes 4718592 | tf_op jit(solution)/shard_map/reduce_scatter | solution.py:755
  592.1 82.2 %copy-start.36 = (bf16[1,172,2048]{2,1,0:T(8,128)(2,1)S(1)}, bf16[1,172,2048]{2,1,0:T(8,128)(2,1)}, u32[]{:S(2)}) copy-start(bf16[1,172,2048]{2,1,0:T(8,128)(2,1)} %reduce-scatter.7.cloned.1.call-done) | copy-start | bytes 2113540
  627.4 45.4 %copy-start.17 = (bf16[4,128,2048]{2,1,0:T(8,128)(2,1)}, bf16[4,128,2048]{2,1,0:T(8,128)(2,1)S(1)}, u32[]{:S(2)}) copy-start(bf16[4,128,2048]{2,1,0:T(8,128)(2,1)S(1)} %all-to-all-done.14) | copy-start | bytes 6291460
  627.4 50.6 %all-to-all-start.15 = ((bf16[4,64,2816]{2,1,0:T(8,128)(2,1)}), bf16[4,64,2816]{2,1,0:T(8,128)(2,1)}, u32[]{:S(2)}, u32[]{:S(2)}) async-start(bf16[4,64,2816]{2,1,0:T(8,128)(2,1)} %reduce-scatter.5.cloned.1.call-done), calls=%async_computation.18 | async-start | bytes 2883584 | tf_op jit(solution)/shard_map/all_to_all | solution.py:526
  678.0 39.5 %all-to-all-start.16 = ((bf16[4,64,3200]{2,1,0:T(8,128)(2,1)}), bf16[4,64,3200]{2,1,0:T(8,128)(2,1)S(1)}, u32[]{:S(2)}, u32[]{:S(2)}) async-start(bf16[4,64,3200]{2,1,0:T(8,128)(2,1)} %reduce-scatter.9.cloned.1.call-done), calls=%async_computation.19 | async-start | bytes 3276800 | tf_op jit(solution)/shard_map/all_to_all | solution.py:526
  (26 other events, 35.9 us)
Sparse Core Ops, SparseCore 0:
  60.0 55.7 all-gather.7
  118.2 36.7 all-gather.9
  157.0 36.8 all-gather.11
  195.6 43.3 all-gather.15
  240.7 67.6 all-gather.13
  383.5 84.9 reduce-scatter.4
  471.9 59.0 reduce-scatter.6
  535.0 95.1 reduce-scatter.8
  633.9 51.3 reduce-scatter.10

commit v3 on v2

--- a/solution.py
+++ b/solution.py
@@ -115,12 +115,11 @@
     return jnp.where(inside, jnp.exp(jnp.where(inside, summed, 0.0)), 0.0)
 
 
-def unit_lower_inverse(strict):
-    size = strict.shape[0]
+def unit_lower_inverses(blocks):
+    size = blocks[0].shape[0]
     rows = lax.broadcasted_iota(jnp.int32, (size, size), 0)
     cols = lax.broadcasted_iota(jnp.int32, (size, size), 1)
-    result = jnp.where(rows == cols, 1.0, 0.0).astype(F32)
-    level = 0
+    level, results = 0, []
     while (1 << level) < size:
         width = 1 << level
         joint = (
@@ -128,13 +127,15 @@
             & ((rows & width) != 0)
             & ((cols & width) == 0)
         )
-        part = jnp.where(joint, strict, 0.0)
+        parts = [jnp.where(joint, block, 0.0) for block in blocks]
         if level == 0:
-            result = result - part
+            unit = jnp.where(rows == cols, 1.0, 0.0).astype(F32)
+            results = [unit - part for part in parts]
         else:
-            result = result - dot3(result, dot3(part, result))
+            inner = [dot3(part, result) for part, result in zip(parts, results)]
+            results = [result - dot3(result, term) for result, term in zip(results, inner)]
         level += 1
-    return result
+    return results
 
 
 def read_rows(ref, offset, width):
@@ -188,30 +189,31 @@
     count = sent_ref.shape[0] * sent_ref.shape[2]
     place, start, rows, cols = pack_masks(pack_ends(lengths_ref, micro, docs), count)
     blocks = count // BLOCK
+    parts = []
     for local in range(per_step):
         head = pl.program_id(0) * per_step + local
         made = head_inputs(sent_ref, taps_ref, rate_ref, head, heads, place, start)
         query = unit_rows(made["q"][5])[0] * DK ** (-0.5)
         keys = unit_rows(made["k"][5])[0]
-        values = made["v"][5]
         beta = made["beta"]
         decay = decay_grid(made["log"], start, rows, cols)
         system = jnp.where(cols < rows, decay, 0.0) * beta * dot3(keys, keys, NT)
-        target = beta * values
+        parts.append((system, beta * made["v"][5], decay * dot1(query, keys, NT)))
+    spans = [slice(block * BLOCK, (block + 1) * BLOCK) for block in range(blocks)]
+    inverses = unit_lower_inverses([system[at, at] for system, _, _ in parts for at in spans])
+    for local in range(per_step):
+        system, target, scores = parts[local]
         updates = []
-        for block in range(blocks):
-            at = slice(block * BLOCK, (block + 1) * BLOCK)
-            inverse = unit_lower_inverse(system[at, at])
+        for block, at in enumerate(spans):
+            inverse = inverses[local * blocks + block]
             inverse_ref[local, block] = inverse
             right = target[at]
             for earlier in range(block):
-                right = right - dot3(
-                    system[at, earlier * BLOCK : (earlier + 1) * BLOCK], updates[earlier]
-                )
+                right = right - dot3(system[at, spans[earlier]], updates[earlier])
             updates.append(dot3(inverse, right))
         update = jnp.concatenate(updates, axis=0)
         update_ref[local] = update
-        scores = decay * dot1(query, keys, NT)
+        head = pl.program_id(0) * per_step + local
         write_rows(mixed_ref, pl.multiple_of(head * DV, LANES), dot1(scores, update))
 
 
@@ -335,6 +337,37 @@
         )
 
 
+def pack_kernel(query_ref, key_ref, value_ref, pairs_ref, gate_ref, out_ref):
+    at = 0
+    for ref in (query_ref, key_ref, value_ref, pairs_ref, gate_ref):
+        block = ref[...].reshape(out_ref.shape[1], ref.shape[-1])
+        out_ref[0, :, at : at + ref.shape[-1]] = block
+        at += ref.shape[-1]
+
+
+def pack_columns(weight, pairs, spans):
+    rows = weight.shape[0]
+    qw, vw = H * DK // spans, H * DV // spans
+    width = 2 * qw + 2 * vw + pairs.shape[2]
+    start = 2 * H * DK // vw
+
+    def spec(columns, first):
+        return pl.BlockSpec((rows, columns), lambda s: (0, first + s))
+
+    return pl.pallas_call(
+        pack_kernel,
+        grid=(spans,),
+        in_specs=[
+            spec(qw, 0), spec(qw, spans), spec(vw, start),
+            pl.BlockSpec((1, rows, pairs.shape[2]), lambda s: (s, 0, 0)),
+            spec(vw, start + spans),
+        ],
+        out_specs=pl.BlockSpec((1, rows, width), lambda s: (s, 0, 0)),
+        out_shape=jax.ShapeDtypeStruct((spans, rows, width), BF16),
+        name="pack_columns",
+    )(weight, weight, weight, pairs, weight)
+
+
 def row_spec(array, micro):
     spans, micros, length, width = array.shape
     pick = micro if micros > 1 else 0
@@ -362,7 +395,7 @@
 
 def mixer_forward(micro, lengths, rates, sent, taps, heads):
     spans, _, length, width = sent.shape
-    count, per_step = spans * length, 2 if heads % 2 == 0 else 1
+    count, per_step = spans * length, 4 if heads % 4 == 0 else 1 + (heads % 2 == 0)
     blocks = count // BLOCK
     smem = pl.BlockSpec(memory_space=pltpu.SMEM)
     mixed = jax.ShapeDtypeStruct((spans, 1, length, heads * DV), BF16)
@@ -408,7 +441,7 @@
             jax.ShapeDtypeStruct((8, LANES), F32),
         ],
         compiler_params=pltpu.CompilerParams(vmem_limit_bytes=40 * 1024 * 1024),
-        cost_estimate=mixer_cost(sent, heads, 1),
+        cost_estimate=mixer_cost(sent, heads, 40),
         name="mixer_backward",
     )(lengths, rates, sent, taps, update, inverse, grad)
 
@@ -587,13 +620,7 @@
     pairs = jnp.concatenate([decay_weight.reshape(share, spans, 2 * heads), small], axis=2)
     pair_at = 2 * qw + vw
     mix_width = pair_at + LANES
-    in_blocks = by_span([
-        columns(in_weight, 0, qw),
-        columns(in_weight, H * DK, qw),
-        columns(in_weight, 2 * H * DK, vw),
-        widen(pairs, LANES),
-        columns(in_weight, 2 * H * DK + H * DV, vw),
-    ])
+    in_blocks = pack_columns(in_weight, widen(pairs, LANES).swapaxes(0, 1), spans)
     up_blocks = by_span([
         widen(columns(up_weight, 0, fw), fp),
         widen(columns(up_weight, FF, fw), fp),
@@ -684,7 +711,7 @@
         sums.append(rows)
     act = jnp.stack(acts, axis=1).reshape(all_rows, fp)[:, :fw]
     final_rows = [dot(a.reshape(-1, fp)[:, :fw], w_down).astype(BF16) for a in acts]
-    down_grads = outer(act, cot).astype(BF16).reshape(packs, -1, D)
+    down_grads = outer(after(act, act), cot).astype(BF16).reshape(packs, -1, D)
     spare = [final_rows[:1], final_rows[1:] + [down_grads]]
     grad_middles, grad_branches, grad_gain2 = [], [], 0.0
     for micro in range(micros):
@@ -741,24 +768,32 @@
     )
     in_product = outer(after(first, finals[0]), grad_proj)
     in_grads = reduce_rows(in_product, spans)
-    grad_proj = after(grad_proj, in_product, finals[-1])
+    grad_proj = after(grad_proj, in_product)
     grad_first = dot_back(grad_proj[:, :mix_width], w_mix) + dot_back(
         grad_proj[:, mix_width:], w_gate
     )
     grad_gain1 = jnp.sum(inputs * input_scale * grad_first, axis=0)
     first_rows = grad_first.astype(BF16)
-    first_rows, grad_down, up_grads = lax.optimization_barrier((first_rows, grad_down, up_grads))
-    grad_first = scatter_rows(first_rows, spans)
+    grad_first = scatter_rows(after(first_rows, grad_down, up_grads), spans)
     out_grads = outer(
         all_micros([n[:, 0] for n in normeds]), after(all_micros(grad_branches), first_rows)
     )
     grad_out = lax.psum_scatter(
         out_grads.astype(BF16), "fsdp", scatter_dimension=0, tiled=True
     ).astype(F32)
+    gain_rows = jnp.stack([grad_gain1, grad_gain2[0]])
+    flat = jnp.concatenate([
+        grad_taps[:, :pair_at].reshape(-1), gain_rows.reshape(-1), grad_gain.reshape(-1),
+        grad_small[:2].reshape(-1),
+    ])
+    flat = jnp.pad(flat, (0, round_up(flat.size, 8 * LANES) - flat.size)).reshape(-1, LANES)
+    flat = lax.psum(after(flat, grad_gain1), "fsdp")
+    flat = lax.all_gather(flat, "seq", axis=0).reshape(spans, -1)
     grad_norm1, _ = norm_back(
         local_tokens.astype(F32), gains[0], jnp.sum(grad_first.astype(F32), axis=0)
     )
     grad_tokens = jnp.stack(grad_middles).reshape(local_rows, D) + grad_norm1
+    up_grads, flat = lax.optimization_barrier((up_grads, flat))
     up_grads = exchange(after(up_grads, grad_first))
     in_grads = exchange(after(in_grads, up_grads))
     grad_up = jnp.concatenate([joined(up_grads, 0, fw), joined(up_grads, fp, fw)], axis=1)
@@ -773,14 +808,6 @@
     )
     grad_decay = joined(in_grads, pair_at, 2 * heads)
 
-    gain_rows = jnp.stack([grad_gain1, grad_gain2[0]])
-    flat = jnp.concatenate([
-        grad_taps[:, :pair_at].reshape(-1), gain_rows.reshape(-1), grad_gain.reshape(-1),
-        grad_small[:2].reshape(-1),
-    ])
-    flat = jnp.pad(flat, (0, round_up(flat.size, 8 * LANES) - flat.size)).reshape(-1, LANES)
-    flat = lax.psum(flat, "fsdp")
-    flat = lax.all_gather(flat, "seq", axis=0).reshape(spans, -1)
     taps_flat = flat[:, : CONV * pair_at].reshape(spans, CONV, pair_at)
 
     def all_taps(start, width):

time: 735 us -> 709 us (0.965)
  blocking collectives: 119 us -> 93.2 us
  Pallas kernels: 90.6 us -> 70.7 us
  waiting for transfers between devices: 195 us -> 205 us
    all_to_all x2 -> x1, blocking collectives: 77.8 us -> 50.2 us  [exchange(): lax.all_to_all(blocks, 'seq', split_axis=0, concat_axis=0, tiled=True)]
    pallas_call x2, Pallas kernels: 40.4 us -> 17.1 us  [mixer_forward(): pl.pallas_call(partial(mixer_forward_kernel, micro, per_step, heads, leng...]
    reduce_scatter x1, waiting for transfers between devices: 0.01 us -> 16.5 us  [shards(): lax.psum_scatter(out_grads.astype(BF16), 'fsdp', scatter_dimension=0, til...]
    all_to_all x15 -> x16, waiting for transfers between devices: 184 us -> 172 us  [exchange(): lax.all_to_all(blocks, 'seq', split_axis=0, concat_axis=0, tiled=True)]
    all_to_all x15 -> x16, starting transfers between devices: 64.8 us -> 68.1 us  [exchange(): lax.all_to_all(blocks, 'seq', split_axis=0, concat_axis=0, tiled=True)]
    unnamed x117 -> x100, local copies, waits for them, and re-layouts: 31.4 us -> 29.1 us
  transfers between devices with their start and end apart: 24 -> 25, of which waited for: 15 -> 19; matrix products, arithmetic and copies ran while one was open for 26% -> 29% of each run, Pallas kernels for 12% -> 10%
where the time goes in v3:
time: 709 us; the launch traced here: 702 us
  waiting for transfers between devices  205 us (29%)
  matrix products  135 us (19%)
  blocking collectives  93.2 us (13%)
  Pallas kernels  70.7 us (10%)
  starting transfers between devices  69.4 us (10%)
  local copies, waits for them, and re-layouts  65.3 us (9%)
  other arithmetic  48.6 us (7%)
  between operations  15 us (2%)
    all_to_all x16, waiting for transfers between devices, exchange(): lax.all_to_all(blocks, 'seq', split_axis=0, concat_axis=0, tiled=True)  172 us
    all_to_all x16, starting transfers between devices, exchange(): lax.all_to_all(blocks, 'seq', split_axis=0, concat_axis=0, tiled=True)  68.1 us
    dot_general x8, matrix products, dot(): return jnp.dot(left, right, preferred_element_type=F32)  52 us
    all_to_all x1, blocking collectives, exchange(): lax.all_to_all(blocks, 'seq', split_axis=0, concat_axis=0, tiled=True)  50.2 us
    dot_general x7, matrix products, dot_back(): return lax.dot_general(left, right, NT, preferred_element_type=F32)  48.9 us
    dot_general x4, matrix products, outer(): return lax.dot_general(left, right, TN, preferred_element_type=F32)  34.3 us
    unnamed x100, local copies, waits for them, and re-layouts  29.1 us
    psum x1, blocking collectives, shards(): flat = lax.psum(after(flat, grad_gain1), 'fsdp')  24.5 us
  transfers between devices with their start and end apart: 25, of which 19 were waited for; matrix products, arithmetic and copies ran while one was open for 29% of the time, Pallas kernels for 10%

profile of v3, /device:TPU:0, one launch (start us, length us, event | category | flops | bytes accessed | tf_op | source)
XLA Modules:
  0.0 702.4 jit_solution(10873094299921878006)
XLA Ops:
  14.2 6.3 all-to-all-start
  30.9 28.0 %all-to-all-done = bf16[4,64,3200]{2,1,0:T(8,128)(2,1)S(1)} async-done(((bf16[4,64,3200]{2,1,0:T(8,128)(2,1)}), bf16[4,64,3200]{2,1,0:T(8,128)(2,1)S(1)}, u32[]{:S(2)}, u32[]{:S(2)}) %all-to-all-start) | async-done | bytes 1638432 | tf_op jit(solution)/shard_map/all_to_all | solution.py:559
  60.7 50.2 %all_to_all.85 = bf16[4,128,2048]{2,1,0:T(8,128)(2,1)S(1)} all-to-all(bf16[4,128,2048]{2,1,0:T(8,128)(2,1)S(1)} %broadcast_in_dim.9), channel_id=1, replica_groups=mesh['seq'=4,'fsdp'=8] {'seq'}, dimensions={0} | all-to-all | bytes 4194304 | tf_op jit(solution)/shard_map/all_to_all | solution.py:559
  118.3 5.1 all-to-all-start.2
  133.3 9.1 %convolution_convert_fusion.2 = bf16[512,2176]{1,0:T(8,128)(2,1)S(1)} fusion(bf16[512,2048]{1,0:T(8,128)(2,1)} %bitcast.250, bf16[2048,2176]{1,0:T(8,128)(2,1)} %bitcast.286), kind=kOutput, calls=%fused_computation.4 | convolution fusion | flops 4564516864 | bytes 13238272 | tf_op jit(solution)/shard_map/dot_general | solution.py:539
  142.4 8.6 %mixer_forward.2 = (bf16[4,1,64,1024]{3,2,1,0:T(8,128)(2,1)S(1)}, f32[4,256,256]{2,1,0:T(8,128)S(1)}, f32[4,2,128,128]{3,2,1,0:T(8,128)S(1)}) custom-call(s32[2,4]{1,0:T(2,128)S(1)} %bitcast.220, f32[2,4]{1,0:T(2,128)S(1)} %pad_maximum_fusion.10.rate_ref, bf16[4,2,64,2176]{3,2,1,0:T(8,128)(2,1)S(1)} %bitcast.224, f32[4,2176]{1,0:T(4,128)S(1)} %maximum_convert_fusion.2.taps_ref), custom_call_target="tpu_custom_call" | custom-call | flops 8053063680 | bytes 62914560 | tf_op jit(solution)/shard_map/mixer_forward/pallas_call | solution.py:402
  154.2 18.0 %all-to-all-done.2 = bf16[4,128,2048]{2,1,0:T(8,128)(2,1)} async-done(((bf16[4,128,2048]{2,1,0:T(8,128)(2,1)}), bf16[4,128,2048]{2,1,0:T(8,128)(2,1)}, u32[]{:S(2)}, u32[]{:S(2)}) %all-to-all-start.2) | async-done | bytes 2097184 | tf_op jit(solution)/shard_map/all_to_all | solution.py:559
  176.0 6.5 fusion.43.gate_ref
  186.2 7.6 %all-gather.12.cloned.1.call-done = bf16[1024,2048]{1,0:T(8,128)(2,1)} async-done(((bf16[128,2048]{1,0:T(8,128)(2,1)}), bf16[1024,2048]{1,0:T(8,128)(2,1)}) %all-gather.12.cloned.1.call-update) | async-done | bytes 4194320 | tf_op jit(solution)/shard_map/all_gather | solution.py:664
  193.8 4.6 convolution_convert_fusion.7
  198.4 11.1 %all-to-all-done.3 = bf16[4,64,2816]{2,1,0:T(8,128)(2,1)S(1)} async-done(((bf16[4,64,2816]{2,1,0:T(8,128)(2,1)}), bf16[4,64,2816]{2,1,0:T(8,128)(2,1)S(1)}, u32[]{:S(2)}, u32[]{:S(2)}) %all-to-all-start.3) | async-done | bytes 1441824 | tf_op jit(solution)/shard_map/all_to_all | solution.py:559
  216.6 8.6 %mixer_forward.3 = (bf16[4,1,64,1024]{3,2,1,0:T(8,128)(2,1)S(1)}, f32[4,256,256]{2,1,0:T(8,128)S(1)}, f32[4,2,128,128]{3,2,1,0:T(8,128)S(1)}) custom-call(s32[2,4]{1,0:T(2,128)S(1)} %bitcast.221, f32[2,4]{1,0:T(2,128)S(1)} %pad_maximum_fusion.10.rate_ref, bf16[4,2,64,2176]{3,2,1,0:T(8,128)(2,1)S(1)} %bitcast.225, f32[4,2176]{1,0:T(4,128)S(1)} %maximum_convert_fusion.2.taps_ref), custom_call_target="tpu_custom_call" | custom-call | flops 8053063680 | bytes 62914560 | tf_op jit(solution)/shard_map/mixer_forward/pallas_call | solution.py:402
  229.6 4.7 convolution_convert_fusion.6
  234.3 5.9 all-to-all-done.4.terms_ref
  247.9 21.9 %all-to-all-done.9.terms_ref = bf16[4,64,2048]{2,1,0:T(8,128)(2,1)} async-done(((bf16[4,64,2048]{2,1,0:T(8,128)(2,1)}), bf16[4,64,2048]{2,1,0:T(8,128)(2,1)}, u32[]{:S(2)}, u32[]{:S(2)}) %all-to-all-start.9) | async-done | bytes 1048608 | tf_op jit(solution)/shard_map/all_to_all | solution.py:559
  276.5 5.9 reshape.472
  282.3 6.5 fusion
  290.6 8.0 %all-to-all-done.5 = bf16[4,64,2048]{2,1,0:T(8,128)(2,1)S(1)} async-done(((bf16[4,64,2048]{2,1,0:T(8,128)(2,1)}), bf16[4,64,2048]{2,1,0:T(8,128)(2,1)S(1)}, u32[]{:S(2)}, u32[]{:S(2)}) %all-to-all-start.5) | async-done | bytes 1048608 | tf_op jit(solution)/shard_map/all_to_all | solution.py:559
  302.9 6.0 all-gather.14.cloned.1.call-done
  309.0 6.4 fusion.44
  318.2 8.4 %convolution_convert_fusion.5 = bf16[256,2048]{1,0:T(8,128)(2,1)} fusion(bf16[2048,2816]{1,0:T(8,128)(2,1)} %bitcast.303, bf16[256,1408]{1,0:T(8,128)(2,1)S(1)} %get-tuple-element.195, bf16[256,1408]{1,0:T(8,128)(2,1)S(1)} %get-tuple-element.194), kind=kOutput, calls=%fused_computation.24 | convolution fusion | flops 2956197888 | bytes 14024704 | tf_op jit(solution)/shard_map/dot_general | solution.py:547
  328.2 9.3 %fusion.45 = f32[256,2816]{1,0:T(8,128)} fusion(bf16[256,2048]{1,0:T(8,128)(2,1)} %bitcast.43, bf16[2048,2816]{1,0:T(8,128)(2,1)} %bitcast.304), kind=kOutput, calls=%fused_computation.131 | convolution fusion | flops 2952790016 | bytes 15466496 | tf_op jit(solution)/shard_map/dot_general | solution.py:539
  350.6 8.4 %convolution_convert_fusion.4 = bf16[256,2048]{1,0:T(8,128)(2,1)} fusion(bf16[2048,2816]{1,0:T(8,128)(2,1)} %bitcast.305, bf16[256,1408]{1,0:T(8,128)(2,1)S(1)} %get-tuple-element.193, bf16[256,1408]{1,0:T(8,128)(2,1)S(1)} %get-tuple-element.192), kind=kOutput, calls=%fused_computation.23 | convolution fusion | flops 2956197888 | bytes 14024704 | tf_op jit(solution)/shard_map/dot_general | solution.py:547
  359.0 7.8 %all-to-all-done.6.terms_ref = bf16[4,64,2048]{2,1,0:T(8,128)(2,1)S(1)} async-done(((bf16[4,64,2048]{2,1,0:T(8,128)(2,1)}), bf16[4,64,2048]{2,1,0:T(8,128)(2,1)S(1)}, u32[]{:S(2)}, u32[]{:S(2)}) %all-to-all-start.6) | async-done | bytes 1048608 | tf_op jit(solution)/shard_map/all_to_all | solution.py:559
  366.7 11.4 %convolution_convert_fusion = bf16[2048,2816]{1,0:T(8,128)(2,1)} fusion(bf16[512,2048]{1,0:T(8,128)(2,1)} %bitcast.248, bf16[512,2816]{1,0:T(8,128)(2,1)} %bitcast.243), kind=kOutput, calls=%fused_computation | convolution fusion | flops 5911347200 | bytes 16515072 | tf_op jit(solution)/shard_map/dot_general | solution.py:543
  385.6 8.2 %convolution_convert_fusion.1 = bf16[1376,2048]{1,0:T(8,128)(2,1)} fusion(bf16[512,1376]{1,0:T(8,128)(2,1)S(1)} %bitcast.254, bf16[512,2048]{1,0:T(8,128)(2,1)} %bitcast.24), kind=kOutput, calls=%fused_computation.1 | convolution fusion | flops 2888499200 | bytes 9142272 | tf_op jit(solution)/shard_map/dot_general | solution.py:543
  393.9 6.0 reshape.431
  399.9 5.6 convolution_convert_fusion.9
  408.7 4.8 all-to-all-start.7
  413.5 5.9 convolution_convert_fusion.8
  422.6 16.2 %all-to-all-done.7 = bf16[4,64,2048]{2,1,0:T(8,128)(2,1)} async-done(((bf16[4,64,2048]{2,1,0:T(8,128)(2,1)}), bf16[4,64,2048]{2,1,0:T(8,128)(2,1)}, u32[]{:S(2)}, u32[]{:S(2)}) %all-to-all-start.7) | async-done | bytes 1048608 | tf_op jit(solution)/shard_map/all_to_all | solution.py:559
  438.8 4.5 all-to-all-start.13
  443.3 5.6 fusion.11.grad_ref
  456.9 11.2 %mixer_backward.2 = (bf16[4,1,64,2176]{3,2,1,0:T(8,128)(2,1)S(1)}, f32[4,2176]{1,0:T(4,128)S(1)}, f32[8,128]{1,0:T(8,128)S(1)}) custom-call(s32[2,4]{1,0:T(2,128)S(1)} %bitcast.222, f32[2,4]{1,0:T(2,128)S(1)} %pad_maximum_fusion.10.rate_ref, bf16[4,2,64,2176]{3,2,1,0:T(8,128)(2,1)S(1)} %bitcast.226, f32[4,2176]{1,0:T(4,128)S(1)} %maximum_convert_fusion.2.taps_ref, ...), custom_call_target="tpu_custom_call" | custom-call | flops 5368709120 | bytes 41943040 | tf_op jit(solution)/shard_map/mixer_backward/pallas_call | solution.py:428
  468.5 4.6 all-to-all-start.8
  487.7 10.4 %all-to-all-done.8 = bf16[4,64,2048]{2,1,0:T(8,128)(2,1)} async-done(((bf16[4,64,2048]{2,1,0:T(8,128)(2,1)}), bf16[4,64,2048]{2,1,0:T(8,128)(2,1)}, u32[]{:S(2)}, u32[]{:S(2)}) %all-to-all-start.8) | async-done | bytes 1048608 | tf_op jit(solution)/shard_map/all_to_all | solution.py:559
  499.7 11.3 %mixer_backward.3 = (bf16[4,1,64,2176]{3,2,1,0:T(8,128)(2,1)S(1)}, f32[4,2176]{1,0:T(4,128)S(1)}, f32[8,128]{1,0:T(8,128)S(1)}) custom-call(s32[2,4]{1,0:T(2,128)S(1)} %bitcast.223, f32[2,4]{1,0:T(2,128)S(1)} %pad_maximum_fusion.10.rate_ref, bf16[4,2,64,2176]{3,2,1,0:T(8,128)(2,1)S(1)} %bitcast.227, f32[4,2176]{1,0:T(4,128)S(1)} %maximum_convert_fusion.2.taps_ref, ...), custom_call_target="tpu_custom_call" | custom-call | flops 5368709120 | bytes 41943040 | tf_op jit(solution)/shard_map/mixer_backward/pallas_call | solution.py:428
  515.2 10.3 %fusion.46 = bf16[2048,3200]{1,0:T(8,128)(2,1)} fusion(bf16[512,2048]{1,0:T(8,128)(2,1)S(1)} %copy-done.31, bf16[512,3200]{1,0:T(8,128)(2,1)S(1)} %bitcast.238), kind=kOutput, calls=%fused_computation.132 | convolution fusion | flops 6710886400 | bytes 18481152 | tf_op jit(solution)/shard_map/dot_general | solution.py:543
  529.6 5.0 fusion.22
  534.7 11.4 %multiply_reduce_fusion = (f32[2048]{0:T(1024)S(1)}, bf16[512,2048]{1,0:T(8,128)(2,1)}) fusion(bf16[4,128,2048]{2,1,0:T(8,128)(2,1)S(1)} %copy-done.12, f32[512]{0:T(512)S(1)} %get-tuple-element.222, f32[512,2048]{1,0:T(8,128)S(1)} %fusion.22, bf16[2048,2176]{1,0:T(8,128)(2,1)} %bitcast.287, bf16[512,3200]{1,0:T(8,128)(2,1)S(1)} %bitcast.240), kind=kOutput, calls=%fused_computation.10 | convolution fusion | flops 4569692160 | bytes 19539968 | tf_op jit(solution)/shard_map/dot_general | solution.py:547
  546.1 8.7 %all-to-all-done.11 = bf16[4,64,2048]{2,1,0:T(8,128)(2,1)S(1)} async-done(((bf16[4,64,2048]{2,1,0:T(8,128)(2,1)}), bf16[4,64,2048]{2,1,0:T(8,128)(2,1)S(1)}, u32[]{:S(2)}, u32[]{:S(2)}) %all-to-all-start.11) | async-done | bytes 1048608 | tf_op jit(solution)/shard_map/all_to_all | solution.py:559
  564.8 4.3 convolution_convert_fusion.3
  570.8 24.5 %psum.7 = f32[1,104,128]{2,1,0:T(8,128)S(1)} all-reduce(f32[1,104,128]{2,1,0:T(8,128)S(1)} %bitcast.276), channel_id=1, replica_groups=mesh['seq'=4,'fsdp'=8] {'fsdp'}, use_global_device_ids=true, to_apply=%region_10.11 | all-reduce | flops 13312 | bytes 106496 | tf_op jit(solution)/shard_map/psum | solution.py:790
  595.3 18.6 %all_gather.31 = f32[4,104,128]{2,1,0:T(8,128)S(1)} all-gather(f32[1,104,128]{2,1,0:T(8,128)S(1)} %psum.7), channel_id=1, replica_groups=mesh['seq'=4,'fsdp'=8] {'seq'}, dimensions={0}, use_global_device_ids=true | all-gather | bytes 266240 | tf_op jit(solution)/shard_map/all_gather | solution.py:791
  614.0 4.3 all-to-all-start.15
  627.2 23.9 %all-to-all-done.15 = bf16[4,64,2816]{2,1,0:T(8,128)(2,1)} async-done(((bf16[4,64,2816]{2,1,0:T(8,128)(2,1)}), bf16[4,64,2816]{2,1,0:T(8,128)(2,1)}, u32[]{:S(2)}, u32[]{:S(2)}) %all-to-all-start.15) | async-done | bytes 1441824 | tf_op jit(solution)/shard_map/all_to_all | solution.py:559
  664.7 16.5 %reduce-scatter.11.cloned.1.call-done = bf16[128,2048]{1,0:T(8,128)(2,1)} async-done(((bf16[1024,2048]{1,0:T(8,128)(2,1)}), bf16[128,2048]{1,0:T(8,128)(2,1)}) %reduce-scatter.11.cloned.1.call-update) | async-done | bytes 524304 | tf_op jit(solution)/shard_map/reduce_scatter | solution.py:781
  683.3 9.5 %all-to-all-done.16 = bf16[4,64,3200]{2,1,0:T(8,128)(2,1)S(1)} async-done(((bf16[4,64,3200]{2,1,0:T(8,128)(2,1)}), bf16[4,64,3200]{2,1,0:T(8,128)(2,1)S(1)}, u32[]{:S(2)}, u32[]{:S(2)}) %all-to-all-start.16) | async-done | bytes 1638432 | tf_op jit(solution)/shard_map/all_to_all | solution.py:559
  (240 shorter events, 181.9 us)
Async XLA Ops:
  14.2 44.7 %all-to-all-start = ((bf16[4,64,3200]{2,1,0:T(8,128)(2,1)}), bf16[4,64,3200]{2,1,0:T(8,128)(2,1)S(1)}, u32[]{:S(2)}, u32[]{:S(2)}) async-start(bf16[4,64,3200]{2,1,0:T(8,128)(2,1)} %pack_columns.1), calls=%async_computation | async-start | bytes 3276800 | tf_op jit(solution)/shard_map/all_to_all | solution.py:559
  20.5 95.4 %all-gather.8.cloned.1.call-start = ((), (), s32[]{:S(2)}) async-start(), calls=%async_computation.21 | async-start | bytes 10027008 | tf_op jit(solution)/shard_map/all_gather | solution.py:613
  30.9 29.5 %copy-start.13 = (bf16[2,1,64,2048]{3,2,1,0:T(8,128)(2,1)S(1)}, bf16[2,1,64,2048]{3,2,1,0:T(8,128)(2,1)}, u32[]{:S(2)}) copy-start(bf16[2,1,64,2048]{3,2,1,0:T(8,128)(2,1)} %param.13) | copy-start | bytes 1572868
  60.1 115.9 %all-gather.10.cloned.1.call-start = ((), (), s32[]{:S(2)}) async-start(), calls=%async_computation.22 | async-start | bytes 4718592 | tf_op jit(solution)/shard_map/all_gather | solution.py:613
  110.9 19.0 %copy-start.11 = (bf16[4,128,2048]{2,1,0:T(8,128)(2,1)}, bf16[4,128,2048]{2,1,0:T(8,128)(2,1)S(1)}, u32[]{:S(2)}) copy-start(bf16[4,128,2048]{2,1,0:T(8,128)(2,1)S(1)} %all_to_all.85) | copy-start | bytes 6291460
  110.9 5.7 copy-start.40
  110.9 5.7 copy-start.41
  110.9 5.8 copy-start.28
  113.3 80.5 %all-gather.12.cloned.1.call-start = ((), (), s32[]{:S(2)}) async-start(), calls=%async_computation.23 | async-start | bytes 4718592 | tf_op jit(solution)/shard_map/all_gather | solution.py:664
  116.0 160.5 %all-gather.16.cloned.1.call-start = ((), (), s32[]{:S(2)}) async-start(), calls=%async_computation.29 | async-start | bytes 6488064 | tf_op jit(solution)/shard_map/all_gather | solution.py:663
  118.3 53.9 %all-to-all-start.2 = ((bf16[4,128,2048]{2,1,0:T(8,128)(2,1)}), bf16[4,128,2048]{2,1,0:T(8,128)(2,1)}, u32[]{:S(2)}, u32[]{:S(2)}) async-start(bf16[4,128,2048]{2,1,0:T(8,128)(2,1)} %broadcast_in_dim.11), calls=%async_computation.2 | async-start | bytes 4194304 | tf_op jit(solution)/shard_map/all_to_all | solution.py:559
  125.2 6.5 copy-start.32
  129.8 343.6 %copy-start.34 = (f32[1,2048]{1,0:T(1,128)}, f32[1,2048]{1,0:T(1,128)S(1)}, u32[]{:S(2)}) copy-start(f32[1,2048]{1,0:T(1,128)S(1)} %get-tuple-element.221) | copy-start | bytes 24580
  133.3 9.1 %copy-start.4 = (s32[2,1,4]{2,1,0:T(1,128)S(1)}, s32[2,1,4]{2,1,0:T(1,128)}, u32[]{:S(2)}) copy-start(s32[2,1,4]{2,1,0:T(1,128)} %param.14) | copy-start | bytes 100
  172.2 37.3 %all-to-all-start.3 = ((bf16[4,64,2816]{2,1,0:T(8,128)(2,1)}), bf16[4,64,2816]{2,1,0:T(8,128)(2,1)S(1)}, u32[]{:S(2)}, u32[]{:S(2)}) async-start(bf16[4,64,2816]{2,1,0:T(8,128)(2,1)} %fusion.10), calls=%async_computation.3 | async-start | bytes 2883584 | tf_op jit(solution)/shard_map/all_to_all | solution.py:559
  175.8 133.2 %all-gather.14.cloned.1.call-start = ((), (), s32[]{:S(2)}) async-start(), calls=%async_computation.24 | async-start | bytes 12976128 | tf_op jit(solution)/shard_map/all_gather | solution.py:613
  210.7 29.5 %all-to-all-start.4 = ((bf16[4,64,2048]{2,1,0:T(8,128)(2,1)}), bf16[4,64,2048]{2,1,0:T(8,128)(2,1)}, u32[]{:S(2)}, u32[]{:S(2)}) async-start(bf16[4,64,2048]{2,1,0:T(8,128)(2,1)} %bitcast.260), calls=%async_computation.4 | async-start | bytes 2097152 | tf_op jit(solution)/shard_map/all_to_all | solution.py:559
  240.2 29.5 %all-to-all-start.9 = ((bf16[4,64,2048]{2,1,0:T(8,128)(2,1)}), bf16[4,64,2048]{2,1,0:T(8,128)(2,1)}, u32[]{:S(2)}, u32[]{:S(2)}) async-start(bf16[4,64,2048]{2,1,0:T(8,128)(2,1)} %bitcast.261), calls=%async_computation.9 | async-start | bytes 2097152 | tf_op jit(solution)/shard_map/all_to_all | solution.py:559
  269.7 28.9 %all-to-all-start.5 = ((bf16[4,64,2048]{2,1,0:T(8,128)(2,1)}), bf16[4,64,2048]{2,1,0:T(8,128)(2,1)S(1)}, u32[]{:S(2)}, u32[]{:S(2)}) async-start(bf16[4,64,2048]{2,1,0:T(8,128)(2,1)} %get-tuple-element.81), calls=%async_computation.5 | async-start | bytes 2097152 | tf_op jit(solution)/shard_map/all_to_all | solution.py:559
  298.7 16.7 %copy-start.24 = (bf16[4,64,2048]{2,1,0:T(8,128)(2,1)}, bf16[4,64,2048]{2,1,0:T(8,128)(2,1)S(1)}, u32[]{:S(2)}) copy-start(bf16[4,64,2048]{2,1,0:T(8,128)(2,1)S(1)} %all-to-all-done.5) | copy-start | bytes 3145732
  298.7 29.5 %all-to-all-start.10 = ((bf16[4,64,2048]{2,1,0:T(8,128)(2,1)}), bf16[4,64,2048]{2,1,0:T(8,128)(2,1)}, u32[]{:S(2)}, u32[]{:S(2)}) async-start(bf16[4,64,2048]{2,1,0:T(8,128)(2,1)} %get-tuple-element.96), calls=%async_computation.10 | async-start | bytes 2097152 | tf_op jit(solution)/shard_map/all_to_all | solution.py:559
  309.0 6.4 copy-start.21
  337.5 29.2 %all-to-all-start.6 = ((bf16[4,64,2048]{2,1,0:T(8,128)(2,1)}), bf16[4,64,2048]{2,1,0:T(8,128)(2,1)S(1)}, u32[]{:S(2)}, u32[]{:S(2)}) async-start(bf16[4,64,2048]{2,1,0:T(8,128)(2,1)} %bitcast.259), calls=%async_computation.6 | async-start | bytes 2097152 | tf_op jit(solution)/shard_map/all_to_all | solution.py:559
  341.1 157.0 %reduce-scatter.5.cloned.1.call-start = ((), (), s32[]{:S(2)}) async-start(), calls=%async_computation.25 | async-start | bytes 12976128 | tf_op jit(solution)/shard_map/reduce_scatter | solution.py:728
  341.5 3.4 copy-start.27
  366.7 11.4 %copy-start.22 = (bf16[4,64,2048]{2,1,0:T(8,128)(2,1)}, bf16[4,64,2048]{2,1,0:T(8,128)(2,1)S(1)}, u32[]{:S(2)}) copy-start(bf16[4,64,2048]{2,1,0:T(8,128)(2,1)S(1)} %all-to-all-done.6.terms_ref) | copy-start | bytes 3145732
  380.0 28.7 %all-to-all-start.12 = ((bf16[4,64,2048]{2,1,0:T(8,128)(2,1)}), bf16[4,64,2048]{2,1,0:T(8,128)(2,1)S(1)}, u32[]{:S(2)}, u32[]{:S(2)}) async-start(bf16[4,64,2048]{2,1,0:T(8,128)(2,1)} %bitcast.258), calls=%async_computation.12 | async-start | bytes 2097152 | tf_op jit(solution)/shard_map/all_to_all | solution.py:559
  383.6 235.6 %reduce-scatter.7.cloned.1.call-start = ((), (), s32[]{:S(2)}) async-start(), calls=%async_computation.26 | async-start | bytes 6488064 | tf_op jit(solution)/shard_map/reduce_scatter | solution.py:766
  408.7 10.7 %copy-start.23 = (bf16[4,64,2048]{2,1,0:T(8,128)(2,1)}, bf16[4,64,2048]{2,1,0:T(8,128)(2,1)S(1)}, u32[]{:S(2)}) copy-start(bf16[4,64,2048]{2,1,0:T(8,128)(2,1)S(1)} %all-to-all-done.12.terms_ref) | copy-start | bytes 3145732
  408.7 30.1 %all-to-all-start.7 = ((bf16[4,64,2048]{2,1,0:T(8,128)(2,1)}), bf16[4,64,2048]{2,1,0:T(8,128)(2,1)}, u32[]{:S(2)}, u32[]{:S(2)}) async-start(bf16[4,64,2048]{2,1,0:T(8,128)(2,1)} %get-tuple-element.90), calls=%async_computation.7 | async-start | bytes 2097152 | tf_op jit(solution)/shard_map/all_to_all | solution.py:559
  438.8 29.8 %all-to-all-start.13 = ((bf16[4,64,2048]{2,1,0:T(8,128)(2,1)}), bf16[4,64,2048]{2,1,0:T(8,128)(2,1)}, u32[]{:S(2)}, u32[]{:S(2)}) async-start(bf16[4,64,2048]{2,1,0:T(8,128)(2,1)} %get-tuple-element.105), calls=%async_computation.13 | async-start | bytes 2097152 | tf_op jit(solution)/shard_map/all_to_all | solution.py:559
  468.5 29.5 %all-to-all-start.8 = ((bf16[4,64,2048]{2,1,0:T(8,128)(2,1)}), bf16[4,64,2048]{2,1,0:T(8,128)(2,1)}, u32[]{:S(2)}, u32[]{:S(2)}) async-start(bf16[4,64,2048]{2,1,0:T(8,128)(2,1)} %bitcast.257), calls=%async_computation.8 | async-start | bytes 2097152 | tf_op jit(solution)/shard_map/all_to_all | solution.py:559
  473.2 177.9 %reduce-scatter.9.cloned.1.call-start = ((), (), s32[]{:S(2)}) async-start(), calls=%async_computation.27 | async-start | bytes 14745600 | tf_op jit(solution)/shard_map/reduce_scatter | solution.py:728
  473.4 4.2 copy-start.42
  485.3 12.8 %copy-start.2 = (bf16[4,1,64,1024]{3,2,1,0:T(8,128)(2,1)S(1)}, bf16[4,1,64,1024]{3,2,1,0:T(8,128)(2,1)}, u32[]{:S(2)}) copy-start(bf16[4,1,64,1024]{3,2,1,0:T(8,128)(2,1)} %get-tuple-element.109.grad_ref) | copy-start | bytes 1572868
  499.7 11.3 %copy-start.33 = (bf16[4,1,64,1024]{3,2,1,0:T(8,128)(2,1)S(1)}, bf16[4,1,64,1024]{3,2,1,0:T(8,128)(2,1)}, u32[]{:S(2)}) copy-start(bf16[4,1,64,1024]{3,2,1,0:T(8,128)(2,1)} %get-tuple-element.111) | copy-start | bytes 1572868
  512.8 2.4 copy-start.31
  513.1 12.5 %copy-start.25 = (bf16[4,2,64,3200]{3,2,1,0:T(8,128)(2,1)}, bf16[4,2,64,3200]{3,2,1,0:T(8,128)(2,1)S(1)}, u32[]{:S(2)}) copy-start(bf16[4,2,64,3200]{3,2,1,0:T(8,128)(2,1)S(1)} %copy.133) | copy-start | bytes 9830404
  525.6 29.2 %all-to-all-start.11 = ((bf16[4,64,2048]{2,1,0:T(8,128)(2,1)}), bf16[4,64,2048]{2,1,0:T(8,128)(2,1)S(1)}, u32[]{:S(2)}, u32[]{:S(2)}) async-start(bf16[4,64,2048]{2,1,0:T(8,128)(2,1)} %bitcast.44), calls=%async_computation.11 | async-start | bytes 2097152 | tf_op jit(solution)/shard_map/all_to_all | solution.py:559
  529.6 5.1 copy-start.12
  529.6 5.1 copy-start.26
  554.8 59.2 %all-to-all-start.14 = ((bf16[4,128,2048]{2,1,0:T(8,128)(2,1)}), bf16[4,128,2048]{2,1,0:T(8,128)(2,1)S(1)}, u32[]{:S(2)}, u32[]{:S(2)}) async-start(bf16[4,128,2048]{2,1,0:T(8,128)(2,1)} %bitcast.247), calls=%async_computation.16 | async-start | bytes 4194304 | tf_op jit(solution)/shard_map/all_to_all | solution.py:559
  558.4 122.8 %reduce-scatter.11.cloned.1.call-start = ((), (), s32[]{:S(2)}) async-start(), calls=%async_computation.28 | async-start | bytes 4718592 | tf_op jit(solution)/shard_map/reduce_scatter | solution.py:781
  613.9 5.2 copy-start.15
  614.0 37.2 %all-to-all-start.15 = ((bf16[4,64,2816]{2,1,0:T(8,128)(2,1)}), bf16[4,64,2816]{2,1,0:T(8,128)(2,1)}, u32[]{:S(2)}, u32[]{:S(2)}) async-start(bf16[4,64,2816]{2,1,0:T(8,128)(2,1)} %reduce-scatter.5.cloned.1.call-done), calls=%async_computation.18 | async-start | bytes 2883584 | tf_op jit(solution)/shard_map/all_to_all | solution.py:559
  621.5 5.4 copy-start.14
  621.5 5.4 copy-start.35
  651.1 41.7 %all-to-all-start.16 = ((bf16[4,64,3200]{2,1,0:T(8,128)(2,1)}), bf16[4,64,3200]{2,1,0:T(8,128)(2,1)S(1)}, u32[]{:S(2)}, u32[]{:S(2)}) async-start(bf16[4,64,3200]{2,1,0:T(8,128)(2,1)} %reduce-scatter.9.cloned.1.call-done), calls=%async_computation.19 | async-start | bytes 3276800 | tf_op jit(solution)/shard_map/all_to_all | solution.py:559
  (20 other events, 26.1 us)
Sparse Core Ops, SparseCore 0:
  60.2 55.7 all-gather.7
  118.4 36.7 all-gather.9
  157.1 36.7 all-gather.11
  195.5 43.3 all-gather.15
  241.2 67.6 all-gather.13
  378.3 84.9 reduce-scatter.4
  466.7 59.0 reduce-scatter.6
  529.8 96.2 reduce-scatter.8
  629.8 51.3 reduce-scatter.10

commit v4 on v3

--- a/solution.py
+++ b/solution.py
@@ -414,7 +414,7 @@
             jax.ShapeDtypeStruct((heads, blocks, BLOCK, BLOCK), F32),
         ],
         compiler_params=pltpu.CompilerParams(vmem_limit_bytes=40 * 1024 * 1024),
-        cost_estimate=mixer_cost(sent, heads, 60),
+        cost_estimate=mixer_cost(sent, heads, 300),
         name="mixer_forward",
     )(lengths, rates, sent, taps)
 
@@ -471,7 +471,7 @@
         out_specs=[span_spec(out, 0), span_spec(out, 0), whole_spec(1, DV)],
         out_shape=[out, out, jax.ShapeDtypeStruct((1, DV), F32)],
         cost_estimate=pl.CostEstimate(
-            flops=40 * mixed.size, bytes_accessed=14 * mixed.size, transcendentals=mixed.size
+            flops=40 * mixed.size, bytes_accessed=100 * mixed.size, transcendentals=mixed.size
         ),
         name="gate_backward",
     )(mixed, gate, gain, grad)
@@ -559,9 +559,10 @@
     return lax.all_to_all(blocks, "seq", split_axis=0, concat_axis=0, tiled=True)
 
 
-def gather_rows(rows):
+def gather_rows(rows, *earlier):
     spans = lax.axis_size("seq")
-    return exchange(jnp.broadcast_to(rows[None], (spans,) + rows.shape))
+    copies = jnp.broadcast_to(rows[None], (spans,) + rows.shape)
+    return exchange(after(lax.optimization_barrier(copies), *earlier))
 
 
 def scatter_rows(partial_rows, spans):
@@ -632,9 +633,9 @@
 
     in_blocks, up_blocks = lax.optimization_barrier((exchange(in_blocks), up_blocks))
     w_mix = gather_weight(in_blocks[:, :, :mix_width])
-    all_tokens = gather_rows(after(local_tokens, in_blocks))
-
-    cot = gather_rows(after(local_cot, all_tokens)).reshape(all_rows, D)
+    all_tokens = gather_rows(local_tokens, in_blocks)
+
+    cot = gather_rows(local_cot, all_tokens).reshape(all_rows, D)
     small_at = pair_at + 2 * heads
     small = plain(w_mix[:, small_at : small_at + conv_cols + 2])
     gains = small[:, conv_cols:].T.astype(F32)
@@ -659,7 +660,7 @@
     input_scale = norm_scale(inputs)
     first = (inputs * input_scale * gains[0]).astype(BF16)
     sent = dot(first, w_mix).astype(BF16)
-    w_gate = gather_weight(after(in_blocks, all_tokens)[:, :, mix_width:])
+    w_gate = gather_weight(after(in_blocks[:, :, mix_width:], all_tokens))
     w_down = lax.all_gather(after(down_weight, w_mix), "fsdp", axis=0)
     w_out = lax.all_gather(after(out_weight, w_mix), "fsdp", axis=0, tiled=True)
     sent = sent.reshape(grouped + (mix_width,))
@@ -766,7 +767,7 @@
     grad_down = lax.psum_scatter(
         after(down_grads, grad_middles[0]), "fsdp", scatter_dimension=0
     )
-    in_product = outer(after(first, finals[0]), grad_proj)
+    in_product = outer(after(first, finals[0], up_grads), grad_proj)
     in_grads = reduce_rows(in_product, spans)
     grad_proj = after(grad_proj, in_product)
     grad_first = dot_back(grad_proj[:, :mix_width], w_mix) + dot_back(

time: 709 us -> 701 us (0.989)
  blocking collectives: 93.2 us -> 41.7 us
  waiting for transfers between devices: 205 us -> 244 us
    all_to_all x1 -> x0, blocking collectives: 50.2 us -> none  [exchange(): lax.all_to_all(blocks, 'seq', split_axis=0, concat_axis=0, tiled=True)]
    all_to_all x16 -> x17, waiting for transfers between devices: 172 us -> 201 us  [exchange(): lax.all_to_all(blocks, 'seq', split_axis=0, concat_axis=0, tiled=True)]
    reduce_scatter x1, waiting for transfers between devices: 16.5 us -> 25.3 us  [shards(): lax.psum_scatter(out_grads.astype(BF16), 'fsdp', scatter_dimension=0, til...]
    all_to_all x16 -> x17, starting transfers between devices: 68.1 us -> 73.3 us  [exchange(): lax.all_to_all(blocks, 'seq', split_axis=0, concat_axis=0, tiled=True)]
    unnamed x100 -> x116, local copies, waits for them, and re-layouts: 29.1 us -> 27.2 us
  transfers between devices with their start and end apart: 25 -> 26, of which waited for: 19 -> 18; matrix products, arithmetic and copies ran while one was open for 29% -> 29% of each run, Pallas kernels for 10% -> 10%
where the time goes in v4:
time: 701 us; the launch traced here: 694 us
  waiting for transfers between devices  244 us (35%)
  matrix products  134 us (19%)
  starting transfers between devices  75.1 us (11%)
  Pallas kernels  71.3 us (10%)
  local copies, waits for them, and re-layouts  62.1 us (9%)
  other arithmetic  50.9 us (7%)
  blocking collectives  41.7 us (6%)
  between operations  15 us (2%)
    all_to_all x17, waiting for transfers between devices, exchange(): lax.all_to_all(blocks, 'seq', split_axis=0, concat_axis=0, tiled=True)  201 us
    all_to_all x17, starting transfers between devices, exchange(): lax.all_to_all(blocks, 'seq', split_axis=0, concat_axis=0, tiled=True)  73.3 us
    dot_general x8, matrix products, dot(): return jnp.dot(left, right, preferred_element_type=F32)  49.4 us
    dot_general x7, matrix products, dot_back(): return lax.dot_general(left, right, NT, preferred_element_type=F32)  47.3 us
    dot_general x4, matrix products, outer(): return lax.dot_general(left, right, TN, preferred_element_type=F32)  37.6 us
    unnamed x116, local copies, waits for them, and re-layouts  27.2 us
    reduce_scatter x1, waiting for transfers between devices, shards(): lax.psum_scatter(out_grads.astype(BF16), 'fsdp', scatter_dimension=0, til...  25.3 us
    psum x1, blocking collectives, shards(): flat = lax.psum(after(flat, grad_gain1), 'fsdp')  24.6 us
  transfers between devices with their start and end apart: 26, of which 18 were waited for; matrix products, arithmetic and copies ran while one was open for 29% of the time, Pallas kernels for 10%

profile of v4, /device:TPU:0, one launch (start us, length us, event | category | flops | bytes accessed | tf_op | source)
XLA Modules:
  0.0 694.2 jit_solution(3966848979809608281)
XLA Ops:
  14.2 6.3 all-to-all-start
  27.2 31.7 %all-to-all-done = bf16[4,64,3200]{2,1,0:T(8,128)(2,1)S(1)} async-done(((bf16[4,64,3200]{2,1,0:T(8,128)(2,1)}), bf16[4,64,3200]{2,1,0:T(8,128)(2,1)S(1)}, u32[]{:S(2)}, u32[]{:S(2)}) %all-to-all-start) | async-done | bytes 1638432 | tf_op jit(solution)/shard_map/all_to_all | solution.py:559
  67.4 45.6 %all-to-all-done.1 = bf16[4,128,2048]{2,1,0:T(8,128)(2,1)S(1)} async-done(((bf16[4,128,2048]{2,1,0:T(8,128)(2,1)}), bf16[4,128,2048]{2,1,0:T(8,128)(2,1)S(1)}, u32[]{:S(2)}, u32[]{:S(2)}) %all-to-all-start.1) | async-done | bytes 2097184 | tf_op jit(solution)/shard_map/all_to_all | solution.py:559
  117.7 4.6 all-to-all-start.2
  132.0 9.5 %convolution_convert_fusion.2 = bf16[512,2176]{1,0:T(8,128)(2,1)S(1)} fusion(bf16[512,2048]{1,0:T(8,128)(2,1)S(1)} %bitcast.252, bf16[2048,2176]{1,0:T(8,128)(2,1)} %bitcast.288), kind=kOutput, calls=%fused_computation.4 | convolution fusion | flops 4564516864 | bytes 13238272 | tf_op jit(solution)/shard_map/dot_general | solution.py:539
  141.6 8.6 %mixer_forward.2 = (bf16[4,1,64,1024]{3,2,1,0:T(8,128)(2,1)S(1)}, f32[4,256,256]{2,1,0:T(8,128)S(1)}, f32[4,2,128,128]{3,2,1,0:T(8,128)S(1)}) custom-call(s32[2,4]{1,0:T(2,128)S(1)} %bitcast.220, f32[2,4]{1,0:T(2,128)S(1)} %pad_maximum_fusion.10.rate_ref, bf16[4,2,64,2176]{3,2,1,0:T(8,128)(2,1)S(1)} %bitcast.224, f32[4,2176]{1,0:T(4,128)S(1)} %maximum_convert_fusion.2.taps_ref), custom_call_target="tpu_custom_call" | custom-call | flops 40265318400 | bytes 314572800 | tf_op jit(solution)/shard_map/mixer_forward/pallas_call | solution.py:402
  152.8 18.3 %all-to-all-done.2 = bf16[4,128,2048]{2,1,0:T(8,128)(2,1)} async-done(((bf16[4,128,2048]{2,1,0:T(8,128)(2,1)}), bf16[4,128,2048]{2,1,0:T(8,128)(2,1)}, u32[]{:S(2)}, u32[]{:S(2)}) %all-to-all-start.2) | async-done | bytes 2097184 | tf_op jit(solution)/shard_map/all_to_all | solution.py:559
  171.1 4.4 all-to-all-start.3
  175.7 6.5 fusion.43.gate_ref
  185.9 7.9 %all-gather.12.cloned.1.call-done = bf16[1024,2048]{1,0:T(8,128)(2,1)} async-done(((bf16[128,2048]{1,0:T(8,128)(2,1)}), bf16[1024,2048]{1,0:T(8,128)(2,1)}) %all-gather.12.cloned.1.call-update) | async-done | bytes 4194320 | tf_op jit(solution)/shard_map/all_gather | solution.py:665
  193.8 4.6 convolution_convert_fusion.7
  198.4 11.0 %all-to-all-done.3 = bf16[4,64,2816]{2,1,0:T(8,128)(2,1)} async-done(((bf16[4,64,2816]{2,1,0:T(8,128)(2,1)}), bf16[4,64,2816]{2,1,0:T(8,128)(2,1)}, u32[]{:S(2)}, u32[]{:S(2)}) %all-to-all-start.3) | async-done | bytes 1441824 | tf_op jit(solution)/shard_map/all_to_all | solution.py:559
  209.4 4.3 all-to-all-start.4
  213.7 8.6 %mixer_forward.3 = (bf16[4,1,64,1024]{3,2,1,0:T(8,128)(2,1)S(1)}, f32[4,256,256]{2,1,0:T(8,128)S(1)}, f32[4,2,128,128]{3,2,1,0:T(8,128)S(1)}) custom-call(s32[2,4]{1,0:T(2,128)S(1)} %bitcast.221, f32[2,4]{1,0:T(2,128)S(1)} %pad_maximum_fusion.10.rate_ref, bf16[4,2,64,2176]{3,2,1,0:T(8,128)(2,1)S(1)} %bitcast.225, f32[4,2176]{1,0:T(4,128)S(1)} %maximum_convert_fusion.2.taps_ref), custom_call_target="tpu_custom_call" | custom-call | flops 40265318400 | bytes 314572800 | tf_op jit(solution)/shard_map/mixer_forward/pallas_call | solution.py:402
  228.5 4.6 convolution_convert_fusion.6
  233.1 5.8 all-to-all-done.4.terms_ref
  246.6 21.8 %all-to-all-done.9.terms_ref = bf16[4,64,2048]{2,1,0:T(8,128)(2,1)} async-done(((bf16[4,64,2048]{2,1,0:T(8,128)(2,1)}), bf16[4,64,2048]{2,1,0:T(8,128)(2,1)}, u32[]{:S(2)}, u32[]{:S(2)}) %all-to-all-start.9) | async-done | bytes 1048608 | tf_op jit(solution)/shard_map/all_to_all | solution.py:559
  275.0 5.9 reshape.465
  281.0 6.5 fusion
  289.2 8.2 %all-to-all-done.5 = bf16[4,64,2048]{2,1,0:T(8,128)(2,1)S(1)} async-done(((bf16[4,64,2048]{2,1,0:T(8,128)(2,1)}), bf16[4,64,2048]{2,1,0:T(8,128)(2,1)S(1)}, u32[]{:S(2)}, u32[]{:S(2)}) %all-to-all-start.5) | async-done | bytes 1048608 | tf_op jit(solution)/shard_map/all_to_all | solution.py:559
  297.4 4.3 all-to-all-start.10
  301.7 6.7 all-gather.14.cloned.1.call-done
  308.4 6.4 fusion.44
  317.8 8.4 %convolution_convert_fusion.5 = bf16[256,2048]{1,0:T(8,128)(2,1)} fusion(bf16[2048,2816]{1,0:T(8,128)(2,1)} %bitcast.305, bf16[256,1408]{1,0:T(8,128)(2,1)S(1)} %get-tuple-element.195, bf16[256,1408]{1,0:T(8,128)(2,1)S(1)} %get-tuple-element.194), kind=kOutput, calls=%fused_computation.24 | convolution fusion | flops 2956197888 | bytes 14024704 | tf_op jit(solution)/shard_map/dot_general | solution.py:547
  326.9 9.3 %fusion.45 = f32[256,2816]{1,0:T(8,128)} fusion(bf16[256,2048]{1,0:T(8,128)(2,1)} %bitcast.43, bf16[2048,2816]{1,0:T(8,128)(2,1)} %bitcast.306), kind=kOutput, calls=%fused_computation.131 | convolution fusion | flops 2952790016 | bytes 15466496 | tf_op jit(solution)/shard_map/dot_general | solution.py:539
  349.5 8.4 %convolution_convert_fusion.4 = bf16[256,2048]{1,0:T(8,128)(2,1)} fusion(bf16[2048,2816]{1,0:T(8,128)(2,1)} %bitcast.307, bf16[256,1408]{1,0:T(8,128)(2,1)S(1)} %get-tuple-element.193, bf16[256,1408]{1,0:T(8,128)(2,1)S(1)} %get-tuple-element.192), kind=kOutput, calls=%fused_computation.23 | convolution fusion | flops 2956197888 | bytes 14024704 | tf_op jit(solution)/shard_map/dot_general | solution.py:547
  357.9 8.3 %all-to-all-done.6.terms_ref = bf16[4,64,2048]{2,1,0:T(8,128)(2,1)S(1)} async-done(((bf16[4,64,2048]{2,1,0:T(8,128)(2,1)}), bf16[4,64,2048]{2,1,0:T(8,128)(2,1)S(1)}, u32[]{:S(2)}, u32[]{:S(2)}) %all-to-all-start.6) | async-done | bytes 1048608 | tf_op jit(solution)/shard_map/all_to_all | solution.py:559
  366.3 11.4 %convolution_convert_fusion = bf16[2048,2816]{1,0:T(8,128)(2,1)} fusion(bf16[512,2048]{1,0:T(8,128)(2,1)} %bitcast.250, bf16[512,2816]{1,0:T(8,128)(2,1)} %bitcast.245), kind=kOutput, calls=%fused_computation | convolution fusion | flops 5911347200 | bytes 16515072 | tf_op jit(solution)/shard_map/dot_general | solution.py:543
  385.4 9.0 %convolution_convert_fusion.1 = bf16[1376,2048]{1,0:T(8,128)(2,1)} fusion(bf16[512,1376]{1,0:T(8,128)(2,1)S(1)} %bitcast.256, bf16[512,2048]{1,0:T(8,128)(2,1)} %bitcast.24), kind=kOutput, calls=%fused_computation.1 | convolution fusion | flops 2888499200 | bytes 9142272 | tf_op jit(solution)/shard_map/dot_general | solution.py:543
  397.2 5.9 reshape.424
  408.4 4.3 all-to-all-start.7
  412.7 5.7 convolution_convert_fusion.8
  421.8 16.2 %all-to-all-done.7 = bf16[4,64,2048]{2,1,0:T(8,128)(2,1)} async-done(((bf16[4,64,2048]{2,1,0:T(8,128)(2,1)}), bf16[4,64,2048]{2,1,0:T(8,128)(2,1)}, u32[]{:S(2)}, u32[]{:S(2)}) %all-to-all-start.7) | async-done | bytes 1048608 | tf_op jit(solution)/shard_map/all_to_all | solution.py:559
  437.9 4.5 all-to-all-start.13
  457.5 11.3 %mixer_backward.2 = (bf16[4,1,64,2176]{3,2,1,0:T(8,128)(2,1)S(1)}, f32[4,2176]{1,0:T(4,128)S(1)}, f32[8,128]{1,0:T(8,128)S(1)}) custom-call(s32[2,4]{1,0:T(2,128)S(1)} %bitcast.222, f32[2,4]{1,0:T(2,128)S(1)} %pad_maximum_fusion.10.rate_ref, bf16[4,2,64,2176]{3,2,1,0:T(8,128)(2,1)S(1)} %bitcast.226, f32[4,2176]{1,0:T(4,128)S(1)} %maximum_convert_fusion.2.taps_ref, ...), custom_call_target="tpu_custom_call" | custom-call | flops 5368709120 | bytes 41943040 | tf_op jit(solution)/shard_map/mixer_backward/pallas_call | solution.py:428
  468.8 5.1 all-to-all-start.8
  476.6 5.4 fusion.14.grad_ref
  488.3 11.3 %mixer_backward.3 = (bf16[4,1,64,2176]{3,2,1,0:T(8,128)(2,1)S(1)}, f32[4,2176]{1,0:T(4,128)S(1)}, f32[8,128]{1,0:T(8,128)S(1)}) custom-call(s32[2,4]{1,0:T(2,128)S(1)} %bitcast.223, f32[2,4]{1,0:T(2,128)S(1)} %pad_maximum_fusion.10.rate_ref, bf16[4,2,64,2176]{3,2,1,0:T(8,128)(2,1)S(1)} %bitcast.227, f32[4,2176]{1,0:T(4,128)S(1)} %maximum_convert_fusion.2.taps_ref, ...), custom_call_target="tpu_custom_call" | custom-call | flops 5368709120 | bytes 41943040 | tf_op jit(solution)/shard_map/mixer_backward/pallas_call | solution.py:428
  503.8 12.3 %fusion.46 = bf16[2048,3200]{1,0:T(8,128)(2,1)} fusion(bf16[512,2048]{1,0:T(8,128)(2,1)S(1)} %copy-done.34, bf16[512,3200]{1,0:T(8,128)(2,1)} %bitcast.240), kind=kOutput, calls=%fused_computation.132 | convolution fusion | flops 6710886400 | bytes 18481152 | tf_op jit(solution)/shard_map/dot_general | solution.py:543
  516.1 5.7 all-to-all-start.11
  521.8 5.1 fusion.22
  526.9 10.0 %multiply_reduce_fusion = (f32[2048]{0:T(1024)S(1)}, bf16[512,2048]{1,0:T(8,128)(2,1)}) fusion(bf16[4,128,2048]{2,1,0:T(8,128)(2,1)S(1)} %copy-done.14, f32[512]{0:T(512)S(1)} %copy-done.41, f32[512,2048]{1,0:T(8,128)S(1)} %fusion.22, bf16[2048,2176]{1,0:T(8,128)(2,1)} %bitcast.289, bf16[512,3200]{1,0:T(8,128)(2,1)S(1)} %bitcast.242), kind=kOutput, calls=%fused_computation.10 | convolution fusion | flops 4569692160 | bytes 19539968 | tf_op jit(solution)/shard_map/dot_general | solution.py:547
  537.0 8.2 %all-to-all-done.11 = bf16[4,64,2048]{2,1,0:T(8,128)(2,1)S(1)} async-done(((bf16[4,64,2048]{2,1,0:T(8,128)(2,1)}), bf16[4,64,2048]{2,1,0:T(8,128)(2,1)S(1)}, u32[]{:S(2)}, u32[]{:S(2)}) %all-to-all-start.11) | async-done | bytes 1048608 | tf_op jit(solution)/shard_map/all_to_all | solution.py:559
  555.0 4.9 convolution_convert_fusion.3
  563.0 24.6 %psum.7 = f32[1,104,128]{2,1,0:T(8,128)S(1)} all-reduce(f32[1,104,128]{2,1,0:T(8,128)S(1)} %bitcast.278), channel_id=1, replica_groups=mesh['seq'=4,'fsdp'=8] {'fsdp'}, use_global_device_ids=true, to_apply=%region_10.11 | all-reduce | flops 13312 | bytes 106496 | tf_op jit(solution)/shard_map/psum | solution.py:791
  587.6 17.1 %all_gather.31 = f32[4,104,128]{2,1,0:T(8,128)S(1)} all-gather(f32[1,104,128]{2,1,0:T(8,128)S(1)} %psum.7), channel_id=1, replica_groups=mesh['seq'=4,'fsdp'=8] {'seq'}, dimensions={0}, use_global_device_ids=true | all-gather | bytes 266240 | tf_op jit(solution)/shard_map/all_gather | solution.py:792
  620.5 21.5 %all-to-all-done.15 = bf16[4,64,2816]{2,1,0:T(8,128)(2,1)S(1)} async-done(((bf16[4,64,2816]{2,1,0:T(8,128)(2,1)}), bf16[4,64,2816]{2,1,0:T(8,128)(2,1)S(1)}, u32[]{:S(2)}, u32[]{:S(2)}) %all-to-all-start.15) | async-done | bytes 1441824 | tf_op jit(solution)/shard_map/all_to_all | solution.py:559
  655.4 25.3 %reduce-scatter.11.cloned.1.call-done = bf16[128,2048]{1,0:T(8,128)(2,1)} async-done(((bf16[1024,2048]{1,0:T(8,128)(2,1)}), bf16[128,2048]{1,0:T(8,128)(2,1)}) %reduce-scatter.11.cloned.1.call-update) | async-done | bytes 524304 | tf_op jit(solution)/shard_map/reduce_scatter | solution.py:782
  (258 shorter events, 178.1 us)
Async XLA Ops:
  14.2 44.7 %all-to-all-start = ((bf16[4,64,3200]{2,1,0:T(8,128)(2,1)}), bf16[4,64,3200]{2,1,0:T(8,128)(2,1)S(1)}, u32[]{:S(2)}, u32[]{:S(2)}) async-start(bf16[4,64,3200]{2,1,0:T(8,128)(2,1)} %pack_columns.1), calls=%async_computation | async-start | bytes 3276800 | tf_op jit(solution)/shard_map/all_to_all | solution.py:559
  20.5 95.4 %all-gather.8.cloned.1.call-start = ((), (), s32[]{:S(2)}) async-start(), calls=%async_computation.21 | async-start | bytes 10027008 | tf_op jit(solution)/shard_map/all_gather | solution.py:614
  27.2 32.9 %copy-start.15 = (bf16[2,1,64,2048]{3,2,1,0:T(8,128)(2,1)S(1)}, bf16[2,1,64,2048]{3,2,1,0:T(8,128)(2,1)}, u32[]{:S(2)}) copy-start(bf16[2,1,64,2048]{3,2,1,0:T(8,128)(2,1)} %param.13) | copy-start | bytes 1572868
  61.7 51.3 %all-to-all-start.1 = ((bf16[4,128,2048]{2,1,0:T(8,128)(2,1)}), bf16[4,128,2048]{2,1,0:T(8,128)(2,1)S(1)}, u32[]{:S(2)}, u32[]{:S(2)}) async-start(bf16[4,128,2048]{2,1,0:T(8,128)(2,1)} %broadcast_in_dim.13), calls=%async_computation.1 | async-start | bytes 4194304 | tf_op jit(solution)/shard_map/all_to_all | solution.py:559
  65.3 50.7 %copy-start.31 = (bf16[2,1,64,2048]{3,2,1,0:T(8,128)(2,1)S(1)}, bf16[2,1,64,2048]{3,2,1,0:T(8,128)(2,1)}, u32[]{:S(2)}) copy-start(bf16[2,1,64,2048]{3,2,1,0:T(8,128)(2,1)} %param.25) | copy-start | bytes 1572868
  65.3 110.4 %all-gather.10.cloned.1.call-start = ((), (), s32[]{:S(2)}) async-start(), calls=%async_computation.22 | async-start | bytes 4718592 | tf_op jit(solution)/shard_map/all_gather | solution.py:614
  67.3 50.2 %copy-start.46 = (f32[16]{0:T(128)S(1)}, f32[16]{0:T(128)}, u32[]{:S(2)}) copy-start(f32[16]{0:T(128)} %param.19) | copy-start | bytes 196
  67.3 50.2 %copy-start.47 = (f32[16]{0:T(128)S(1)}, f32[16]{0:T(128)}, u32[]{:S(2)}) copy-start(f32[16]{0:T(128)} %param.18) | copy-start | bytes 196
  112.9 18.5 %copy-start.13 = (bf16[4,128,2048]{2,1,0:T(8,128)(2,1)}, bf16[4,128,2048]{2,1,0:T(8,128)(2,1)S(1)}, u32[]{:S(2)}) copy-start(bf16[4,128,2048]{2,1,0:T(8,128)(2,1)S(1)} %all-to-all-done.1) | copy-start | bytes 6291460
  113.0 80.8 %all-gather.12.cloned.1.call-start = ((), (), s32[]{:S(2)}) async-start(), calls=%async_computation.23 | async-start | bytes 4718592 | tf_op jit(solution)/shard_map/all_gather | solution.py:665
  117.7 53.4 %all-to-all-start.2 = ((bf16[4,128,2048]{2,1,0:T(8,128)(2,1)}), bf16[4,128,2048]{2,1,0:T(8,128)(2,1)}, u32[]{:S(2)}, u32[]{:S(2)}) async-start(bf16[4,128,2048]{2,1,0:T(8,128)(2,1)} %broadcast_in_dim.31), calls=%async_computation.2 | async-start | bytes 4194304 | tf_op jit(solution)/shard_map/all_to_all | solution.py:559
  122.3 152.7 %all-gather.16.cloned.1.call-start = ((), (), s32[]{:S(2)}) async-start(), calls=%async_computation.29 | async-start | bytes 6488064 | tf_op jit(solution)/shard_map/all_gather | solution.py:664
  132.0 9.6 %copy-start.35 = (bf16[4,128,2048]{2,1,0:T(8,128)(2,1)}, bf16[4,128,2048]{2,1,0:T(8,128)(2,1)S(1)}, u32[]{:S(2)}) copy-start(bf16[4,128,2048]{2,1,0:T(8,128)(2,1)S(1)} %multiply_convert_fusion.1) | copy-start | bytes 6291460
  132.0 9.6 %copy-start.4 = (s32[2,1,4]{2,1,0:T(1,128)S(1)}, s32[2,1,4]{2,1,0:T(1,128)}, u32[]{:S(2)}) copy-start(s32[2,1,4]{2,1,0:T(1,128)} %param.14) | copy-start | bytes 100
  171.1 38.3 %all-to-all-start.3 = ((bf16[4,64,2816]{2,1,0:T(8,128)(2,1)}), bf16[4,64,2816]{2,1,0:T(8,128)(2,1)}, u32[]{:S(2)}, u32[]{:S(2)}) async-start(bf16[4,64,2816]{2,1,0:T(8,128)(2,1)} %fusion.10), calls=%async_computation.3 | async-start | bytes 2883584 | tf_op jit(solution)/shard_map/all_to_all | solution.py:559
  175.5 132.9 %all-gather.14.cloned.1.call-start = ((), (), s32[]{:S(2)}) async-start(), calls=%async_computation.24 | async-start | bytes 12976128 | tf_op jit(solution)/shard_map/all_gather | solution.py:614
  209.4 29.5 %all-to-all-start.4 = ((bf16[4,64,2048]{2,1,0:T(8,128)(2,1)}), bf16[4,64,2048]{2,1,0:T(8,128)(2,1)}, u32[]{:S(2)}, u32[]{:S(2)}) async-start(bf16[4,64,2048]{2,1,0:T(8,128)(2,1)} %bitcast.262), calls=%async_computation.4 | async-start | bytes 2097152 | tf_op jit(solution)/shard_map/all_to_all | solution.py:559
  238.9 29.5 %all-to-all-start.9 = ((bf16[4,64,2048]{2,1,0:T(8,128)(2,1)}), bf16[4,64,2048]{2,1,0:T(8,128)(2,1)}, u32[]{:S(2)}, u32[]{:S(2)}) async-start(bf16[4,64,2048]{2,1,0:T(8,128)(2,1)} %bitcast.263), calls=%async_computation.9 | async-start | bytes 2097152 | tf_op jit(solution)/shard_map/all_to_all | solution.py:559
  268.5 28.9 %all-to-all-start.5 = ((bf16[4,64,2048]{2,1,0:T(8,128)(2,1)}), bf16[4,64,2048]{2,1,0:T(8,128)(2,1)S(1)}, u32[]{:S(2)}, u32[]{:S(2)}) async-start(bf16[4,64,2048]{2,1,0:T(8,128)(2,1)} %get-tuple-element.81), calls=%async_computation.5 | async-start | bytes 2097152 | tf_op jit(solution)/shard_map/all_to_all | solution.py:559
  297.4 17.5 %copy-start.27 = (bf16[4,64,2048]{2,1,0:T(8,128)(2,1)}, bf16[4,64,2048]{2,1,0:T(8,128)(2,1)S(1)}, u32[]{:S(2)}) copy-start(bf16[4,64,2048]{2,1,0:T(8,128)(2,1)S(1)} %all-to-all-done.5) | copy-start | bytes 3145732
  297.4 29.5 %all-to-all-start.10 = ((bf16[4,64,2048]{2,1,0:T(8,128)(2,1)}), bf16[4,64,2048]{2,1,0:T(8,128)(2,1)}, u32[]{:S(2)}, u32[]{:S(2)}) async-start(bf16[4,64,2048]{2,1,0:T(8,128)(2,1)} %get-tuple-element.96), calls=%async_computation.10 | async-start | bytes 2097152 | tf_op jit(solution)/shard_map/all_to_all | solution.py:559
  308.4 6.4 copy-start.24
  336.3 30.0 %all-to-all-start.6 = ((bf16[4,64,2048]{2,1,0:T(8,128)(2,1)}), bf16[4,64,2048]{2,1,0:T(8,128)(2,1)S(1)}, u32[]{:S(2)}, u32[]{:S(2)}) async-start(bf16[4,64,2048]{2,1,0:T(8,128)(2,1)} %bitcast.261), calls=%async_computation.6 | async-start | bytes 2097152 | tf_op jit(solution)/shard_map/all_to_all | solution.py:559
  340.1 146.1 %reduce-scatter.5.cloned.1.call-start = ((), (), s32[]{:S(2)}) async-start(), calls=%async_computation.25 | async-start | bytes 12976128 | tf_op jit(solution)/shard_map/reduce_scatter | solution.py:729
  366.3 11.4 %copy-start.25 = (bf16[4,64,2048]{2,1,0:T(8,128)(2,1)}, bf16[4,64,2048]{2,1,0:T(8,128)(2,1)S(1)}, u32[]{:S(2)}) copy-start(bf16[4,64,2048]{2,1,0:T(8,128)(2,1)S(1)} %all-to-all-done.6.terms_ref) | copy-start | bytes 3145732
  379.6 28.8 %all-to-all-start.12 = ((bf16[4,64,2048]{2,1,0:T(8,128)(2,1)}), bf16[4,64,2048]{2,1,0:T(8,128)(2,1)S(1)}, u32[]{:S(2)}, u32[]{:S(2)}) async-start(bf16[4,64,2048]{2,1,0:T(8,128)(2,1)} %bitcast.260), calls=%async_computation.12 | async-start | bytes 2097152 | tf_op jit(solution)/shard_map/all_to_all | solution.py:559
  383.1 227.8 %reduce-scatter.7.cloned.1.call-start = ((), (), s32[]{:S(2)}) async-start(), calls=%async_computation.26 | async-start | bytes 6488064 | tf_op jit(solution)/shard_map/reduce_scatter | solution.py:767
  383.3 11.1 %slice-start = ((s8[5636096]{0:T(1024)(128)(4,1)}), s8[4194304]{0:T(1024)(128)(4,1)S(1)}, s32[]{:S(2)}) async-start(s8[5636096]{0:T(1024)(128)(4,1)} %bitcast.236), calls=%async_computation.30 | async-start | bytes 8388608
  385.4 9.0 %slice-start.1 = ((s8[5636096]{0:T(1024)(128)(4,1)}), s8[1441792]{0:T(1024)(128)(4,1)S(1)}, s32[]{:S(2)}) async-start(s8[5636096]{0:T(1024)(128)(4,1)} %bitcast.236), calls=%async_computation.31 | async-start | bytes 2883584
  385.4 9.0 %copy-start.29 = (bf16[256,1408]{1,0:T(8,128)(2,1)S(1)}, bf16[256,1408]{1,0:T(8,128)(2,1)}, u32[]{:S(2)}) copy-start(bf16[256,1408]{1,0:T(8,128)(2,1)} %get-tuple-element.201) | copy-start | bytes 2162692
  408.4 10.0 %copy-start.26 = (bf16[4,64,2048]{2,1,0:T(8,128)(2,1)}, bf16[4,64,2048]{2,1,0:T(8,128)(2,1)S(1)}, u32[]{:S(2)}) copy-start(bf16[4,64,2048]{2,1,0:T(8,128)(2,1)S(1)} %all-to-all-done.12.terms_ref) | copy-start | bytes 3145732
  408.4 29.5 %all-to-all-start.7 = ((bf16[4,64,2048]{2,1,0:T(8,128)(2,1)}), bf16[4,64,2048]{2,1,0:T(8,128)(2,1)}, u32[]{:S(2)}, u32[]{:S(2)}) async-start(bf16[4,64,2048]{2,1,0:T(8,128)(2,1)} %get-tuple-element.90), calls=%async_computation.7 | async-start | bytes 2097152 | tf_op jit(solution)/shard_map/all_to_all | solution.py:559
  418.4 24.0 %copy-start.40 = (f32[1,2048]{1,0:T(1,128)S(1)}, f32[1,2048]{1,0:T(1,128)}, u32[]{:S(2)}) copy-start(f32[1,2048]{1,0:T(1,128)} %copy-done.39) | copy-start | bytes 24580
  418.4 24.0 %copy-start.41 = (f32[512]{0:T(512)S(1)}, f32[512]{0:T(512)}, u32[]{:S(2)}) copy-start(f32[512]{0:T(512)} %get-tuple-element.222) | copy-start | bytes 6148
  437.9 30.9 %all-to-all-start.13 = ((bf16[4,64,2048]{2,1,0:T(8,128)(2,1)}), bf16[4,64,2048]{2,1,0:T(8,128)(2,1)}, u32[]{:S(2)}, u32[]{:S(2)}) async-start(bf16[4,64,2048]{2,1,0:T(8,128)(2,1)} %get-tuple-element.105), calls=%async_computation.13 | async-start | bytes 2097152 | tf_op jit(solution)/shard_map/all_to_all | solution.py:559
  442.4 4.2 copy-start.48
  468.8 34.5 %all-to-all-start.8 = ((bf16[4,64,2048]{2,1,0:T(8,128)(2,1)}), bf16[4,64,2048]{2,1,0:T(8,128)(2,1)}, u32[]{:S(2)}, u32[]{:S(2)}) async-start(bf16[4,64,2048]{2,1,0:T(8,128)(2,1)} %bitcast.259), calls=%async_computation.8 | async-start | bytes 2097152 | tf_op jit(solution)/shard_map/all_to_all | solution.py:559
  473.9 168.0 %reduce-scatter.9.cloned.1.call-start = ((), (), s32[]{:S(2)}) async-start(), calls=%async_computation.27 | async-start | bytes 14745600 | tf_op jit(solution)/shard_map/reduce_scatter | solution.py:729
  488.3 11.3 %copy-start.38 = (bf16[4,1,64,1024]{3,2,1,0:T(8,128)(2,1)S(1)}, bf16[4,1,64,1024]{3,2,1,0:T(8,128)(2,1)}, u32[]{:S(2)}) copy-start(bf16[4,1,64,1024]{3,2,1,0:T(8,128)(2,1)} %get-tuple-element.111) | copy-start | bytes 1572868
  516.1 29.0 %all-to-all-start.11 = ((bf16[4,64,2048]{2,1,0:T(8,128)(2,1)}), bf16[4,64,2048]{2,1,0:T(8,128)(2,1)S(1)}, u32[]{:S(2)}, u32[]{:S(2)}) async-start(bf16[4,64,2048]{2,1,0:T(8,128)(2,1)} %bitcast.44), calls=%async_computation.11 | async-start | bytes 2097152 | tf_op jit(solution)/shard_map/all_to_all | solution.py:559
  521.8 5.1 copy-start.14
  521.8 5.1 copy-start.28
  545.1 60.3 %all-to-all-start.14 = ((bf16[4,128,2048]{2,1,0:T(8,128)(2,1)}), bf16[4,128,2048]{2,1,0:T(8,128)(2,1)S(1)}, u32[]{:S(2)}, u32[]{:S(2)}) async-start(bf16[4,128,2048]{2,1,0:T(8,128)(2,1)} %bitcast.249), calls=%async_computation.16 | async-start | bytes 4194304 | tf_op jit(solution)/shard_map/all_to_all | solution.py:559
  548.8 131.9 %reduce-scatter.11.cloned.1.call-start = ((), (), s32[]{:S(2)}) async-start(), calls=%async_computation.28 | async-start | bytes 4718592 | tf_op jit(solution)/shard_map/reduce_scatter | solution.py:782
  605.5 5.4 copy-start.17
  605.5 36.4 %all-to-all-start.15 = ((bf16[4,64,2816]{2,1,0:T(8,128)(2,1)}), bf16[4,64,2816]{2,1,0:T(8,128)(2,1)S(1)}, u32[]{:S(2)}, u32[]{:S(2)}) async-start(bf16[4,64,2816]{2,1,0:T(8,128)(2,1)} %reduce-scatter.5.cloned.1.call-done), calls=%async_computation.18 | async-start | bytes 2883584 | tf_op jit(solution)/shard_map/all_to_all | solution.py:559
  613.3 6.8 copy-start.16
  643.0 41.6 %all-to-all-start.16 = ((bf16[4,64,3200]{2,1,0:T(8,128)(2,1)}), bf16[4,64,3200]{2,1,0:T(8,128)(2,1)S(1)}, u32[]{:S(2)}, u32[]{:S(2)}) async-start(bf16[4,64,3200]{2,1,0:T(8,128)(2,1)} %reduce-scatter.9.cloned.1.call-done), calls=%async_computation.19 | async-start | bytes 3276800 | tf_op jit(solution)/shard_map/all_to_all | solution.py:559
  (29 other events, 46.6 us)
Sparse Core Ops, SparseCore 0:
  60.2 55.7 all-gather.7
  118.4 36.7 all-gather.9
  157.1 36.7 all-gather.11
  195.6 43.3 all-gather.15
  240.7 67.7 all-gather.13
  377.8 84.9 reduce-scatter.4
  466.2 59.0 reduce-scatter.6
  529.3 96.2 reduce-scatter.8
  629.3 51.3 reduce-scatter.10

commit v5 on v4

--- a/solution.py
+++ b/solution.py
@@ -632,12 +632,13 @@
     all_rows = spans * local_rows
 
     in_blocks, up_blocks = lax.optimization_barrier((exchange(in_blocks), up_blocks))
-    w_mix = gather_weight(in_blocks[:, :, :mix_width])
+    w_in = gather_weight(in_blocks)
+    w_mix, w_gate = w_in[:, :mix_width], w_in[:, mix_width:]
     all_tokens = gather_rows(local_tokens, in_blocks)
 
     cot = gather_rows(local_cot, all_tokens).reshape(all_rows, D)
     small_at = pair_at + 2 * heads
-    small = plain(w_mix[:, small_at : small_at + conv_cols + 2])
+    small = plain(w_in[:, small_at : small_at + conv_cols + 2])
     gains = small[:, conv_cols:].T.astype(F32)
 
     def own(base, width):
@@ -660,9 +661,8 @@
     input_scale = norm_scale(inputs)
     first = (inputs * input_scale * gains[0]).astype(BF16)
     sent = dot(first, w_mix).astype(BF16)
-    w_gate = gather_weight(after(in_blocks[:, :, mix_width:], all_tokens))
-    w_down = lax.all_gather(after(down_weight, w_mix), "fsdp", axis=0)
-    w_out = lax.all_gather(after(out_weight, w_mix), "fsdp", axis=0, tiled=True)
+    w_down = lax.all_gather(after(down_weight, all_tokens), "fsdp", axis=0)
+    w_out = lax.all_gather(after(out_weight, all_tokens), "fsdp", axis=0, tiled=True)
     sent = sent.reshape(grouped + (mix_width,))
     mixers = []
     for micro in range(micros):
@@ -765,14 +765,12 @@
         jnp.concatenate(pair, axis=-1) for pair in zip(grad_sents, grad_gates)
     ])
     grad_down = lax.psum_scatter(
-        after(down_grads, grad_middles[0]), "fsdp", scatter_dimension=0
+        after(down_grads, down_grads), "fsdp", scatter_dimension=0
     )
     in_product = outer(after(first, finals[0], up_grads), grad_proj)
     in_grads = reduce_rows(in_product, spans)
     grad_proj = after(grad_proj, in_product)
-    grad_first = dot_back(grad_proj[:, :mix_width], w_mix) + dot_back(
-        grad_proj[:, mix_width:], w_gate
-    )
+    grad_first = dot_back(grad_proj, w_in)
     grad_gain1 = jnp.sum(inputs * input_scale * grad_first, axis=0)
     first_rows = grad_first.astype(BF16)
     grad_first = scatter_rows(after(first_rows, grad_down, up_grads), spans)

time: 701 us -> 693 us (0.989)
  blocking collectives: 41.7 us -> 92.4 us
  waiting for transfers between devices: 244 us -> 196 us
  other arithmetic: 50.9 us -> 42.9 us
    all_to_all x0 -> x1, blocking collectives: none -> 50.3 us  [exchange(): lax.all_to_all(blocks, 'seq', split_axis=0, concat_axis=0, tiled=True)]
    all_to_all x17 -> x16, waiting for transfers between devices: 201 us -> 158 us  [exchange(): lax.all_to_all(blocks, 'seq', split_axis=0, concat_axis=0, tiled=True)]
    all_gather x2, waiting for transfers between devices: 7.94 us -> 0.01 us  [the longest x1 0.01 us: shards(): lax.all_gather(after(out_weight, all_tokens), 'fsdp', axis=0, tiled=True)]
    all_gather x3 -> x2, waiting for transfers between devices: 9.65 us -> 15.4 us  [gather_weight(): full = plain(lax.all_gather(plain(blocks), 'fsdp', axis=1, tiled=True))]
    all_to_all x17 -> x16, starting transfers between devices: 73.3 us -> 69.4 us  [exchange(): lax.all_to_all(blocks, 'seq', split_axis=0, concat_axis=0, tiled=True)]
    unnamed x116 -> x102, local copies, waits for them, and re-layouts: 27.2 us -> 25.6 us
    dot_general x7 -> x6, matrix products: 47.3 us -> 46.9 us  [dot_back(): return lax.dot_general(left, right, NT, preferred_element_type=F32)]
  transfers between devices with their start and end apart: 26 -> 24, of which waited for: 18 -> 15; matrix products, arithmetic and copies ran while one was open for 29% -> 29% of each run, Pallas kernels for 10% -> 10%
where the time goes in v5:
time: 693 us; the launch traced here: 686 us
  waiting for transfers between devices  196 us (28%)
  matrix products  136 us (20%)
  blocking collectives  92.4 us (13%)
  starting transfers between devices  71.3 us (10%)
  Pallas kernels  70.8 us (10%)
  local copies, waits for them, and re-layouts  61.8 us (9%)
  other arithmetic  42.9 us (6%)
  between operations  15.2 us (2%)
    all_to_all x16, waiting for transfers between devices, exchange(): lax.all_to_all(blocks, 'seq', split_axis=0, concat_axis=0, tiled=True)  158 us
    all_to_all x16, starting transfers between devices, exchange(): lax.all_to_all(blocks, 'seq', split_axis=0, concat_axis=0, tiled=True)  69.4 us
    dot_general x8, matrix products, dot(): return jnp.dot(left, right, preferred_element_type=F32)  52.7 us
    all_to_all x1, blocking collectives, exchange(): lax.all_to_all(blocks, 'seq', split_axis=0, concat_axis=0, tiled=True)  50.3 us
    dot_general x6, matrix products, dot_back(): return lax.dot_general(left, right, NT, preferred_element_type=F32)  46.9 us
    dot_general x4, matrix products, outer(): return lax.dot_general(left, right, TN, preferred_element_type=F32)  36.5 us
    unnamed x102, local copies, waits for them, and re-layouts  25.6 us
    psum x1, blocking collectives, shards(): flat = lax.psum(after(flat, grad_gain1), 'fsdp')  25 us
  transfers between devices with their start and end apart: 24, of which 15 were waited for; matrix products, arithmetic and copies ran while one was open for 29% of the time, Pallas kernels for 10%

profile of v5, /device:TPU:0, one launch (start us, length us, event | category | flops | bytes accessed | tf_op | source)
XLA Modules:
  0.0 686.0 jit_solution(9471076428337745556)
XLA Ops:
  14.2 6.3 all-to-all-start
  27.2 31.7 %all-to-all-done = bf16[4,64,3200]{2,1,0:T(8,128)(2,1)S(1)} async-done(((bf16[4,64,3200]{2,1,0:T(8,128)(2,1)}), bf16[4,64,3200]{2,1,0:T(8,128)(2,1)S(1)}, u32[]{:S(2)}, u32[]{:S(2)}) %all-to-all-start) | async-done | bytes 1638432 | tf_op jit(solution)/shard_map/all_to_all | solution.py:559
  60.4 50.3 %all_to_all.85 = bf16[4,128,2048]{2,1,0:T(8,128)(2,1)S(1)} all-to-all(bf16[4,128,2048]{2,1,0:T(8,128)(2,1)S(1)} %broadcast_in_dim.13), channel_id=1, replica_groups=mesh['seq'=4,'fsdp'=8] {'seq'}, dimensions={0} | all-to-all | bytes 4194304 | tf_op jit(solution)/shard_map/all_to_all | solution.py:559
  112.7 4.6 all-to-all-start.2
  118.3 15.4 %all-gather.7.cloned.1.call-done = bf16[4,512,3200]{2,1,0:T(8,128)(2,1)} async-done(((bf16[4,64,3200]{2,1,0:T(8,128)(2,1)}), bf16[4,512,3200]{2,1,0:T(8,128)(2,1)}) %all-gather.7.cloned.1.call-update) | async-done | bytes 13107216 | tf_op jit(solution)/shard_map/all_gather | solution.py:614
  141.7 9.8 %fusion.4 = bf16[512,2176]{1,0:T(8,128)(2,1)S(1)} fusion(bf16[512,2048]{1,0:T(8,128)(2,1)S(1)} %multiply_convert_fusion.1, bf16[2048,3200]{1,0:T(8,128)(2,1)} %bitcast.282), kind=kOutput, calls=%fused_computation.6 | convolution fusion | flops 4564516864 | bytes 13238272 | tf_op jit(solution)/shard_map/dot_general | solution.py:539
  151.5 8.6 %mixer_forward.2 = (bf16[4,1,64,1024]{3,2,1,0:T(8,128)(2,1)S(1)}, f32[4,256,256]{2,1,0:T(8,128)S(1)}, f32[4,2,128,128]{3,2,1,0:T(8,128)S(1)}) custom-call(s32[2,4]{1,0:T(2,128)S(1)} %bitcast.217, f32[2,4]{1,0:T(2,128)S(1)} %pad_maximum_fusion.10.rate_ref, bf16[4,2,64,2176]{3,2,1,0:T(8,128)(2,1)S(1)} %bitcast.221, f32[4,2176]{1,0:T(4,128)S(1)} %maximum_convert_fusion.2.taps_ref), custom_call_target="tpu_custom_call" | custom-call | flops 40265318400 | bytes 314572800 | tf_op jit(solution)/shard_map/mixer_forward/pallas_call | solution.py:402
  164.4 4.3 all-to-all-start.3
  169.1 6.5 fusion.7.gate_ref
  179.2 4.9 convolution_convert_fusion.6
  184.1 18.4 %all-to-all-done.3 = bf16[4,64,2816]{2,1,0:T(8,128)(2,1)} async-done(((bf16[4,64,2816]{2,1,0:T(8,128)(2,1)}), bf16[4,64,2816]{2,1,0:T(8,128)(2,1)}, u32[]{:S(2)}, u32[]{:S(2)}) %all-to-all-start.3) | async-done | bytes 1441824 | tf_op jit(solution)/shard_map/all_to_all | solution.py:559
  202.5 4.3 all-to-all-start.4
  206.8 8.6 %mixer_forward.3 = (bf16[4,1,64,1024]{3,2,1,0:T(8,128)(2,1)S(1)}, f32[4,256,256]{2,1,0:T(8,128)S(1)}, f32[4,2,128,128]{3,2,1,0:T(8,128)S(1)}) custom-call(s32[2,4]{1,0:T(2,128)S(1)} %bitcast.218, f32[2,4]{1,0:T(2,128)S(1)} %pad_maximum_fusion.10.rate_ref, bf16[4,2,64,2176]{3,2,1,0:T(8,128)(2,1)S(1)} %bitcast.222, f32[4,2176]{1,0:T(4,128)S(1)} %maximum_convert_fusion.2.taps_ref), custom_call_target="tpu_custom_call" | custom-call | flops 40265318400 | bytes 314572800 | tf_op jit(solution)/shard_map/mixer_forward/pallas_call | solution.py:402
  221.7 4.6 convolution_convert_fusion.5
  226.2 5.8 all-to-all-done.4.terms_ref
  232.0 4.5 all-to-all-start.9
  237.3 5.9 reshape.446
  245.9 15.9 %all-to-all-done.9.terms_ref = bf16[4,64,2048]{2,1,0:T(8,128)(2,1)} async-done(((bf16[4,64,2048]{2,1,0:T(8,128)(2,1)}), bf16[4,64,2048]{2,1,0:T(8,128)(2,1)}, u32[]{:S(2)}, u32[]{:S(2)}) %all-to-all-start.9) | async-done | bytes 1048608 | tf_op jit(solution)/shard_map/all_to_all | solution.py:559
  265.3 6.5 fusion.2
  276.3 14.2 %all-to-all-done.5 = bf16[4,64,2048]{2,1,0:T(8,128)(2,1)S(1)} async-done(((bf16[4,64,2048]{2,1,0:T(8,128)(2,1)}), bf16[4,64,2048]{2,1,0:T(8,128)(2,1)S(1)}, u32[]{:S(2)}, u32[]{:S(2)}) %all-to-all-start.5) | async-done | bytes 1048608 | tf_op jit(solution)/shard_map/all_to_all | solution.py:559
  294.8 6.4 fusion.49
  304.2 8.4 %convolution_convert_fusion.4 = bf16[256,2048]{1,0:T(8,128)(2,1)} fusion(bf16[2048,2816]{1,0:T(8,128)(2,1)} %bitcast.300, bf16[256,1408]{1,0:T(8,128)(2,1)S(1)} %get-tuple-element.193, bf16[256,1408]{1,0:T(8,128)(2,1)S(1)} %get-tuple-element.192), kind=kOutput, calls=%fused_computation.27 | convolution fusion | flops 2956197888 | bytes 14024704 | tf_op jit(solution)/shard_map/dot_general | solution.py:547
  312.6 7.4 %all-to-all-done.10 = bf16[4,64,2048]{2,1,0:T(8,128)(2,1)} async-done(((bf16[4,64,2048]{2,1,0:T(8,128)(2,1)}), bf16[4,64,2048]{2,1,0:T(8,128)(2,1)}, u32[]{:S(2)}, u32[]{:S(2)}) %all-to-all-start.10) | async-done | bytes 1048608 | tf_op jit(solution)/shard_map/all_to_all | solution.py:559
  320.0 9.3 %fusion.50 = f32[256,2816]{1,0:T(8,128)} fusion(bf16[256,2048]{1,0:T(8,128)(2,1)} %bitcast.43, bf16[2048,2816]{1,0:T(8,128)(2,1)} %bitcast.301), kind=kOutput, calls=%fused_computation.133 | convolution fusion | flops 2952790016 | bytes 15466496 | tf_op jit(solution)/shard_map/dot_general | solution.py:539
  342.3 8.4 %convolution_convert_fusion.3 = bf16[256,2048]{1,0:T(8,128)(2,1)} fusion(bf16[2048,2816]{1,0:T(8,128)(2,1)} %bitcast.302, bf16[256,1408]{1,0:T(8,128)(2,1)S(1)} %get-tuple-element.191, bf16[256,1408]{1,0:T(8,128)(2,1)S(1)} %get-tuple-element.190), kind=kOutput, calls=%fused_computation.26 | convolution fusion | flops 2956197888 | bytes 14024704 | tf_op jit(solution)/shard_map/dot_general | solution.py:547
  350.8 7.3 %all-to-all-done.6.terms_ref = bf16[4,64,2048]{2,1,0:T(8,128)(2,1)S(1)} async-done(((bf16[4,64,2048]{2,1,0:T(8,128)(2,1)}), bf16[4,64,2048]{2,1,0:T(8,128)(2,1)S(1)}, u32[]{:S(2)}, u32[]{:S(2)}) %all-to-all-start.6) | async-done | bytes 1048608 | tf_op jit(solution)/shard_map/all_to_all | solution.py:559
  358.1 11.4 %convolution_convert_fusion = bf16[2048,2816]{1,0:T(8,128)(2,1)} fusion(bf16[512,2048]{1,0:T(8,128)(2,1)} %bitcast.245, bf16[512,2816]{1,0:T(8,128)(2,1)} %bitcast.240), kind=kOutput, calls=%fused_computation | convolution fusion | flops 5911347200 | bytes 16515072 | tf_op jit(solution)/shard_map/dot_general | solution.py:543
  375.2 8.1 %convolution_convert_fusion.1 = bf16[1376,2048]{1,0:T(8,128)(2,1)} fusion(bf16[512,1376]{1,0:T(8,128)(2,1)S(1)} %bitcast.249, bf16[512,2048]{1,0:T(8,128)(2,1)} %bitcast.24), kind=kOutput, calls=%fused_computation.3 | convolution fusion | flops 2888499200 | bytes 9142272 | tf_op jit(solution)/shard_map/dot_general | solution.py:543
  383.3 6.4 reshape.404
  391.5 5.6 convolution_convert_fusion.8
  400.4 5.0 all-to-all-start.7
  405.4 5.6 convolution_convert_fusion.7
  414.4 16.5 %all-to-all-done.7 = bf16[4,64,2048]{2,1,0:T(8,128)(2,1)} async-done(((bf16[4,64,2048]{2,1,0:T(8,128)(2,1)}), bf16[4,64,2048]{2,1,0:T(8,128)(2,1)}, u32[]{:S(2)}, u32[]{:S(2)}) %all-to-all-start.7) | async-done | bytes 1048608 | tf_op jit(solution)/shard_map/all_to_all | solution.py:559
  430.9 4.5 all-to-all-start.13
  435.4 5.7 fusion.18.grad_ref
  448.5 11.3 %mixer_backward.2 = (bf16[4,1,64,2176]{3,2,1,0:T(8,128)(2,1)S(1)}, f32[4,2176]{1,0:T(4,128)S(1)}, f32[8,128]{1,0:T(8,128)S(1)}) custom-call(s32[2,4]{1,0:T(2,128)S(1)} %bitcast.219, f32[2,4]{1,0:T(2,128)S(1)} %pad_maximum_fusion.10.rate_ref, bf16[4,2,64,2176]{3,2,1,0:T(8,128)(2,1)S(1)} %bitcast.223, f32[4,2176]{1,0:T(4,128)S(1)} %maximum_convert_fusion.2.taps_ref, ...), custom_call_target="tpu_custom_call" | custom-call | flops 5368709120 | bytes 41943040 | tf_op jit(solution)/shard_map/mixer_backward/pallas_call | solution.py:428
  467.7 5.5 fusion.21.grad_ref
  479.5 11.3 %mixer_backward.3 = (bf16[4,1,64,2176]{3,2,1,0:T(8,128)(2,1)S(1)}, f32[4,2176]{1,0:T(4,128)S(1)}, f32[8,128]{1,0:T(8,128)S(1)}) custom-call(s32[2,4]{1,0:T(2,128)S(1)} %bitcast.220, f32[2,4]{1,0:T(2,128)S(1)} %pad_maximum_fusion.10.rate_ref, bf16[4,2,64,2176]{3,2,1,0:T(8,128)(2,1)S(1)} %bitcast.224, f32[4,2176]{1,0:T(4,128)S(1)} %maximum_convert_fusion.2.taps_ref, ...), custom_call_target="tpu_custom_call" | custom-call | flops 5368709120 | bytes 41943040 | tf_op jit(solution)/shard_map/mixer_backward/pallas_call | solution.py:428
  495.0 12.2 %fusion.51 = bf16[2048,3200]{1,0:T(8,128)(2,1)} fusion(bf16[512,2048]{1,0:T(8,128)(2,1)S(1)} %copy-done.30, bf16[512,3200]{1,0:T(8,128)(2,1)} %bitcast.236), kind=kOutput, calls=%fused_computation.134 | convolution fusion | flops 6710886400 | bytes 18481152 | tf_op jit(solution)/shard_map/dot_general | solution.py:543
  507.2 5.3 all-to-all-start.11
  512.6 12.3 %multiply_reduce_fusion = (f32[2048]{0:T(1024)S(1)}, bf16[512,2048]{1,0:T(8,128)(2,1)}) fusion(bf16[4,128,2048]{2,1,0:T(8,128)(2,1)S(1)} %copy-done.14, f32[512]{0:T(512)S(1)} %copy-done.37, bf16[512,3200]{1,0:T(8,128)(2,1)} %bitcast.237, bf16[2048,3200]{1,0:T(8,128)(2,1)} %bitcast.284), kind=kOutput, calls=%fused_computation.14 | convolution fusion | flops 6716127232 | bytes 20588544 | tf_op jit(solution)/shard_map/dot_general | solution.py:547
  524.9 12.7 %all-to-all-done.11 = bf16[4,64,2048]{2,1,0:T(8,128)(2,1)S(1)} async-done(((bf16[4,64,2048]{2,1,0:T(8,128)(2,1)}), bf16[4,64,2048]{2,1,0:T(8,128)(2,1)S(1)}, u32[]{:S(2)}, u32[]{:S(2)}) %all-to-all-start.11) | async-done | bytes 1048608 | tf_op jit(solution)/shard_map/all_to_all | solution.py:559
  547.6 4.7 convolution_convert_fusion.2
  554.8 25.0 %psum.7 = f32[1,104,128]{2,1,0:T(8,128)S(1)} all-reduce(f32[1,104,128]{2,1,0:T(8,128)S(1)} %bitcast.272), channel_id=1, replica_groups=mesh['seq'=4,'fsdp'=8] {'fsdp'}, use_global_device_ids=true, to_apply=%region_10.11 | all-reduce | flops 13312 | bytes 106496 | tf_op jit(solution)/shard_map/psum | solution.py:789
  579.8 17.0 %all_gather.27 = f32[4,104,128]{2,1,0:T(8,128)S(1)} all-gather(f32[1,104,128]{2,1,0:T(8,128)S(1)} %psum.7), channel_id=1, replica_groups=mesh['seq'=4,'fsdp'=8] {'seq'}, dimensions={0}, use_global_device_ids=true | all-gather | bytes 266240 | tf_op jit(solution)/shard_map/all_gather | solution.py:790
  596.9 4.3 all-to-all-start.15
  610.1 24.5 %all-to-all-done.15 = bf16[4,64,2816]{2,1,0:T(8,128)(2,1)} async-done(((bf16[4,64,2816]{2,1,0:T(8,128)(2,1)}), bf16[4,64,2816]{2,1,0:T(8,128)(2,1)}, u32[]{:S(2)}, u32[]{:S(2)}) %all-to-all-start.15) | async-done | bytes 1441824 | tf_op jit(solution)/shard_map/all_to_all | solution.py:559
  651.1 22.4 %reduce-scatter.11.cloned.1.call-done = bf16[128,2048]{1,0:T(8,128)(2,1)} async-done(((bf16[1024,2048]{1,0:T(8,128)(2,1)}), bf16[128,2048]{1,0:T(8,128)(2,1)}) %reduce-scatter.11.cloned.1.call-update) | async-done | bytes 524304 | tf_op jit(solution)/shard_map/reduce_scatter | solution.py:780
  (236 shorter events, 155.1 us)
Async XLA Ops:
  14.2 44.7 %all-to-all-start = ((bf16[4,64,3200]{2,1,0:T(8,128)(2,1)}), bf16[4,64,3200]{2,1,0:T(8,128)(2,1)S(1)}, u32[]{:S(2)}, u32[]{:S(2)}) async-start(bf16[4,64,3200]{2,1,0:T(8,128)(2,1)} %pack_columns.1), calls=%async_computation | async-start | bytes 3276800 | tf_op jit(solution)/shard_map/all_to_all | solution.py:559
  20.5 113.2 %all-gather.7.cloned.1.call-start = ((), (), s32[]{:S(2)}) async-start(), calls=%async_computation.21 | async-start | bytes 14745600 | tf_op jit(solution)/shard_map/all_gather | solution.py:614
  26.0 34.1 %copy-start.15 = (bf16[2,1,64,2048]{3,2,1,0:T(8,128)(2,1)S(1)}, bf16[2,1,64,2048]{3,2,1,0:T(8,128)(2,1)}, u32[]{:S(2)}) copy-start(bf16[2,1,64,2048]{3,2,1,0:T(8,128)(2,1)} %param.13) | copy-start | bytes 1572868
  60.1 119.2 %all-gather.9.cloned.1.call-start = ((), (), s32[]{:S(2)}) async-start(), calls=%async_computation.22 | async-start | bytes 4718592 | tf_op jit(solution)/shard_map/all_gather | solution.py:665
  60.4 50.4 %copy-start.27 = (bf16[2,1,64,2048]{3,2,1,0:T(8,128)(2,1)S(1)}, bf16[2,1,64,2048]{3,2,1,0:T(8,128)(2,1)}, u32[]{:S(2)}) copy-start(bf16[2,1,64,2048]{3,2,1,0:T(8,128)(2,1)} %param.25) | copy-start | bytes 1572868
  110.7 30.4 %copy-start.13 = (bf16[4,128,2048]{2,1,0:T(8,128)(2,1)}, bf16[4,128,2048]{2,1,0:T(8,128)(2,1)S(1)}, u32[]{:S(2)}) copy-start(bf16[4,128,2048]{2,1,0:T(8,128)(2,1)S(1)} %all_to_all.85) | copy-start | bytes 6291460
  112.7 51.8 %all-to-all-start.2 = ((bf16[4,128,2048]{2,1,0:T(8,128)(2,1)}), bf16[4,128,2048]{2,1,0:T(8,128)(2,1)}, u32[]{:S(2)}, u32[]{:S(2)}) async-start(bf16[4,128,2048]{2,1,0:T(8,128)(2,1)} %broadcast_in_dim.31), calls=%async_computation.2 | async-start | bytes 4194304 | tf_op jit(solution)/shard_map/all_to_all | solution.py:559
  117.2 120.1 %all-gather.13.cloned.1.call-start = ((), (), s32[]{:S(2)}) async-start(), calls=%async_computation.28 | async-start | bytes 6488064 | tf_op jit(solution)/shard_map/all_gather | solution.py:664
  118.2 22.9 %copy-start.36 = (f32[512]{0:T(512)}, f32[512]{0:T(512)S(1)}, u32[]{:S(2)}) copy-start(f32[512]{0:T(512)S(1)} %get-tuple-element.221) | copy-start | bytes 6148
  134.9 4.0 copy-start.32
  141.1 28.0 %copy-start.34 = (f32[1,2048]{1,0:T(1,128)}, f32[1,2048]{1,0:T(1,128)S(1)}, u32[]{:S(2)}) copy-start(f32[1,2048]{1,0:T(1,128)S(1)} %get-tuple-element.219) | copy-start | bytes 24580
  141.7 9.8 %copy-start.29 = (bf16[512,2048]{1,0:T(8,128)(2,1)}, bf16[512,2048]{1,0:T(8,128)(2,1)S(1)}, u32[]{:S(2)}) copy-start(bf16[512,2048]{1,0:T(8,128)(2,1)S(1)} %multiply_convert_fusion.1) | copy-start | bytes 6291460
  141.7 9.8 %copy-start.4 = (s32[2,1,4]{2,1,0:T(1,128)S(1)}, s32[2,1,4]{2,1,0:T(1,128)}, u32[]{:S(2)}) copy-start(s32[2,1,4]{2,1,0:T(1,128)} %param.14) | copy-start | bytes 100
  164.4 38.0 %all-to-all-start.3 = ((bf16[4,64,2816]{2,1,0:T(8,128)(2,1)}), bf16[4,64,2816]{2,1,0:T(8,128)(2,1)}, u32[]{:S(2)}, u32[]{:S(2)}) async-start(bf16[4,64,2816]{2,1,0:T(8,128)(2,1)} %fusion.17), calls=%async_computation.3 | async-start | bytes 2883584 | tf_op jit(solution)/shard_map/all_to_all | solution.py:559
  168.8 126.0 %all-gather.11.cloned.1.call-start = ((), (), s32[]{:S(2)}) async-start(), calls=%async_computation.23 | async-start | bytes 12976128 | tf_op jit(solution)/shard_map/all_gather | solution.py:614
  202.5 29.5 %all-to-all-start.4 = ((bf16[4,64,2048]{2,1,0:T(8,128)(2,1)}), bf16[4,64,2048]{2,1,0:T(8,128)(2,1)}, u32[]{:S(2)}, u32[]{:S(2)}) async-start(bf16[4,64,2048]{2,1,0:T(8,128)(2,1)} %bitcast.256), calls=%async_computation.4 | async-start | bytes 2097152 | tf_op jit(solution)/shard_map/all_to_all | solution.py:559
  232.0 29.7 %all-to-all-start.9 = ((bf16[4,64,2048]{2,1,0:T(8,128)(2,1)}), bf16[4,64,2048]{2,1,0:T(8,128)(2,1)}, u32[]{:S(2)}, u32[]{:S(2)}) async-start(bf16[4,64,2048]{2,1,0:T(8,128)(2,1)} %bitcast.257), calls=%async_computation.9 | async-start | bytes 2097152 | tf_op jit(solution)/shard_map/all_to_all | solution.py:559
  261.8 28.7 %all-to-all-start.5 = ((bf16[4,64,2048]{2,1,0:T(8,128)(2,1)}), bf16[4,64,2048]{2,1,0:T(8,128)(2,1)S(1)}, u32[]{:S(2)}, u32[]{:S(2)}) async-start(bf16[4,64,2048]{2,1,0:T(8,128)(2,1)} %get-tuple-element.79), calls=%async_computation.5 | async-start | bytes 2097152 | tf_op jit(solution)/shard_map/all_to_all | solution.py:559
  290.5 10.7 %copy-start.25 = (bf16[4,64,2048]{2,1,0:T(8,128)(2,1)}, bf16[4,64,2048]{2,1,0:T(8,128)(2,1)S(1)}, u32[]{:S(2)}) copy-start(bf16[4,64,2048]{2,1,0:T(8,128)(2,1)S(1)} %all-to-all-done.5) | copy-start | bytes 3145732
  290.5 29.5 %all-to-all-start.10 = ((bf16[4,64,2048]{2,1,0:T(8,128)(2,1)}), bf16[4,64,2048]{2,1,0:T(8,128)(2,1)}, u32[]{:S(2)}, u32[]{:S(2)}) async-start(bf16[4,64,2048]{2,1,0:T(8,128)(2,1)} %get-tuple-element.94), calls=%async_computation.10 | async-start | bytes 2097152 | tf_op jit(solution)/shard_map/all_to_all | solution.py:559
  294.8 6.5 copy-start.22
  329.4 28.7 %all-to-all-start.6 = ((bf16[4,64,2048]{2,1,0:T(8,128)(2,1)}), bf16[4,64,2048]{2,1,0:T(8,128)(2,1)S(1)}, u32[]{:S(2)}, u32[]{:S(2)}) async-start(bf16[4,64,2048]{2,1,0:T(8,128)(2,1)} %bitcast.255), calls=%async_computation.6 | async-start | bytes 2097152 | tf_op jit(solution)/shard_map/all_to_all | solution.py:559
  332.9 144.5 %reduce-scatter.5.cloned.1.call-start = ((), (), s32[]{:S(2)}) async-start(), calls=%async_computation.24 | async-start | bytes 12976128 | tf_op jit(solution)/shard_map/reduce_scatter | solution.py:729
  333.3 3.4 copy-start.26
  335.2 2.2 copy-start.21
  358.1 11.4 %copy-start.23 = (bf16[4,64,2048]{2,1,0:T(8,128)(2,1)}, bf16[4,64,2048]{2,1,0:T(8,128)(2,1)S(1)}, u32[]{:S(2)}) copy-start(bf16[4,64,2048]{2,1,0:T(8,128)(2,1)S(1)} %all-to-all-done.6.terms_ref) | copy-start | bytes 3145732
  369.5 30.8 %all-to-all-start.12 = ((bf16[4,64,2048]{2,1,0:T(8,128)(2,1)}), bf16[4,64,2048]{2,1,0:T(8,128)(2,1)S(1)}, u32[]{:S(2)}, u32[]{:S(2)}) async-start(bf16[4,64,2048]{2,1,0:T(8,128)(2,1)} %bitcast.254), calls=%async_computation.12 | async-start | bytes 2097152 | tf_op jit(solution)/shard_map/all_to_all | solution.py:559
  373.1 229.1 %reduce-scatter.7.cloned.1.call-start = ((), (), s32[]{:S(2)}) async-start(), calls=%async_computation.25 | async-start | bytes 6488064 | tf_op jit(solution)/shard_map/reduce_scatter | solution.py:767
  400.3 10.7 %copy-start.24 = (bf16[4,64,2048]{2,1,0:T(8,128)(2,1)}, bf16[4,64,2048]{2,1,0:T(8,128)(2,1)S(1)}, u32[]{:S(2)}) copy-start(bf16[4,64,2048]{2,1,0:T(8,128)(2,1)S(1)} %all-to-all-done.12.terms_ref) | copy-start | bytes 3145732
  400.4 30.5 %all-to-all-start.7 = ((bf16[4,64,2048]{2,1,0:T(8,128)(2,1)}), bf16[4,64,2048]{2,1,0:T(8,128)(2,1)}, u32[]{:S(2)}, u32[]{:S(2)}) async-start(bf16[4,64,2048]{2,1,0:T(8,128)(2,1)} %get-tuple-element.88), calls=%async_computation.7 | async-start | bytes 2097152 | tf_op jit(solution)/shard_map/all_to_all | solution.py:559
  430.9 29.7 %all-to-all-start.13 = ((bf16[4,64,2048]{2,1,0:T(8,128)(2,1)}), bf16[4,64,2048]{2,1,0:T(8,128)(2,1)}, u32[]{:S(2)}, u32[]{:S(2)}) async-start(bf16[4,64,2048]{2,1,0:T(8,128)(2,1)} %get-tuple-element.103), calls=%async_computation.13 | async-start | bytes 2097152 | tf_op jit(solution)/shard_map/all_to_all | solution.py:559
  460.6 33.8 %all-to-all-start.8 = ((bf16[4,64,2048]{2,1,0:T(8,128)(2,1)}), bf16[4,64,2048]{2,1,0:T(8,128)(2,1)}, u32[]{:S(2)}, u32[]{:S(2)}) async-start(bf16[4,64,2048]{2,1,0:T(8,128)(2,1)} %bitcast.253), calls=%async_computation.8 | async-start | bytes 2097152 | tf_op jit(solution)/shard_map/all_to_all | solution.py:559
  464.9 169.8 %reduce-scatter.9.cloned.1.call-start = ((), (), s32[]{:S(2)}) async-start(), calls=%async_computation.26 | async-start | bytes 14745600 | tf_op jit(solution)/shard_map/reduce_scatter | solution.py:729
  473.2 4.2 copy-start.8
  479.5 11.3 %copy-start.33 = (bf16[4,1,64,1024]{3,2,1,0:T(8,128)(2,1)S(1)}, bf16[4,1,64,1024]{3,2,1,0:T(8,128)(2,1)}, u32[]{:S(2)}) copy-start(bf16[4,1,64,1024]{3,2,1,0:T(8,128)(2,1)} %get-tuple-element.109) | copy-start | bytes 1572868
  492.5 2.5 copy-start.30
  507.2 5.4 copy-start.37
  507.2 5.3 copy-start.14
  507.2 30.3 %all-to-all-start.11 = ((bf16[4,64,2048]{2,1,0:T(8,128)(2,1)}), bf16[4,64,2048]{2,1,0:T(8,128)(2,1)S(1)}, u32[]{:S(2)}, u32[]{:S(2)}) async-start(bf16[4,64,2048]{2,1,0:T(8,128)(2,1)} %bitcast.252), calls=%async_computation.11 | async-start | bytes 2097152 | tf_op jit(solution)/shard_map/all_to_all | solution.py:559
  537.6 59.3 %all-to-all-start.14 = ((bf16[4,128,2048]{2,1,0:T(8,128)(2,1)}), bf16[4,128,2048]{2,1,0:T(8,128)(2,1)S(1)}, u32[]{:S(2)}, u32[]{:S(2)}) async-start(bf16[4,128,2048]{2,1,0:T(8,128)(2,1)} %bitcast.244), calls=%async_computation.16 | async-start | bytes 4194304 | tf_op jit(solution)/shard_map/all_to_all | solution.py:559
  541.3 132.1 %reduce-scatter.11.cloned.1.call-start = ((), (), s32[]{:S(2)}) async-start(), calls=%async_computation.27 | async-start | bytes 4718592 | tf_op jit(solution)/shard_map/reduce_scatter | solution.py:780
  552.3 2.3 copy-start.28
  554.7 46.6 %copy-start.31 = (bf16[1,1,64,2048]{3,2,1,0:T(8,128)(2,1)S(1)}, bf16[1,1,64,2048]{3,2,1,0:T(8,128)(2,1)}, u32[]{:S(2)}) copy-start(bf16[1,1,64,2048]{3,2,1,0:T(8,128)(2,1)} %fusion.31) | copy-start | bytes 786436
  596.9 5.2 copy-start.17
  596.9 37.7 %all-to-all-start.15 = ((bf16[4,64,2816]{2,1,0:T(8,128)(2,1)}), bf16[4,64,2816]{2,1,0:T(8,128)(2,1)}, u32[]{:S(2)}, u32[]{:S(2)}) async-start(bf16[4,64,2816]{2,1,0:T(8,128)(2,1)} %reduce-scatter.5.cloned.1.call-done), calls=%async_computation.18 | async-start | bytes 2883584 | tf_op jit(solution)/shard_map/all_to_all | solution.py:559
  604.5 5.3 copy-start.16
  604.5 5.3 copy-start.35
  634.7 41.4 %all-to-all-start.16 = ((bf16[4,64,3200]{2,1,0:T(8,128)(2,1)}), bf16[4,64,3200]{2,1,0:T(8,128)(2,1)S(1)}, u32[]{:S(2)}, u32[]{:S(2)}) async-start(bf16[4,64,3200]{2,1,0:T(8,128)(2,1)} %reduce-scatter.9.cloned.1.call-done), calls=%async_computation.19 | async-start | bytes 3276800 | tf_op jit(solution)/shard_map/all_to_all | solution.py:559
  (20 other events, 22.5 us)
Sparse Core Ops, SparseCore 0:
  60.2 73.4 all-gather.6
  135.6 36.7 all-gather.8
  174.2 43.3 all-gather.12
  219.3 67.6 all-gather.10
  369.6 86.0 reduce-scatter.4
  459.0 59.0 reduce-scatter.6
  522.1 96.2 reduce-scatter.8
  622.1 51.3 reduce-scatter.10
